TPU v7x, 128 devices: a whole 4x4x4 slice. The times are simulated.
128 devices in a mesh: dp: 32 (over z_hi, y, x), mp: 4 (over z_lo, core).
Axes of the slice: x: 4, y: 4, z: 4 (z_hi: 2, z_lo: 2; z = z_hi * 2 + z_lo), core: 2. Of those that a mesh axis runs over, the one named last changes fastest.
Arguments:
- gradients: bfloat16 [32, 40, 512, 512], P('dp', 'mp'), may hold values from -16 to 16
- factor_state: float32 [4, 32, 2, 2, 512, 512], P('mp', 'dp'), as said below
- block_owner: int32 [4, 10], P('mp'), may hold values from 0 to 31, as said below
Outputs:
- directions: bfloat16 [40, 512, 512], P('mp')
- next_state: float32 [4, 32, 2, 2, 512, 512], P('mp', 'dp')
Inputs may be any that keep to these rules, and one draw needn't show every extreme that they name: `block_owner`: within one row (one index of mp) no owner appears more than 2 times, and some owner appears exactly 2 times. Every index of dp owns some block. `factor_state`: every factor matrix is symmetric positive definite.
All inputs are finite; a program needn't handle non-finite values.
Results may differ from a plain program's by a relative error of at most 0.0004.
Values may be sent and summed in bfloat16 or wider, within the bound.
No kernel may reach another device: no remote copies, remote signals or barrier semaphores. Data moves between devices by JAX's collectives and lax.ppermute only.
A program may use at most 128 MiB of HBM per device.

v0:
```python
import functools

import jax
import jax.numpy as jnp
from jax import lax
from jax.experimental import pallas as pl
from jax.experimental.pallas import tpu as pltpu
from jax.sharding import PartitionSpec as P

SLOTS = 2
N = 512
BLK = 10
NDP = 32
PIECE = N // NDP
ROWS = 2 * PIECE
HALF = BLK // 2
TR = 256
SMALL = 16 << 20
F32 = jnp.float32
BF = jnp.bfloat16

decay_rate = 0.95
ridge_term = 0.001
tiny_offset = 1e-06


def dp_pairs(dx, dy, dz):
    pairs = []
    for z in range(2):
        for y in range(4):
            for x in range(4):
                to = ((z + dz) % 2) * 16 + ((y + dy) % 4) * 4 + (x + dx) % 4
                pairs.append((z * 16 + y * 4 + x, to))
    return pairs


CORE_PAIRS = [(0, 1), (1, 0), (2, 3), (3, 2)]


def split(v):
    hi = v.astype(BF)
    return hi, (v - hi.astype(F32)).astype(BF)


def dot(a, b):
    return jnp.dot(a, b, preferred_element_type=F32)


def on_diagonal(r):
    i = lax.broadcasted_iota(jnp.int32, (TR, N), 0) + r * TR
    j = lax.broadcasted_iota(jnp.int32, (TR, N), 1)
    return i == j


def store(ref, rows, v):
    hi, lo = split(v)
    ref[0, rows, :] = hi
    ref[1, rows, :] = lo


def product(a, b, finish):
    for r in range(N // TR):
        rows = pl.ds(r * TR, TR)
        ah = a[0, rows, :]
        al = a[1, rows, :]
        finish(r, rows, dot(ah, b[0]) + (dot(ah, b[1]) + dot(al, b[0])))


def power_eighth(total):
    wide = jnp.full((8, 128), total, F32)
    return (1.0 / jnp.sqrt(jnp.sqrt(jnp.sqrt(wide))))[0:1, 0:1]


def add_kernel(across, place, own, r1, r2, r3, o0, o1, o2, o3, total):
    value = own[...].reshape(4, ROWS, N).astype(F32)
    for other in (r1, r2, r3):
        value += other[...].reshape(4, ROWS, N).astype(F32)
    total[...] = value
    here = place[across]
    for step, out in enumerate((o0, o1, o2, o3)):
        out[0] = total[lax.rem(here + step, 4)]


def add_pieces(place, grads, received, group):
    if group == 0:
        own = pl.BlockSpec((1, 1, 4, ROWS, N), lambda b, p: (b, p[0], 0, 0, 0))
        across = 1
    else:
        own = pl.BlockSpec((1, 4, 1, ROWS, N), lambda b, p: (HALF + b, 0, p[1], 0, 0))
        across = 0
    return pl.pallas_call(
        functools.partial(add_kernel, across),
        grid_spec=pltpu.PrefetchScalarGridSpec(
            num_scalar_prefetch=1,
            grid=(HALF,),
            in_specs=[own] + [pl.BlockSpec((1, 4, ROWS, N), lambda b, p: (b, 0, 0, 0))] * 3,
            out_specs=[pl.BlockSpec((1, ROWS, N), lambda b, p: (b, 0, 0))] * 4,
            scratch_shapes=[pltpu.VMEM((4, ROWS, N), F32)],
        ),
        out_shape=[jax.ShapeDtypeStruct((HALF, ROWS, N), F32)] * 4,
        compiler_params=pltpu.CompilerParams(dimension_semantics=("arbitrary",), vmem_limit_bytes=SMALL),
        cost_estimate=pl.CostEstimate(flops=2_000_000, bytes_accessed=4_000_000, transcendentals=0),
    )(place, grads, *received)


def add_again_kernel(place, *refs):
    keep, send, total = refs[8], refs[9], refs[10]
    for group in range(2):
        a, b, c, d = (ref[0] for ref in refs[4 * group : 4 * group + 4])
        total[group] = (a + b) + (c + d)
    z = place[2]
    near = pl.multiple_of(z * PIECE, PIECE)
    far = pl.multiple_of((1 - z) * PIECE, PIECE)
    keep[:, 0] = total[:, pl.ds(near, PIECE), :]
    send[:, 0] = total[:, pl.ds(far, PIECE), :]


def add_again(place, first, second):
    spec = pl.BlockSpec((2, 1, PIECE, N), lambda b, p: (0, b, 0, 0))
    return pl.pallas_call(
        add_again_kernel,
        grid_spec=pltpu.PrefetchScalarGridSpec(
            num_scalar_prefetch=1,
            grid=(HALF,),
            in_specs=[pl.BlockSpec((1, ROWS, N), lambda b, p: (b, 0, 0))] * 8,
            out_specs=[spec] * 2,
            scratch_shapes=[pltpu.VMEM((2, ROWS, N), F32)],
        ),
        out_shape=[jax.ShapeDtypeStruct((2, HALF, PIECE, N), F32)] * 2,
        compiler_params=pltpu.CompilerParams(dimension_semantics=("arbitrary",), vmem_limit_bytes=SMALL),
        cost_estimate=pl.CostEstimate(flops=1_000_000, bytes_accessed=3_300_000, transcendentals=0),
        name="add_again",
    )(place, *first, *second)


def pack_kernel(index_ref, keep, recv, out_ref, square_ref, total):
    squares = jnp.zeros((PIECE, N), F32)
    for b in range(BLK):
        value = keep[b // HALF, b % HALF] + recv[b // HALF, b % HALF]
        total[b] = value
        squares += value * value
    square_ref[...] = jnp.broadcast_to(jnp.sum(squares), square_ref.shape)

    @pl.loop(0, NDP)
    def _(o):
        for s in range(SLOTS):
            out_ref[o, s] = total[index_ref[s, o]]


def pack(index, keep, recv):
    return pl.pallas_call(
        pack_kernel,
        in_specs=[pl.BlockSpec(memory_space=pltpu.SMEM)] + [pl.BlockSpec(memory_space=pltpu.VMEM)] * 2,
        out_specs=[pl.BlockSpec(memory_space=pltpu.VMEM)] * 2,
        out_shape=[
            jax.ShapeDtypeStruct((NDP, SLOTS, PIECE, N), F32),
            jax.ShapeDtypeStruct((8, 128), F32),
        ],
        scratch_shapes=[pltpu.VMEM((BLK, PIECE, N), F32)],
        compiler_params=pltpu.CompilerParams(vmem_limit_bytes=SMALL),
        cost_estimate=pl.CostEstimate(flops=300_000, bytes_accessed=3_000_000, transcendentals=0),
        name="pack",
    )(index, keep, recv)


def piece_row(device):
    return (device % 4) * 128 + (device // 4 % 4) * ROWS + (device // 16) * PIECE


def task_kernel(occ, clip, own_g, own_old, other_g, other_old, own_dir, other_dir, g2, gt2, full, m, f, p, q, m1, f1, x, u, norms):
    task = pl.program_id(0)

    def halves_to(ref):
        return lambda r, rows, acc: store(ref, rows, acc)

    def factor(r, moving):
        return jnp.where(on_diagonal(r), 1.25, 0.0) - 0.25 * moving

    @pl.when(occ[task] > 0)
    def _():
        @pl.when(task == 0)
        def _():
            for source in range(NDP):
                full[pl.ds(piece_row(source), PIECE), :] = other_g[source, 0] * clip[0]

        @pl.when(task == 1)
        def _():
            for source in range(NDP):
                full[pl.ds(piece_row(source), PIECE), :] = own_g[source, 0] * clip[0]

        g = full[...]
        squares = jnp.sum(g * g)
        store(g2, pl.ds(0, N), g)
        store(gt2, pl.ds(0, N), g.T)

        def root(side, carry):
            def gram(a, b):
                def finish(r, rows, acc):
                    full[rows, :] = (1.0 - decay_rate) * acc + jnp.where(on_diagonal(r), ridge_term, 0.0)

                product(a, b, finish)

            @pl.when(side == 0)
            def _():
                gram(g2, gt2)

            @pl.when(side == 1)
            def _():
                gram(gt2, g2)

            @pl.when(task == 0)
            def _():
                full[...] += decay_rate * other_old[0, 0, 0, side]

            @pl.when(task == 1)
            def _():
                full[...] += decay_rate * own_old[0, 0, 0, side]

            whole = full[...]
            norm2 = jnp.sum(whole * whole)
            norms[side] = norm2
            inverse = (1.0 / jnp.sqrt(jnp.full((8, 128), norm2, F32)))[0:1, 0:1]
            for r in range(N // TR):
                rows = pl.ds(r * TR, TR)
                moving = full[rows, :] * inverse
                store(m, rows, moving)
                store(f, rows, factor(r, moving))

            def first(r, rows, acc):
                store(m1, rows, acc)
                store(f1, rows, factor(r, acc))

            product(f, f, halves_to(p))
            product(p, p, halves_to(q))
            product(q, m, first)
            product(f, f1, halves_to(x))
            product(f1, f1, halves_to(p))
            product(p, p, halves_to(q))
            product(q, m1, lambda r, rows, acc: store(m, rows, factor(r, acc)))
            product(x, m, halves_to(u.at[side]))
            return carry

        lax.fori_loop(0, 2, root, 0)

        def last(r, rows, acc):
            full[rows, :] = acc

        product(u.at[0], g2, halves_to(p))
        product(p, u.at[1], last)
        precond = full[...] * (power_eighth(norms[0]) * power_eighth(norms[1]))
        entries = N * N
        actual = jnp.full((8, 128), jnp.sum(precond * precond) / entries + tiny_offset, F32)
        target = jnp.full((8, 128), squares / entries + tiny_offset, F32)
        graft = (jnp.sqrt(target) / jnp.sqrt(actual))[0:1, 0:1]
        full[...] = precond * graft

        @pl.when(task == 0)
        def _():
            for device in range(NDP):
                other_dir[device, 0] = full[pl.ds(piece_row(device), PIECE), :].astype(BF)

        @pl.when(task == 1)
        def _():
            for device in range(NDP):
                own_dir[device, 0] = full[pl.ds(piece_row(device), PIECE), :].astype(BF)


def pair():
    return pltpu.VMEM((2, N, N), BF)


def run_tasks(occupied, clip, own_g, own_pairs, other_g, other_pair):
    result = jax.ShapeDtypeStruct((NDP, 1, PIECE, N), BF)
    return pl.pallas_call(
        task_kernel,
        grid=(2,),
        in_specs=[pl.BlockSpec(memory_space=pltpu.SMEM)] * 2 + [pl.BlockSpec(memory_space=pltpu.VMEM)] * 4,
        out_specs=[pl.BlockSpec(memory_space=pltpu.VMEM)] * 2,
        out_shape=[result, result],
        scratch_shapes=[pair(), pair(), pltpu.VMEM((N, N), F32)]
        + [pair() for _ in range(7)]
        + [pltpu.VMEM((2, 2, N, N), BF), pltpu.SMEM((2,), F32)],
        compiler_params=pltpu.CompilerParams(dimension_semantics=("arbitrary",), vmem_limit_bytes=36 << 20),
        cost_estimate=pl.CostEstimate(flops=16_000_000_000, bytes_accessed=3_500_000, transcendentals=0),
        name="tasks",
    )(occupied, clip, own_g, own_pairs, other_g, other_pair)


def state_kernel(occ, clip, g_ref, old_ref, new_ref, full, g2, gt2):
    s = pl.program_id(0)

    @pl.when(occ[s] > 0)
    def _():
        for source in range(NDP):
            full[pl.ds(piece_row(source), PIECE), :] = g_ref[source, 0] * clip[0]
        g = full[...]
        store(g2, pl.ds(0, N), g)
        store(gt2, pl.ds(0, N), g.T)

        def mix(side):
            def finish(r, rows, acc):
                new_ref[0, 0, 0, side, rows, :] = (
                    decay_rate * old_ref[0, 0, 0, side, rows, :] + (1.0 - decay_rate) * acc
                )

            return finish

        product(g2, gt2, mix(0))
        product(gt2, g2, mix(1))

    @pl.when(occ[s] <= 0)
    def _():
        new_ref[...] = old_ref[...]


def new_state(occupied, clip, gathered, pairs):
    block = pl.BlockSpec((1, 1, 1, 2, N, N), lambda s: (0, 0, s, 0, 0, 0))
    return pl.pallas_call(
        state_kernel,
        grid=(SLOTS,),
        in_specs=[
            pl.BlockSpec(memory_space=pltpu.SMEM),
            pl.BlockSpec(memory_space=pltpu.SMEM),
            pl.BlockSpec((NDP, 1, PIECE, N), lambda s: (0, s, 0, 0)),
            block,
        ],
        out_specs=block,
        out_shape=jax.ShapeDtypeStruct(pairs.shape, F32),
        scratch_shapes=[pltpu.VMEM((N, N), F32), pair(), pair()],
        compiler_params=pltpu.CompilerParams(dimension_semantics=("arbitrary",), vmem_limit_bytes=SMALL),
        cost_estimate=pl.CostEstimate(flops=3_000_000_000, bytes_accessed=10_000_000, transcendentals=0),
        name="state",
    )(occupied, clip, gathered, pairs)


def pick_kernel(owner, slot, recv_ref, out_ref):
    for b in range(BLK):
        out_ref[b] = recv_ref[owner[b], slot[b]]


def pick(owner, slot, recv):
    return pl.pallas_call(
        pick_kernel,
        in_specs=[pl.BlockSpec(memory_space=pltpu.SMEM)] * 2 + [pl.BlockSpec(memory_space=pltpu.VMEM)],
        out_specs=pl.BlockSpec(memory_space=pltpu.VMEM),
        out_shape=jax.ShapeDtypeStruct((BLK, PIECE, N), BF),
        compiler_params=pltpu.CompilerParams(vmem_limit_bytes=SMALL),
        name="pick",
    )(owner, slot, recv)


def place_kernel(place, *refs):
    first, second, out, sems = refs[:4], refs[4:8], refs[8], refs[9]
    x, y, z = place[0], place[1], place[2]
    copies = []
    for far in range(4):
        for near in range(4):
            for dz in range(2):
                for group, dx, dy, ref in ((0, far, near, first[far]), (1, near, far, second[far])):
                    row = lax.rem(z + dz, 2) * PIECE + lax.rem(y + 4 - dy, 4) * ROWS + lax.rem(x + 4 - dx, 4) * 128
                    row = pl.multiple_of(row, PIECE)
                    copies.append(
                        pltpu.make_async_copy(
                            ref.at[near, dz],
                            out.at[pl.ds(group * HALF, HALF), pl.ds(row, PIECE), :],
                            sems.at[len(copies)],
                        )
                    )
    for copy in copies:
        copy.start()
    for copy in copies:
        copy.wait()


def place_all(place, first, second):
    return pl.pallas_call(
        place_kernel,
        in_specs=[pl.BlockSpec(memory_space=pltpu.SMEM)] + [pl.BlockSpec(memory_space=pltpu.VMEM)] * 8,
        out_specs=pl.BlockSpec(memory_space=pl.ANY),
        out_shape=jax.ShapeDtypeStruct((BLK, N, N), BF),
        scratch_shapes=[pltpu.SemaphoreType.DMA((64,))],
        compiler_params=pltpu.CompilerParams(vmem_limit_bytes=SMALL),
        name="place",
    )(place, *first, *second)


def spread(v, dx, dy, dz):
    steps = 2 if dz else 4
    return [v] + [lax.ppermute(v, "dp", dp_pairs(dx * k, dy * k, dz * k)) for k in range(1, steps)]


def owner_slots(owners):
    positions = jnp.arange(owners.shape[0], dtype=jnp.int32)
    same_owner = owners[:, None] == owners[None, :]
    earlier = positions[None, :] < positions[:, None]
    return jnp.sum((same_owner & earlier).astype(jnp.int32), axis=1)


def shards(gradients, factor_state, block_owner):
    owners = block_owner[0]
    myself = lax.axis_index("dp")
    slot_of = owner_slots(owners)
    positions = jnp.arange(BLK, dtype=jnp.int32)
    slots = jnp.arange(SLOTS, dtype=jnp.int32)
    devices = jnp.arange(NDP, dtype=jnp.int32)
    match = (owners == devices[None, :, None]) & (slot_of == slots[:, None, None])
    index = jnp.sum(jnp.where(match, positions, 0), axis=2)
    mine = (owners == myself) & (slot_of == slots[:, None])
    occupied = jnp.max(mine.astype(jnp.int32), axis=1)
    other_occupied = lax.ppermute(occupied[1:2], "mp", CORE_PAIRS)
    other_pair = lax.ppermute(factor_state[:, :, 1:2], "mp", CORE_PAIRS)

    place = jnp.stack([myself % 4, (myself // 4) % 4, myself // 16]).astype(jnp.int32)
    grads = gradients[0].reshape(BLK, 4, 4, ROWS, N)
    first, second = [], []
    zero = jnp.int32(0)
    for k in range(1, 4):
        piece = lax.dynamic_slice(grads, (zero, (place[0] + k) % 4, zero, zero, zero), (HALF, 1, 4, ROWS, N))
        first.append(lax.ppermute(piece.reshape(HALF, 4, ROWS, N), "dp", dp_pairs(k, 0, 0)))
        start = (jnp.int32(HALF), zero, (place[1] + k) % 4, zero, zero)
        piece = lax.dynamic_slice(grads, start, (HALF, 4, 1, ROWS, N))
        second.append(lax.ppermute(piece.reshape(HALF, 4, ROWS, N), "dp", dp_pairs(0, k, 0)))
    first = add_pieces(place, grads, first, 0)
    second = add_pieces(place, grads, second, 1)
    first = [first[0]] + [lax.ppermute(first[k], "dp", dp_pairs(0, k, 0)) for k in range(1, 4)]
    second = [second[0]] + [lax.ppermute(second[k], "dp", dp_pairs(k, 0, 0)) for k in range(1, 4)]
    keep, send = add_again(place, first, second)
    packed, squares = pack(index, keep, lax.ppermute(send, "dp", dp_pairs(0, 0, 1)))
    gathered = lax.all_to_all(packed, "dp", split_axis=0, concat_axis=0, tiled=True)
    hops = [("mp", bit, 4) for bit in (1, 2)] + [("dp", bit, NDP) for bit in (1, 2, 4, 8, 16)]
    for axis, bit, size in hops:
        squares = squares + lax.ppermute(squares, axis, [(i, i ^ bit) for i in range(size)])
    square_sum = squares[0, 0]
    entries = N * N * BLK * 4
    clip = (1.0 / jnp.sqrt(square_sum / entries + tiny_offset)).reshape(1)
    other = lax.ppermute(gathered[:, 1:2], "mp", CORE_PAIRS)

    tasks = jnp.concatenate([other_occupied, occupied[0:1]])
    own, helped = run_tasks(tasks, clip, gathered, factor_state, other, other_pair)
    returned = lax.ppermute(helped, "mp", CORE_PAIRS)
    outgoing = jnp.concatenate([own, returned], axis=1)
    incoming = lax.all_to_all(outgoing, "dp", split_axis=0, concat_axis=0, tiled=True)
    piece = pick(owners, slot_of, incoming)

    column = jnp.stack(spread(piece, 0, 0, 1))
    first = jnp.stack(spread(column[:, :HALF], 0, 1, 0))
    second = jnp.stack(spread(column[:, HALF:], 1, 0, 0))
    first = spread(first, 1, 0, 0)
    second = spread(second, 0, 1, 0)
    directions = place_all(place, first, second)
    next_state = new_state(occupied, clip, gathered, factor_state)
    return directions, next_state


def solution(mesh):
    in_specs = (P("dp", "mp", None, None), P("mp", "dp", None, None, None, None), P("mp", None))
    out_specs = (P("mp", None, None), P("mp", "dp", None, None, None, None))
    return jax.shard_map(shards, mesh=mesh, in_specs=in_specs, out_specs=out_specs, check_vma=False)
```

profile of v0, /device:TPU:14, one launch (start us, length us, event | category | flops | bytes accessed | tf_op | source)
XLA Modules:
  0.0 291.7 jit_solution(18277921088442298984)
XLA Ops:
  0.7 2.8 dynamic-slice_bitcast_fusion.3
  4.4 1.1 collective-permute-start.2
  5.5 2.1 collective-permute-start.1
  7.6 2.8 dynamic-slice_bitcast_fusion
  10.9 2.6 collective-permute-start.8
  13.4 22.0 %collective-permute-done.3.r3 = bf16[5,4,32,512]{3,2,1,0:T(8,128)(2,1)S(1)} collective-permute-done((bf16[5,4,32,512]{3,2,1,0:T(8,128)(2,1)}, bf16[5,4,32,512]{3,2,1,0:T(8,128)(2,1)S(1)}, u32[]{:S(2)}, u32[]{:S(2)}) %collective-permute-start.3) | collective-permute-done | bytes 655392 | tf_op jit(solution)/shard_map/ppermute | solution.py:419
  35.5 1.6 collective-permute-start.7
  37.1 2.5 copy-done
  39.6 2.8 shard_map.50
  43.1 1.3 collective-permute-start.4
  44.4 1.2 collective-permute-start.5
  45.6 1.4 collective-permute-start.6
  47.8 5.5 %collective-permute-done.7.r1 = bf16[5,4,32,512]{3,2,1,0:T(8,128)(2,1)} collective-permute-done((bf16[5,4,32,512]{3,2,1,0:T(8,128)(2,1)}, bf16[5,4,32,512]{3,2,1,0:T(8,128)(2,1)}, u32[]{:S(2)}, u32[]{:S(2)}) %collective-permute-start.7) | collective-permute-done | bytes 655392 | tf_op jit(solution)/shard_map/ppermute | solution.py:422
  53.4 1.1 copy-done.4
  54.5 4.4 %shard_map.51 = (f32[5,32,512]{2,1,0:T(8,128)S(1)}, f32[5,32,512]{2,1,0:T(8,128)}, f32[5,32,512]{2,1,0:T(8,128)}, f32[5,32,512]{2,1,0:T(8,128)}) custom-call(s32[3]{0:T(128)S(1)} %pad_add_fusion.place, bf16[10,4,4,32,512]{4,3,2,1,0:T(8,128)(2,1)S(1)} %bitcast.33, bf16[5,4,32,512]{3,2,1,0:T(8,128)(2,1)} %collective-permute-done.7.r1, ...), custom_call_target="tpu_custom_call" | custom-call | flops 2000000 | bytes 4000000 | tf_op jit(solution)/shard_map/pallas_call | solution.py:91
  60.3 1.3 collective-permute-start.12
  63.4 5.7 %collective-permute-done.10.refs_5_ = f32[5,32,512]{2,1,0:T(8,128)S(1)} collective-permute-done((f32[5,32,512]{2,1,0:T(8,128)}, f32[5,32,512]{2,1,0:T(8,128)S(1)}, u32[]{:S(2)}, u32[]{:S(2)}) %collective-permute-start.10) | collective-permute-done | bytes 327712 | tf_op jit(solution)/shard_map/ppermute | solution.py:426
  69.1 1.6 collective-permute-done.11.refs_6_
  70.7 3.4 %collective-permute-done.12.refs_7_ = f32[5,32,512]{2,1,0:T(8,128)S(1)} collective-permute-done((f32[5,32,512]{2,1,0:T(8,128)}, f32[5,32,512]{2,1,0:T(8,128)S(1)}, u32[]{:S(2)}, u32[]{:S(2)}) %collective-permute-start.12) | collective-permute-done | bytes 327712 | tf_op jit(solution)/shard_map/ppermute | solution.py:426
  74.1 1.0 copy-done.8
  75.1 1.0 copy-done.10
  76.0 1.0 copy-done.12
  77.0 0.9 add_again.1
  77.9 4.0 %collective-permute-start.13 = (f32[2,5,16,512]{3,2,1,0:T(8,128)S(1)}, f32[2,5,16,512]{3,2,1,0:T(8,128)S(1)}, u32[]{:S(2)}, u32[]{:S(2)}) collective-permute-start(f32[2,5,16,512]{3,2,1,0:T(8,128)S(1)} %get-tuple-element.25), channel_id=1, source_target_pairs={{0,64},{4,68},{8,72},{12,76},{16,80},{20,84},{24,88},{28,92},{32,9... | collective-permute-start | bytes 983048 | tf_op jit(solution)/shard_map/ppermute | solution.py:428
  82.0 5.9 %collective-permute-done.13.recv = f32[2,5,16,512]{3,2,1,0:T(8,128)S(1)} collective-permute-done((f32[2,5,16,512]{3,2,1,0:T(8,128)S(1)}, f32[2,5,16,512]{3,2,1,0:T(8,128)S(1)}, u32[]{:S(2)}, u32[]{:S(2)}) %collective-permute-start.13) | collective-permute-done | bytes 327712 | tf_op jit(solution)/shard_map/ppermute | solution.py:428
  87.9 1.0 pack.1
  88.9 1.3 copy-done.1
  90.2 9.7 %all-to-all-start = ((f32[32,2,16,512]{3,2,1,0:T(8,128)}), f32[32,2,16,512]{3,2,1,0:T(8,128)S(1)}, u32[]{:S(2)}, u32[]{:S(2)}) async-start(f32[32,2,16,512]{3,2,1,0:T(8,128)} %copy-done.1), calls=%async_computation | async-start | bytes 4194304 | tf_op jit(solution)/shard_map/all_to_all | solution.py:429
  99.9 3.1 %slice.25 = f32[1,1,1,2,512,512]{5,4,3,2,1,0:T(8,128)} slice(f32[1,1,2,2,512,512]{5,4,3,2,1,0:T(8,128)} %old_ref.1), slice={[0:1], [0:1], [1:2], [0:2], [0:512], [0:512]} | slice | bytes 4194304 | tf_op jit(solution)/shard_map/slice | solution.py:411
  103.0 21.6 %all-to-all-done.own_g.g_ref = f32[32,2,16,512]{3,2,1,0:T(8,128)S(1)} async-done(((f32[32,2,16,512]{3,2,1,0:T(8,128)}), f32[32,2,16,512]{3,2,1,0:T(8,128)S(1)}, u32[]{:S(2)}, u32[]{:S(2)}) %all-to-all-start) | async-done | bytes 2097184 | tf_op jit(solution)/shard_map/all_to_all | solution.py:429
  125.3 2.2 collective-permute-done.14
  127.5 1.0 collective-permute-start.15
  128.5 2.6 collective-permute-done.15
  131.1 0.9 collective-permute-start.16
  132.0 2.7 collective-permute-done.16
  134.7 1.6 collective-permute-start.17
  136.4 3.5 %collective-permute-done.17 = f32[8,128]{1,0:T(8,128)S(1)} collective-permute-done((f32[8,128]{1,0:T(8,128)S(1)}, f32[8,128]{1,0:T(8,128)S(1)}, u32[]{:S(2)}, u32[]{:S(2)}) %collective-permute-start.17) | collective-permute-done | bytes 4128 | tf_op jit(solution)/shard_map/ppermute | solution.py:432
  139.8 1.0 collective-permute-start.18
  141.0 2.5 collective-permute-done.18
  143.4 2.1 collective-permute-start.19
  146.1 2.4 collective-permute-done.19
  149.4 1.2 pad_add_fusion.1.occ
  150.6 3.1 %collective-permute-done.20 = f32[8,128]{1,0:T(8,128)S(1)} collective-permute-done((f32[8,128]{1,0:T(8,128)S(1)}, f32[8,128]{1,0:T(8,128)S(1)}, u32[]{:S(2)}, u32[]{:S(2)}) %collective-permute-start.20) | collective-permute-done | bytes 4128 | tf_op jit(solution)/shard_map/ppermute | solution.py:432
  154.9 2.2 copy-done.2
  157.1 21.5 %tasks.1 = (bf16[32,1,16,512]{3,2,1,0:T(8,128)(2,1)S(1)}, bf16[32,1,16,512]{3,2,1,0:T(8,128)(2,1)S(1)}) custom-call(s32[2]{0:T(128)S(1)} %pad_add_fusion.1.occ, f32[1]{0:T(128)} %bitcast.12.clip, f32[32,2,16,512]{3,2,1,0:T(8,128)S(1)} %all-to-all-done.own_g.g_ref, f32[1,1,2,2,512,512]{5,4,3,2,1,0:T(8,128)S(1)} %copy-done.2, ...), custom_call_target="tpu_custom_call" | custom-call | flops 16000000000 | bytes 3500000 | tf_op jit(solution)/shard_map/tasks/pallas_call | solution.py:274
  178.7 1.9 collective-permute-done.23
  180.7 22.6 %all_to_all.10.recv_ref = bf16[32,2,16,512]{3,2,1,0:T(8,128)(2,1)S(1)} all-to-all(bf16[32,2,16,512]{3,2,1,0:T(8,128)(2,1)S(1)} %pad_maximum_fusion), channel_id=1, replica_groups=mesh['dp'=32,'mp'=4] {'dp'}, dimensions={0} | all-to-all | bytes 2097152 | tf_op jit(solution)/shard_map/all_to_all | solution.py:442
  203.8 1.5 collective-permute-start.24
  205.3 5.9 %collective-permute-done.24 = bf16[10,16,512]{2,1,0:T(8,128)(2,1)S(1)} collective-permute-done((bf16[10,16,512]{2,1,0:T(8,128)(2,1)S(1)}, bf16[10,16,512]{2,1,0:T(8,128)(2,1)S(1)}, u32[]{:S(2)}, u32[]{:S(2)}) %collective-permute-start.24) | collective-permute-done | bytes 163872 | tf_op jit(solution)/shard_map/ppermute | solution.py:389
  211.4 2.1 collective-permute-start.26
  213.5 2.3 collective-permute-start.25
  215.7 4.1 %collective-permute-done.27 = bf16[2,5,16,512]{3,2,1,0:T(8,128)(2,1)S(1)} collective-permute-done((bf16[2,5,16,512]{3,2,1,0:T(8,128)(2,1)S(1)}, bf16[2,5,16,512]{3,2,1,0:T(8,128)(2,1)S(1)}, u32[]{:S(2)}, u32[]{:S(2)}) %collective-permute-start.27) | collective-permute-done | bytes 163872 | tf_op jit(solution)/shard_map/ppermute | solution.py:389
  219.8 1.8 collective-permute-done.25
  221.8 1.3 collective-permute-start.32
  223.2 1.9 collective-permute-start.31
  225.9 2.1 collective-permute-start.29
  228.0 14.4 %collective-permute-done.32 = bf16[2,5,16,512]{3,2,1,0:T(8,128)(2,1)S(1)} collective-permute-done((bf16[2,5,16,512]{3,2,1,0:T(8,128)(2,1)S(1)}, bf16[2,5,16,512]{3,2,1,0:T(8,128)(2,1)S(1)}, u32[]{:S(2)}, u32[]{:S(2)}) %collective-permute-start.32) | collective-permute-done | bytes 163872 | tf_op jit(solution)/shard_map/ppermute | solution.py:389
  242.4 16.2 %collective-permute-done.33 = bf16[2,5,16,512]{3,2,1,0:T(8,128)(2,1)S(1)} collective-permute-done((bf16[2,5,16,512]{3,2,1,0:T(8,128)(2,1)S(1)}, bf16[2,5,16,512]{3,2,1,0:T(8,128)(2,1)S(1)}, u32[]{:S(2)}, u32[]{:S(2)}) %collective-permute-start.33) | collective-permute-done | bytes 163872 | tf_op jit(solution)/shard_map/ppermute | solution.py:389
  258.7 1.0 collective-permute-start.35
  259.7 1.8 collective-permute-start.34
  261.5 2.8 state.1
  264.3 22.0 %collective-permute-done.36.refs_7_ = bf16[4,2,5,16,512]{4,3,2,1,0:T(8,128)(2,1)S(1)} collective-permute-done((bf16[4,2,5,16,512]{4,3,2,1,0:T(8,128)(2,1)S(1)}, bf16[4,2,5,16,512]{4,3,2,1,0:T(8,128)(2,1)S(1)}, u32[]{:S(2)}, u32[]{:S(2)}) %collective-permute-start.36) | collective-permute-done | bytes 655392 | tf_op jit(solution)/shard_map/ppermute | solution.py:389
  286.3 1.8 collective-permute-done.34.refs_5_
  288.1 3.4 %place.1 = bf16[10,512,512]{2,1,0:T(8,128)(2,1)} custom-call(s32[3]{0:T(128)S(1)} %pad_add_fusion.place, bf16[4,2,5,16,512]{4,3,2,1,0:T(8,128)(2,1)S(1)} %pad_maximum_fusion.1.refs_0_, bf16[4,2,5,16,512]{4,3,2,1,0:T(8,128)(2,1)S(1)} %collective-permute-done.28.refs_1_, bf16[4,2,5,16,512]{4,3,2,1,0:T(8,128)(2,1)S(1)} %collective-permute-done.29.refs_2_, ...), custom_call_target="tpu_custom_call" | custom-call | tf_op jit(solution)/shard_map/place/pallas_call | solution.py:376
  (75 shorter events, 11.1 us)
Async XLA Ops:
  3.5 31.9 %collective-permute-start.3 = (bf16[5,4,32,512]{3,2,1,0:T(8,128)(2,1)}, bf16[5,4,32,512]{3,2,1,0:T(8,128)(2,1)S(1)}, u32[]{:S(2)}, u32[]{:S(2)}) collective-permute-start(bf16[5,4,32,512]{3,2,1,0:T(8,128)(2,1)} %get-tuple-element.33), channel_id=1, source_target_pairs={{0,12},{4,0},{8,4},{12,8},{16,28},{20,16},{24,20},{28,24},{32,44},... | collective-permute-start | bytes 1966088 | tf_op jit(solution)/shard_map/ppermute | solution.py:419
  4.4 32.8 %collective-permute-start.2 = (bf16[5,4,32,512]{3,2,1,0:T(8,128)(2,1)}, bf16[5,4,32,512]{3,2,1,0:T(8,128)(2,1)S(1)}, u32[]{:S(2)}, u32[]{:S(2)}) collective-permute-start(bf16[5,4,32,512]{3,2,1,0:T(8,128)(2,1)} %get-tuple-element.34), channel_id=1, source_target_pairs={{0,8},{4,12},{8,0},{12,4},{16,24},{20,28},{24,16},{28,20},{32,40},... | collective-permute-start | bytes 1966088 | tf_op jit(solution)/shard_map/ppermute | solution.py:419
  5.5 31.7 %collective-permute-start.1 = (bf16[5,4,32,512]{3,2,1,0:T(8,128)(2,1)}, bf16[5,4,32,512]{3,2,1,0:T(8,128)(2,1)S(1)}, u32[]{:S(2)}, u32[]{:S(2)}) collective-permute-start(bf16[5,4,32,512]{3,2,1,0:T(8,128)(2,1)} %get-tuple-element.35), channel_id=1, source_target_pairs={{0,4},{4,8},{8,12},{12,0},{16,20},{20,24},{24,28},{28,16},{32,36},... | collective-permute-start | bytes 1966088 | tf_op jit(solution)/shard_map/ppermute | solution.py:419
  10.4 35.2 %collective-permute-start.9 = (bf16[5,4,32,512]{3,2,1,0:T(8,128)(2,1)}, bf16[5,4,32,512]{3,2,1,0:T(8,128)(2,1)S(1)}, u32[]{:S(2)}, u32[]{:S(2)}) collective-permute-start(bf16[5,4,32,512]{3,2,1,0:T(8,128)(2,1)} %get-tuple-element.30), channel_id=1, source_target_pairs={{0,48},{4,52},{8,56},{12,60},{16,0},{20,4},{24,8},{28,12},{32,16},... | collective-permute-start | bytes 1966088 | tf_op jit(solution)/shard_map/ppermute | solution.py:422
  10.9 36.2 %collective-permute-start.8 = (bf16[5,4,32,512]{3,2,1,0:T(8,128)(2,1)}, bf16[5,4,32,512]{3,2,1,0:T(8,128)(2,1)S(1)}, u32[]{:S(2)}, u32[]{:S(2)}) collective-permute-start(bf16[5,4,32,512]{3,2,1,0:T(8,128)(2,1)} %get-tuple-element.31), channel_id=1, source_target_pairs={{0,32},{4,36},{8,40},{12,44},{16,48},{20,52},{24,56},{28,60},{32,0... | collective-permute-start | bytes 1966088 | tf_op jit(solution)/shard_map/ppermute | solution.py:422
  35.5 17.9 %collective-permute-start.7 = (bf16[5,4,32,512]{3,2,1,0:T(8,128)(2,1)}, bf16[5,4,32,512]{3,2,1,0:T(8,128)(2,1)}, u32[]{:S(2)}, u32[]{:S(2)}) collective-permute-start(bf16[5,4,32,512]{3,2,1,0:T(8,128)(2,1)} %get-tuple-element.32), channel_id=1, source_target_pairs={{0,16},{4,20},{8,24},{12,28},{16,32},{20,36},{24,40},{28,44},{32,4... | collective-permute-start | bytes 1966088 | tf_op jit(solution)/shard_map/ppermute | solution.py:422
  37.1 2.5 copy-start
  42.4 0.7 copy-start.5
  43.1 18.5 %copy-start.13 = (s32[1,10]{1,0:T(1,128)S(1)}, s32[1,10]{1,0:T(1,128)}, u32[]{:S(2)}) copy-start(s32[1,10]{1,0:T(1,128)} %param.5) | copy-start | bytes 124
  43.1 17.2 %collective-permute-start.4 = (f32[5,32,512]{2,1,0:T(8,128)S(1)}, f32[5,32,512]{2,1,0:T(8,128)S(1)}, u32[]{:S(2)}, u32[]{:S(2)}) collective-permute-start(f32[5,32,512]{2,1,0:T(8,128)S(1)} %get-tuple-element.17), channel_id=1, source_target_pairs={{0,16},{4,20},{8,24},{12,28},{16,32},{20,36},{24,40},{28,44},{32,4... | collective-permute-start | bytes 983048 | tf_op jit(solution)/shard_map/ppermute | solution.py:425
  44.4 17.5 %collective-permute-start.5 = (f32[5,32,512]{2,1,0:T(8,128)}, f32[5,32,512]{2,1,0:T(8,128)S(1)}, u32[]{:S(2)}, u32[]{:S(2)}) collective-permute-start(f32[5,32,512]{2,1,0:T(8,128)} %get-tuple-element.18), channel_id=1, source_target_pairs={{0,32},{4,36},{8,40},{12,44},{16,48},{20,52},{24,56},{28,60},{32,0... | collective-permute-start | bytes 983048 | tf_op jit(solution)/shard_map/ppermute | solution.py:425
  45.6 17.0 %collective-permute-start.6 = (f32[5,32,512]{2,1,0:T(8,128)}, f32[5,32,512]{2,1,0:T(8,128)S(1)}, u32[]{:S(2)}, u32[]{:S(2)}) collective-permute-start(f32[5,32,512]{2,1,0:T(8,128)} %get-tuple-element.19), channel_id=1, source_target_pairs={{0,48},{4,52},{8,56},{12,60},{16,0},{20,4},{24,8},{28,12},{32,16},... | collective-permute-start | bytes 983048 | tf_op jit(solution)/shard_map/ppermute | solution.py:425
  47.0 0.8 copy-start.3
  53.4 1.1 copy-start.4
  54.5 19.6 %copy-start.6 = (f32[5,32,512]{2,1,0:T(8,128)S(1)}, f32[5,32,512]{2,1,0:T(8,128)}, u32[]{:S(2)}) copy-start(f32[5,32,512]{2,1,0:T(8,128)} %copy-done.5) | copy-start | bytes 983044
  58.9 0.7 copy-start.11
  59.6 9.5 %collective-permute-start.10 = (f32[5,32,512]{2,1,0:T(8,128)}, f32[5,32,512]{2,1,0:T(8,128)S(1)}, u32[]{:S(2)}, u32[]{:S(2)}) collective-permute-start(f32[5,32,512]{2,1,0:T(8,128)} %get-tuple-element.21), channel_id=1, source_target_pairs={{0,4},{4,8},{8,12},{12,0},{16,20},{20,24},{24,28},{28,16},{32,36},... | collective-permute-start | bytes 983048 | tf_op jit(solution)/shard_map/ppermute | solution.py:426
  59.6 11.1 %collective-permute-start.11 = (f32[5,32,512]{2,1,0:T(8,128)}, f32[5,32,512]{2,1,0:T(8,128)S(1)}, u32[]{:S(2)}, u32[]{:S(2)}) collective-permute-start(f32[5,32,512]{2,1,0:T(8,128)} %get-tuple-element.22), channel_id=1, source_target_pairs={{0,8},{4,12},{8,0},{12,4},{16,24},{20,28},{24,16},{28,20},{32,40},... | collective-permute-start | bytes 983048 | tf_op jit(solution)/shard_map/ppermute | solution.py:426
  60.3 13.8 %collective-permute-start.12 = (f32[5,32,512]{2,1,0:T(8,128)}, f32[5,32,512]{2,1,0:T(8,128)S(1)}, u32[]{:S(2)}, u32[]{:S(2)}) collective-permute-start(f32[5,32,512]{2,1,0:T(8,128)} %get-tuple-element.23), channel_id=1, source_target_pairs={{0,12},{4,0},{8,4},{12,8},{16,28},{20,16},{24,20},{28,24},{32,44},... | collective-permute-start | bytes 983048 | tf_op jit(solution)/shard_map/ppermute | solution.py:426
  61.9 0.7 copy-start.7
  62.7 0.7 copy-start.9
  74.1 1.0 copy-start.8
  75.1 1.0 copy-start.10
  76.0 1.0 copy-start.12
  77.9 10.0 %collective-permute-start.13 = (f32[2,5,16,512]{3,2,1,0:T(8,128)S(1)}, f32[2,5,16,512]{3,2,1,0:T(8,128)S(1)}, u32[]{:S(2)}, u32[]{:S(2)}) collective-permute-start(f32[2,5,16,512]{3,2,1,0:T(8,128)S(1)} %get-tuple-element.25), channel_id=1, source_target_pairs={{0,64},{4,68},{8,72},{12,76},{16,80},{20,84},{24,88},{28,92},{32,9... | collective-permute-start | bytes 983048 | tf_op jit(solution)/shard_map/ppermute | solution.py:428
  88.9 1.3 copy-start.1
  90.2 34.4 %all-to-all-start = ((f32[32,2,16,512]{3,2,1,0:T(8,128)}), f32[32,2,16,512]{3,2,1,0:T(8,128)S(1)}, u32[]{:S(2)}, u32[]{:S(2)}) async-start(f32[32,2,16,512]{3,2,1,0:T(8,128)} %copy-done.1), calls=%async_computation | async-start | bytes 4194304 | tf_op jit(solution)/shard_map/all_to_all | solution.py:429
  103.0 51.9 %collective-permute-start.22 = (f32[1,1,1,2,512,512]{5,4,3,2,1,0:T(8,128)}, f32[1,1,1,2,512,512]{5,4,3,2,1,0:T(8,128)}, u32[]{:S(2)}, u32[]{:S(2)}) collective-permute-start(f32[1,1,1,2,512,512]{5,4,3,2,1,0:T(8,128)} %slice.25), channel_id=1, source_target_pairs={{0,1},{1,0},{2,3},{3,2},{4,5},{5,4},{6,7},{7,6},{8,9},{9,8},{10,11... | collective-permute-start | bytes 6291464 | tf_op jit(solution)/shard_map/ppermute | solution.py:411
  124.7 30.2 %collective-permute-start.21 = (f32[32,1,16,512]{3,2,1,0:T(8,128)S(1)}, f32[32,1,16,512]{3,2,1,0:T(8,128)S(1)}, u32[]{:S(2)}, u32[]{:S(2)}) collective-permute-start(f32[32,1,16,512]{3,2,1,0:T(8,128)S(1)} %slice.28), channel_id=1, source_target_pairs={{0,1},{1,0},{2,3},{3,2},{4,5},{5,4},{6,7},{7,6},{8,9},{9,8},{10,11... | collective-permute-start | bytes 3145736 | tf_op jit(solution)/shard_map/ppermute | solution.py:436
  124.8 2.7 collective-permute-start.14
  127.5 3.6 %collective-permute-start.15 = (f32[8,128]{1,0:T(8,128)S(1)}, f32[8,128]{1,0:T(8,128)S(1)}, u32[]{:S(2)}, u32[]{:S(2)}) collective-permute-start(f32[8,128]{1,0:T(8,128)S(1)} %add.108), channel_id=1, source_target_pairs={{0,2},{1,3},{2,0},{3,1},{4,6},{5,7},{6,4},{7,5},{8,10},{9,11},{10,... | collective-permute-start | bytes 12296 | tf_op jit(solution)/shard_map/ppermute | solution.py:432
  131.1 3.6 %collective-permute-start.16 = (f32[8,128]{1,0:T(8,128)S(1)}, f32[8,128]{1,0:T(8,128)S(1)}, u32[]{:S(2)}, u32[]{:S(2)}) collective-permute-start(f32[8,128]{1,0:T(8,128)S(1)} %add.109), channel_id=1, source_target_pairs={{0,4},{4,0},{8,12},{12,8},{16,20},{20,16},{24,28},{28,24},{32,36},... | collective-permute-start | bytes 12296 | tf_op jit(solution)/shard_map/ppermute | solution.py:432
  134.7 5.1 %collective-permute-start.17 = (f32[8,128]{1,0:T(8,128)S(1)}, f32[8,128]{1,0:T(8,128)S(1)}, u32[]{:S(2)}, u32[]{:S(2)}) collective-permute-start(f32[8,128]{1,0:T(8,128)S(1)} %add.110), channel_id=1, source_target_pairs={{0,8},{4,12},{8,0},{12,4},{16,24},{20,28},{24,16},{28,20},{32,40},... | collective-permute-start | bytes 12296 | tf_op jit(solution)/shard_map/ppermute | solution.py:432
  139.8 3.6 %collective-permute-start.18 = (f32[8,128]{1,0:T(8,128)S(1)}, f32[8,128]{1,0:T(8,128)S(1)}, u32[]{:S(2)}, u32[]{:S(2)}) collective-permute-start(f32[8,128]{1,0:T(8,128)S(1)} %add.111), channel_id=1, source_target_pairs={{0,16},{4,20},{8,24},{12,28},{16,0},{20,4},{24,8},{28,12},{32,48},... | collective-permute-start | bytes 12296 | tf_op jit(solution)/shard_map/ppermute | solution.py:432
  143.4 5.1 %collective-permute-start.19 = (f32[8,128]{1,0:T(8,128)S(1)}, f32[8,128]{1,0:T(8,128)S(1)}, u32[]{:S(2)}, u32[]{:S(2)}) collective-permute-start(f32[8,128]{1,0:T(8,128)S(1)} %add.112), channel_id=1, source_target_pairs={{0,32},{4,36},{8,40},{12,44},{16,48},{20,52},{24,56},{28,60},{32,0... | collective-permute-start | bytes 12296 | tf_op jit(solution)/shard_map/ppermute | solution.py:432
  146.1 3.2 %collective-permute-start = (s32[1]{0:T(128)}, s32[1]{0:T(128)}, u32[]{:S(2)}, u32[]{:S(2)}) collective-permute-start(s32[1]{0:T(128)} %get-tuple-element.38), channel_id=1, source_target_pairs={{0,1},{1,0},{2,3},{3,2},{4,5},{5,4},{6,7},{7,6},{8,9},{9,8},{10,11... | collective-permute-start | bytes 20 | tf_op jit(solution)/shard_map/ppermute | solution.py:410
  148.6 5.1 %collective-permute-start.20 = (f32[8,128]{1,0:T(8,128)S(1)}, f32[8,128]{1,0:T(8,128)S(1)}, u32[]{:S(2)}, u32[]{:S(2)}) collective-permute-start(f32[8,128]{1,0:T(8,128)S(1)} %add.113), channel_id=1, source_target_pairs={{0,64},{4,68},{8,72},{12,76},{16,80},{20,84},{24,88},{28,92},{32,9... | collective-permute-start | bytes 12296 | tf_op jit(solution)/shard_map/ppermute | solution.py:432
  154.9 2.2 copy-start.2
  178.6 2.0 collective-permute-start.23
  203.8 7.4 %collective-permute-start.24 = (bf16[10,16,512]{2,1,0:T(8,128)(2,1)S(1)}, bf16[10,16,512]{2,1,0:T(8,128)(2,1)S(1)}, u32[]{:S(2)}, u32[]{:S(2)}) collective-permute-start(bf16[10,16,512]{2,1,0:T(8,128)(2,1)S(1)} %pick.1), channel_id=1, source_target_pairs={{0,64},{4,68},{8,72},{12,76},{16,80},{20,84},{24,88},{28,92},{32,9... | collective-permute-start | bytes 491528 | tf_op jit(solution)/shard_map/ppermute | solution.py:389
  211.3 8.5 %collective-permute-start.27 = (bf16[2,5,16,512]{3,2,1,0:T(8,128)(2,1)S(1)}, bf16[2,5,16,512]{3,2,1,0:T(8,128)(2,1)S(1)}, u32[]{:S(2)}, u32[]{:S(2)}) collective-permute-start(bf16[2,5,16,512]{3,2,1,0:T(8,128)(2,1)S(1)} %get-tuple-element.37), channel_id=1, source_target_pairs={{0,48},{4,52},{8,56},{12,60},{16,0},{20,4},{24,8},{28,12},{32,16},... | collective-permute-start | bytes 491528 | tf_op jit(solution)/shard_map/ppermute | solution.py:389
  211.4 8.5 %collective-permute-start.26 = (bf16[2,5,16,512]{3,2,1,0:T(8,128)(2,1)S(1)}, bf16[2,5,16,512]{3,2,1,0:T(8,128)(2,1)S(1)}, u32[]{:S(2)}, u32[]{:S(2)}) collective-permute-start(bf16[2,5,16,512]{3,2,1,0:T(8,128)(2,1)S(1)} %get-tuple-element.37), channel_id=1, source_target_pairs={{0,32},{4,36},{8,40},{12,44},{16,48},{20,52},{24,56},{28,60},{32,0... | collective-permute-start | bytes 491528 | tf_op jit(solution)/shard_map/ppermute | solution.py:389
  213.5 8.2 %collective-permute-start.25 = (bf16[2,5,16,512]{3,2,1,0:T(8,128)(2,1)S(1)}, bf16[2,5,16,512]{3,2,1,0:T(8,128)(2,1)S(1)}, u32[]{:S(2)}, u32[]{:S(2)}) collective-permute-start(bf16[2,5,16,512]{3,2,1,0:T(8,128)(2,1)S(1)} %get-tuple-element.37), channel_id=1, source_target_pairs={{0,16},{4,20},{8,24},{12,28},{16,32},{20,36},{24,40},{28,44},{32,4... | collective-permute-start | bytes 491528 | tf_op jit(solution)/shard_map/ppermute | solution.py:389
  221.8 37.9 %collective-permute-start.30 = (bf16[4,2,5,16,512]{4,3,2,1,0:T(8,128)(2,1)S(1)}, bf16[4,2,5,16,512]{4,3,2,1,0:T(8,128)(2,1)S(1)}, u32[]{:S(2)}, u32[]{:S(2)}) collective-permute-start(bf16[4,2,5,16,512]{4,3,2,1,0:T(8,128)(2,1)S(1)} %pad_maximum_fusion.1.refs_0_), channel_id=1, source_target_pairs={{0,12},{4,0},{8,4},{12,8},{16,28},{20,16},{24,20},{28,24},{32,44},... | collective-permute-start | bytes 1966088 | tf_op jit(solution)/shard_map/ppermute | solution.py:389
  221.8 20.5 %collective-permute-start.32 = (bf16[2,5,16,512]{3,2,1,0:T(8,128)(2,1)S(1)}, bf16[2,5,16,512]{3,2,1,0:T(8,128)(2,1)S(1)}, u32[]{:S(2)}, u32[]{:S(2)}) collective-permute-start(bf16[2,5,16,512]{3,2,1,0:T(8,128)(2,1)S(1)} %get-tuple-element.36), channel_id=1, source_target_pairs={{0,8},{4,12},{8,0},{12,4},{16,24},{20,28},{24,16},{28,20},{32,40},... | collective-permute-start | bytes 491528 | tf_op jit(solution)/shard_map/ppermute | solution.py:389
  223.2 19.2 %collective-permute-start.31 = (bf16[2,5,16,512]{3,2,1,0:T(8,128)(2,1)S(1)}, bf16[2,5,16,512]{3,2,1,0:T(8,128)(2,1)S(1)}, u32[]{:S(2)}, u32[]{:S(2)}) collective-permute-start(bf16[2,5,16,512]{3,2,1,0:T(8,128)(2,1)S(1)} %get-tuple-element.36), channel_id=1, source_target_pairs={{0,4},{4,8},{8,12},{12,0},{16,20},{20,24},{24,28},{28,16},{32,36},... | collective-permute-start | bytes 491528 | tf_op jit(solution)/shard_map/ppermute | solution.py:389
  225.1 33.4 %collective-permute-start.33 = (bf16[2,5,16,512]{3,2,1,0:T(8,128)(2,1)S(1)}, bf16[2,5,16,512]{3,2,1,0:T(8,128)(2,1)S(1)}, u32[]{:S(2)}, u32[]{:S(2)}) collective-permute-start(bf16[2,5,16,512]{3,2,1,0:T(8,128)(2,1)S(1)} %get-tuple-element.36), channel_id=1, source_target_pairs={{0,12},{4,0},{8,4},{12,8},{16,28},{20,16},{24,20},{28,24},{32,44},... | collective-permute-start | bytes 491528 | tf_op jit(solution)/shard_map/ppermute | solution.py:389
  225.9 38.3 %collective-permute-start.29 = (bf16[4,2,5,16,512]{4,3,2,1,0:T(8,128)(2,1)S(1)}, bf16[4,2,5,16,512]{4,3,2,1,0:T(8,128)(2,1)S(1)}, u32[]{:S(2)}, u32[]{:S(2)}) collective-permute-start(bf16[4,2,5,16,512]{4,3,2,1,0:T(8,128)(2,1)S(1)} %pad_maximum_fusion.1.refs_0_), channel_id=1, source_target_pairs={{0,8},{4,12},{8,0},{12,4},{16,24},{20,28},{24,16},{28,20},{32,40},... | collective-permute-start | bytes 1966088 | tf_op jit(solution)/shard_map/ppermute | solution.py:389
  242.4 21.9 %collective-permute-start.28 = (bf16[4,2,5,16,512]{4,3,2,1,0:T(8,128)(2,1)S(1)}, bf16[4,2,5,16,512]{4,3,2,1,0:T(8,128)(2,1)S(1)}, u32[]{:S(2)}, u32[]{:S(2)}) collective-permute-start(bf16[4,2,5,16,512]{4,3,2,1,0:T(8,128)(2,1)S(1)} %pad_maximum_fusion.1.refs_0_), channel_id=1, source_target_pairs={{0,4},{4,8},{8,12},{12,0},{16,20},{20,24},{24,28},{28,16},{32,36},... | collective-permute-start | bytes 1966088 | tf_op jit(solution)/shard_map/ppermute | solution.py:389
  258.6 27.7 %collective-permute-start.36 = (bf16[4,2,5,16,512]{4,3,2,1,0:T(8,128)(2,1)S(1)}, bf16[4,2,5,16,512]{4,3,2,1,0:T(8,128)(2,1)S(1)}, u32[]{:S(2)}, u32[]{:S(2)}) collective-permute-start(bf16[4,2,5,16,512]{4,3,2,1,0:T(8,128)(2,1)S(1)} %pad_maximum_fusion.2.refs_4_), channel_id=1, source_target_pairs={{0,48},{4,52},{8,56},{12,60},{16,0},{20,4},{24,8},{28,12},{32,16},... | collective-permute-start | bytes 1966088 | tf_op jit(solution)/shard_map/ppermute | solution.py:389
  258.7 27.6 %collective-permute-start.35 = (bf16[4,2,5,16,512]{4,3,2,1,0:T(8,128)(2,1)S(1)}, bf16[4,2,5,16,512]{4,3,2,1,0:T(8,128)(2,1)S(1)}, u32[]{:S(2)}, u32[]{:S(2)}) collective-permute-start(bf16[4,2,5,16,512]{4,3,2,1,0:T(8,128)(2,1)S(1)} %pad_maximum_fusion.2.refs_4_), channel_id=1, source_target_pairs={{0,32},{4,36},{8,40},{12,44},{16,48},{20,52},{24,56},{28,60},{32,0... | collective-permute-start | bytes 1966088 | tf_op jit(solution)/shard_map/ppermute | solution.py:389
  259.7 28.5 %collective-permute-start.34 = (bf16[4,2,5,16,512]{4,3,2,1,0:T(8,128)(2,1)S(1)}, bf16[4,2,5,16,512]{4,3,2,1,0:T(8,128)(2,1)S(1)}, u32[]{:S(2)}, u32[]{:S(2)}) collective-permute-start(bf16[4,2,5,16,512]{4,3,2,1,0:T(8,128)(2,1)S(1)} %pad_maximum_fusion.2.refs_4_), channel_id=1, source_target_pairs={{0,16},{4,20},{8,24},{12,28},{16,32},{20,36},{24,40},{28,44},{32,4... | collective-permute-start | bytes 1966088 | tf_op jit(solution)/shard_map/ppermute | solution.py:389
where the time goes:
time: 292 us
  waiting for transfers between devices  154 us (53%)
  starting transfers between devices  50.6 us (17%)
  Pallas kernels  37.3 us (13%)
  local copies, waits for them, and re-layouts  23.8 us (8%)
  blocking collectives  22.6 us (8%)
    ppermute x13, waiting for transfers between devices, spread(): lax.ppermute(v, 'dp', dp_pairs(dx * k, dy * k, dz * k))  66.3 us
    all_to_all x1, blocking collectives, shards(): lax.all_to_all(outgoing, 'dp', split_axis=0, concat_axis=0, tiled=True)  22.6 us
    ppermute x3, waiting for transfers between devices, shards(): lax.ppermute(piece.reshape(HALF, 4, ROWS, N), 'dp', dp_pairs(k, 0, 0))  22 us
    all_to_all x1, waiting for transfers between devices, shards(): lax.all_to_all(packed, 'dp', split_axis=0, concat_axis=0, tiled=True)  21.6 us
    pallas_call x1, Pallas kernels, run_tasks(): pl.pallas_call(task_kernel, grid=(2,), in_specs=[pl.BlockSpec(memory_spac...  21.5 us
    ppermute x7, waiting for transfers between devices, shards(): lax.ppermute(squares, axis, [(i, i ^ bit) for i in range(size)])  18.9 us
    ppermute x13, starting transfers between devices, spread(): lax.ppermute(v, 'dp', dp_pairs(dx * k, dy * k, dz * k))  15 us
    unnamed x28, local copies, waits for them, and re-layouts  13.7 us
  transfers between devices with their start and end apart: 38, of which 23 were waited for; matrix products, arithmetic and copies ran while one was open for 3% of the time, Pallas kernels for 3%

commit v1 on v0

--- a/solution.py
+++ b/solution.py
@@ -13,6 +13,9 @@
 NDP = 32
 PIECE = N // NDP
 ROWS = 2 * PIECE
+CHUNK = PIECE * N // 128
+MESSAGE = SLOTS * CHUNK + 8
+ENTRIES = N * N * BLK * 4
 HALF = BLK // 2
 TR = 256
 SMALL = 16 << 20
@@ -71,36 +74,25 @@
     return (1.0 / jnp.sqrt(jnp.sqrt(jnp.sqrt(wide))))[0:1, 0:1]
 
 
-def add_kernel(across, place, own, r1, r2, r3, o0, o1, o2, o3, total):
-    value = own[...].reshape(4, ROWS, N).astype(F32)
-    for other in (r1, r2, r3):
-        value += other[...].reshape(4, ROWS, N).astype(F32)
-    total[...] = value
+def add_kernel(across, place, own, r1, r2, r3, *outs):
     here = place[across]
-    for step, out in enumerate((o0, o1, o2, o3)):
-        out[0] = total[lax.rem(here + step, 4)]
-
-
-def add_pieces(place, grads, received, group):
-    if group == 0:
-        own = pl.BlockSpec((1, 1, 4, ROWS, N), lambda b, p: (b, p[0], 0, 0, 0))
-        across = 1
-    else:
-        own = pl.BlockSpec((1, 4, 1, ROWS, N), lambda b, p: (HALF + b, 0, p[1], 0, 0))
-        across = 0
+
+    @pl.loop(0, HALF)
+    def _(b):
+        for step, out in enumerate(outs):
+            j = lax.rem(here + step, 4)
+            out[b] = (own[b, j].astype(F32) + r1[b, j].astype(F32)) + (r2[b, j].astype(F32) + r3[b, j].astype(F32))
+
+
+def add_pieces(place, pieces, across):
     return pl.pallas_call(
         functools.partial(add_kernel, across),
-        grid_spec=pltpu.PrefetchScalarGridSpec(
-            num_scalar_prefetch=1,
-            grid=(HALF,),
-            in_specs=[own] + [pl.BlockSpec((1, 4, ROWS, N), lambda b, p: (b, 0, 0, 0))] * 3,
-            out_specs=[pl.BlockSpec((1, ROWS, N), lambda b, p: (b, 0, 0))] * 4,
-            scratch_shapes=[pltpu.VMEM((4, ROWS, N), F32)],
-        ),
+        in_specs=[pl.BlockSpec(memory_space=pltpu.SMEM)] + [pl.BlockSpec(memory_space=pltpu.VMEM)] * 4,
+        out_specs=[pl.BlockSpec(memory_space=pltpu.VMEM)] * 4,
         out_shape=[jax.ShapeDtypeStruct((HALF, ROWS, N), F32)] * 4,
-        compiler_params=pltpu.CompilerParams(dimension_semantics=("arbitrary",), vmem_limit_bytes=SMALL),
+        compiler_params=pltpu.CompilerParams(vmem_limit_bytes=SMALL),
         cost_estimate=pl.CostEstimate(flops=2_000_000, bytes_accessed=4_000_000, transcendentals=0),
-    )(place, grads, *received)
+    )(place, *pieces)
 
 
 def add_again_kernel(place, *refs):
@@ -133,41 +125,52 @@
     )(place, *first, *second)
 
 
-def pack_kernel(index_ref, keep, recv, out_ref, square_ref, total):
+def pack_kernel(index_ref, keep, recv, out_ref, total):
     squares = jnp.zeros((PIECE, N), F32)
     for b in range(BLK):
         value = keep[b // HALF, b % HALF] + recv[b // HALF, b % HALF]
-        total[b] = value
+        for c in range(4):
+            total[b, pl.ds(c * PIECE, PIECE), :] = value[:, c * 128 : (c + 1) * 128]
         squares += value * value
-    square_ref[...] = jnp.broadcast_to(jnp.sum(squares), square_ref.shape)
+    square = jnp.broadcast_to(jnp.sum(squares), (8, 128))
 
     @pl.loop(0, NDP)
     def _(o):
         for s in range(SLOTS):
-            out_ref[o, s] = total[index_ref[s, o]]
+            out_ref[o, pl.ds(s * CHUNK, CHUNK), :] = total[index_ref[s, o]]
+        out_ref[o, pl.ds(SLOTS * CHUNK, 8), :] = square
 
 
 def pack(index, keep, recv):
     return pl.pallas_call(
         pack_kernel,
         in_specs=[pl.BlockSpec(memory_space=pltpu.SMEM)] + [pl.BlockSpec(memory_space=pltpu.VMEM)] * 2,
-        out_specs=[pl.BlockSpec(memory_space=pltpu.VMEM)] * 2,
-        out_shape=[
-            jax.ShapeDtypeStruct((NDP, SLOTS, PIECE, N), F32),
-            jax.ShapeDtypeStruct((8, 128), F32),
-        ],
-        scratch_shapes=[pltpu.VMEM((BLK, PIECE, N), F32)],
+        out_specs=pl.BlockSpec(memory_space=pltpu.VMEM),
+        out_shape=jax.ShapeDtypeStruct((NDP, MESSAGE, 128), F32),
+        scratch_shapes=[pltpu.VMEM((BLK, CHUNK, 128), F32)],
         compiler_params=pltpu.CompilerParams(vmem_limit_bytes=SMALL),
         cost_estimate=pl.CostEstimate(flops=300_000, bytes_accessed=3_000_000, transcendentals=0),
         name="pack",
     )(index, keep, recv)
 
 
+def unpack(full, ref, offset, scale):
+    for source in range(NDP):
+        for c in range(4):
+            piece = ref[source, pl.ds(offset + c * PIECE, PIECE), :]
+            full[pl.ds(piece_row(source), PIECE), pl.ds(c * 128, 128)] = piece * scale
+
+
+def clip_of(sums):
+    total = (sums[0][...] + sums[1][...]) + (sums[2][...] + sums[3][...])
+    return (1.0 / jnp.sqrt(total / ENTRIES + tiny_offset))[0:1, 0:1]
+
+
 def piece_row(device):
     return (device % 4) * 128 + (device // 4 % 4) * ROWS + (device // 16) * PIECE
 
 
-def task_kernel(occ, clip, own_g, own_old, other_g, other_old, own_dir, other_dir, g2, gt2, full, m, f, p, q, m1, f1, x, u, norms):
+def task_kernel(occ, s0, s1, s2, s3, own_g, own_old, other_g, other_old, own_dir, other_dir, g2, gt2, full, m, f, p, q, m1, f1, x, u, old, norms, sem):
     task = pl.program_id(0)
 
     def halves_to(ref):
@@ -178,15 +181,17 @@
 
     @pl.when(occ[task] > 0)
     def _():
+        clip = clip_of((s0, s1, s2, s3))
+
         @pl.when(task == 0)
         def _():
-            for source in range(NDP):
-                full[pl.ds(piece_row(source), PIECE), :] = other_g[source, 0] * clip[0]
+            pltpu.make_async_copy(other_old.at[0, 0, 0], old, sem).start()
+            unpack(full, other_g, 0, clip)
 
         @pl.when(task == 1)
         def _():
-            for source in range(NDP):
-                full[pl.ds(piece_row(source), PIECE), :] = own_g[source, 0] * clip[0]
+            pltpu.make_async_copy(own_old.at[0, 0, 0], old, sem).start()
+            unpack(full, own_g, 0, clip)
 
         g = full[...]
         squares = jnp.sum(g * g)
@@ -203,19 +208,13 @@
             @pl.when(side == 0)
             def _():
                 gram(g2, gt2)
+                pltpu.make_async_copy(own_old.at[0, 0, 0], old, sem).wait()
 
             @pl.when(side == 1)
             def _():
                 gram(gt2, g2)
 
-            @pl.when(task == 0)
-            def _():
-                full[...] += decay_rate * other_old[0, 0, 0, side]
-
-            @pl.when(task == 1)
-            def _():
-                full[...] += decay_rate * own_old[0, 0, 0, side]
-
+            full[...] += decay_rate * old[side]
             whole = full[...]
             norm2 = jnp.sum(whole * whole)
             norms[side] = norm2
@@ -269,30 +268,31 @@
     return pltpu.VMEM((2, N, N), BF)
 
 
-def run_tasks(occupied, clip, own_g, own_pairs, other_g, other_pair):
+def run_tasks(occupied, sums, own_g, own_pairs, other_g, other_pair):
     result = jax.ShapeDtypeStruct((NDP, 1, PIECE, N), BF)
     return pl.pallas_call(
         task_kernel,
         grid=(2,),
-        in_specs=[pl.BlockSpec(memory_space=pltpu.SMEM)] * 2 + [pl.BlockSpec(memory_space=pltpu.VMEM)] * 4,
+        in_specs=[pl.BlockSpec(memory_space=pltpu.SMEM)]
+        + [pl.BlockSpec(memory_space=pltpu.VMEM)] * 4
+        + [pl.BlockSpec(memory_space=space) for space in (pltpu.VMEM, pltpu.HBM, pltpu.VMEM, pltpu.HBM)],
         out_specs=[pl.BlockSpec(memory_space=pltpu.VMEM)] * 2,
         out_shape=[result, result],
         scratch_shapes=[pair(), pair(), pltpu.VMEM((N, N), F32)]
         + [pair() for _ in range(7)]
-        + [pltpu.VMEM((2, 2, N, N), BF), pltpu.SMEM((2,), F32)],
+        + [pltpu.VMEM((2, 2, N, N), BF), pltpu.VMEM((2, N, N), F32), pltpu.SMEM((2,), F32), pltpu.SemaphoreType.DMA],
         compiler_params=pltpu.CompilerParams(dimension_semantics=("arbitrary",), vmem_limit_bytes=36 << 20),
         cost_estimate=pl.CostEstimate(flops=16_000_000_000, bytes_accessed=3_500_000, transcendentals=0),
         name="tasks",
-    )(occupied, clip, own_g, own_pairs, other_g, other_pair)
-
-
-def state_kernel(occ, clip, g_ref, old_ref, new_ref, full, g2, gt2):
+    )(occupied, *sums, own_g, own_pairs, other_g, other_pair)
+
+
+def state_kernel(occ, s0, s1, s2, s3, g_ref, old_ref, new_ref, full, g2, gt2):
     s = pl.program_id(0)
 
     @pl.when(occ[s] > 0)
     def _():
-        for source in range(NDP):
-            full[pl.ds(piece_row(source), PIECE), :] = g_ref[source, 0] * clip[0]
+        unpack(full, g_ref, pl.multiple_of(s * CHUNK, CHUNK), clip_of((s0, s1, s2, s3)))
         g = full[...]
         store(g2, pl.ds(0, N), g)
         store(gt2, pl.ds(0, N), g.T)
@@ -313,24 +313,23 @@
         new_ref[...] = old_ref[...]
 
 
-def new_state(occupied, clip, gathered, pairs):
+def new_state(occupied, sums, gathered, pairs):
     block = pl.BlockSpec((1, 1, 1, 2, N, N), lambda s: (0, 0, s, 0, 0, 0))
     return pl.pallas_call(
         state_kernel,
         grid=(SLOTS,),
         in_specs=[
             pl.BlockSpec(memory_space=pltpu.SMEM),
-            pl.BlockSpec(memory_space=pltpu.SMEM),
-            pl.BlockSpec((NDP, 1, PIECE, N), lambda s: (0, s, 0, 0)),
-            block,
-        ],
+        ]
+        + [pl.BlockSpec(memory_space=pltpu.VMEM)] * 5
+        + [block],
         out_specs=block,
         out_shape=jax.ShapeDtypeStruct(pairs.shape, F32),
         scratch_shapes=[pltpu.VMEM((N, N), F32), pair(), pair()],
         compiler_params=pltpu.CompilerParams(dimension_semantics=("arbitrary",), vmem_limit_bytes=SMALL),
         cost_estimate=pl.CostEstimate(flops=3_000_000_000, bytes_accessed=10_000_000, transcendentals=0),
         name="state",
-    )(occupied, clip, gathered, pairs)
+    )(occupied, *sums, gathered, pairs)
 
 
 def pick_kernel(owner, slot, recv_ref, out_ref):
@@ -350,19 +349,20 @@
 
 
 def place_kernel(place, *refs):
-    first, second, out, sems = refs[:4], refs[4:8], refs[8], refs[9]
+    groups, out, sems = (refs[:5], refs[5:10]), refs[10], refs[11]
     x, y, z = place[0], place[1], place[2]
     copies = []
     for far in range(4):
         for near in range(4):
             for dz in range(2):
-                for group, dx, dy, ref in ((0, far, near, first[far]), (1, near, far, second[far])):
+                for group, dx, dy in ((0, far, near), (1, near, far)):
+                    here, back, low, high, front = groups[group]
+                    source = (here, back, low if near < 2 else high, front)[far]
                     row = lax.rem(z + dz, 2) * PIECE + lax.rem(y + 4 - dy, 4) * ROWS + lax.rem(x + 4 - dx, 4) * 128
-                    row = pl.multiple_of(row, PIECE)
                     copies.append(
                         pltpu.make_async_copy(
-                            ref.at[near, dz],
-                            out.at[pl.ds(group * HALF, HALF), pl.ds(row, PIECE), :],
+                            source.at[near % 2 if far == 2 else near, dz],
+                            out.at[pl.ds(group * HALF, HALF), pl.ds(pl.multiple_of(row, PIECE), PIECE), :],
                             sems.at[len(copies)],
                         )
                     )
@@ -375,13 +375,20 @@
 def place_all(place, first, second):
     return pl.pallas_call(
         place_kernel,
-        in_specs=[pl.BlockSpec(memory_space=pltpu.SMEM)] + [pl.BlockSpec(memory_space=pltpu.VMEM)] * 8,
+        in_specs=[pl.BlockSpec(memory_space=pltpu.SMEM)] + [pl.BlockSpec(memory_space=pltpu.VMEM)] * 10,
         out_specs=pl.BlockSpec(memory_space=pl.ANY),
         out_shape=jax.ShapeDtypeStruct((BLK, N, N), BF),
         scratch_shapes=[pltpu.SemaphoreType.DMA((64,))],
         compiler_params=pltpu.CompilerParams(vmem_limit_bytes=SMALL),
         name="place",
     )(place, *first, *second)
+
+
+def around(v, dx, dy):
+    ahead, behind = dp_pairs(dx, dy, 0), dp_pairs(3 * dx, 3 * dy, 0)
+    back = lax.ppermute(v, "dp", ahead)
+    front = lax.ppermute(v, "dp", behind)
+    return [v, back, lax.ppermute(back[:2], "dp", ahead), lax.ppermute(front[2:], "dp", behind), front]
 
 
 def spread(v, dx, dy, dz):
@@ -412,31 +419,30 @@
 
     place = jnp.stack([myself % 4, (myself // 4) % 4, myself // 16]).astype(jnp.int32)
     grads = gradients[0].reshape(BLK, 4, 4, ROWS, N)
-    first, second = [], []
+    first, second = [None] * 4, [None] * 4
     zero = jnp.int32(0)
-    for k in range(1, 4):
-        piece = lax.dynamic_slice(grads, (zero, (place[0] + k) % 4, zero, zero, zero), (HALF, 1, 4, ROWS, N))
-        first.append(lax.ppermute(piece.reshape(HALF, 4, ROWS, N), "dp", dp_pairs(k, 0, 0)))
+    for k in (1, 2, 3, 0):
+        start = (zero, (place[0] + k) % 4, zero, zero, zero)
+        piece = lax.dynamic_slice(grads, start, (HALF, 1, 4, ROWS, N)).reshape(HALF, 4, ROWS, N)
+        grads, piece = lax.optimization_barrier((grads, piece))
+        first[k] = lax.ppermute(piece, "dp", dp_pairs(k, 0, 0)) if k else piece
         start = (jnp.int32(HALF), zero, (place[1] + k) % 4, zero, zero)
-        piece = lax.dynamic_slice(grads, start, (HALF, 4, 1, ROWS, N))
-        second.append(lax.ppermute(piece.reshape(HALF, 4, ROWS, N), "dp", dp_pairs(0, k, 0)))
-    first = add_pieces(place, grads, first, 0)
-    second = add_pieces(place, grads, second, 1)
+        piece = lax.dynamic_slice(grads, start, (HALF, 4, 1, ROWS, N)).reshape(HALF, 4, ROWS, N)
+        grads, piece = lax.optimization_barrier((grads, piece))
+        second[k] = lax.ppermute(piece, "dp", dp_pairs(0, k, 0)) if k else piece
+    first = add_pieces(place, first, 1)
+    second = add_pieces(place, second, 0)
     first = [first[0]] + [lax.ppermute(first[k], "dp", dp_pairs(0, k, 0)) for k in range(1, 4)]
     second = [second[0]] + [lax.ppermute(second[k], "dp", dp_pairs(k, 0, 0)) for k in range(1, 4)]
     keep, send = add_again(place, first, second)
-    packed, squares = pack(index, keep, lax.ppermute(send, "dp", dp_pairs(0, 0, 1)))
+    tasks = jnp.concatenate([other_occupied, occupied[0:1]])
+    index, tasks, occupied = lax.optimization_barrier((index, tasks, occupied))
+    packed = pack(index, keep, lax.ppermute(send, "dp", dp_pairs(0, 0, 1)))
     gathered = lax.all_to_all(packed, "dp", split_axis=0, concat_axis=0, tiled=True)
-    hops = [("mp", bit, 4) for bit in (1, 2)] + [("dp", bit, NDP) for bit in (1, 2, 4, 8, 16)]
-    for axis, bit, size in hops:
-        squares = squares + lax.ppermute(squares, axis, [(i, i ^ bit) for i in range(size)])
-    square_sum = squares[0, 0]
-    entries = N * N * BLK * 4
-    clip = (1.0 / jnp.sqrt(square_sum / entries + tiny_offset)).reshape(1)
-    other = lax.ppermute(gathered[:, 1:2], "mp", CORE_PAIRS)
-
-    tasks = jnp.concatenate([other_occupied, occupied[0:1]])
-    own, helped = run_tasks(tasks, clip, gathered, factor_state, other, other_pair)
+    other = lax.ppermute(gathered[:, CHUNK : 2 * CHUNK], "mp", CORE_PAIRS)
+    squares = jnp.sum(gathered[:, SLOTS * CHUNK :], axis=0)
+    sums = [squares] + [lax.ppermute(squares, "mp", [(i, i ^ bit) for i in range(4)]) for bit in (1, 2, 3)]
+    own, helped = run_tasks(tasks, sums, gathered, factor_state, other, other_pair)
     returned = lax.ppermute(helped, "mp", CORE_PAIRS)
     outgoing = jnp.concatenate([own, returned], axis=1)
     incoming = lax.all_to_all(outgoing, "dp", split_axis=0, concat_axis=0, tiled=True)
@@ -445,10 +451,10 @@
     column = jnp.stack(spread(piece, 0, 0, 1))
     first = jnp.stack(spread(column[:, :HALF], 0, 1, 0))
     second = jnp.stack(spread(column[:, HALF:], 1, 0, 0))
-    first = spread(first, 1, 0, 0)
-    second = spread(second, 0, 1, 0)
+    first = around(first, 1, 0)
+    second = around(second, 0, 1)
     directions = place_all(place, first, second)
-    next_state = new_state(occupied, clip, gathered, factor_state)
+    next_state = new_state(occupied, sums, gathered, factor_state)
     return directions, next_state
 
 

time: 292 us -> 235 us (0.80)
  the two profiles are of different devices: /device:TPU:14 before, /device:TPU:2 now
where the time goes in v1:
time: 235 us; the launch traced here: 233 us
  waiting for transfers between devices  90.4 us (38%)
  starting transfers between devices  60.2 us (26%)
  Pallas kernels  35.6 us (15%)
  blocking collectives  23.3 us (10%)
  local copies, waits for them, and re-layouts  19.6 us (8%)
    all_to_all x1, waiting for transfers between devices, shards(): lax.all_to_all(packed, 'dp', split_axis=0, concat_axis=0, tiled=True)  24.3 us
    ppermute x3, waiting for transfers between devices, shards(): second[k] = lax.ppermute(piece, 'dp', dp_pairs(0, k, 0)) if k else piece  23.7 us
    all_to_all x1, blocking collectives, shards(): lax.all_to_all(outgoing, 'dp', split_axis=0, concat_axis=0, tiled=True)  23.3 us
    pallas_call x1, Pallas kernels, run_tasks(): pl.pallas_call(task_kernel, grid=(2,), in_specs=[pl.BlockSpec(memory_spac...  20.6 us
    all_to_all x1, starting transfers between devices, shards(): lax.all_to_all(packed, 'dp', split_axis=0, concat_axis=0, tiled=True)  10.8 us
    ppermute x7, waiting for transfers between devices, spread(): lax.ppermute(v, 'dp', dp_pairs(dx * k, dy * k, dz * k))  9.01 us
    ppermute x3, starting transfers between devices, shards(): lax.ppermute(first[k], 'dp', dp_pairs(0, k, 0))  8.91 us
    ppermute x7, starting transfers between devices, spread(): lax.ppermute(v, 'dp', dp_pairs(dx * k, dy * k, dz * k))  8.66 us
  transfers between devices with their start and end apart: 36, of which 17 were waited for; matrix products, arithmetic and copies ran while one was open for 4% of the time, Pallas kernels for 4%

profile of v1, /device:TPU:2, one launch (start us, length us, event | category | flops | bytes accessed | tf_op | source)
XLA Modules:
  0.0 232.5 jit_solution(8899432623999357309)
XLA Ops:
  0.8 2.0 dynamic-slice_bitcast_fusion.7
  2.8 2.0 dynamic-slice_bitcast_fusion.6
  4.8 2.0 dynamic-slice_bitcast_fusion.5
  6.8 2.0 dynamic-slice_bitcast_fusion.4
  8.8 2.0 dynamic-slice_bitcast_fusion.3
  10.7 1.1 dynamic-slice_bitcast_fusion.2
  11.9 3.1 %collective-permute-start.9 = (bf16[5,4,32,512]{3,2,1,0:T(8,128)(2,1)S(1)}, bf16[5,4,32,512]{3,2,1,0:T(8,128)(2,1)S(1)}, u32[]{:S(2)}, u32[]{:S(2)}) collective-permute-start(bf16[5,4,32,512]{3,2,1,0:T(8,128)(2,1)S(1)} %dynamic-slice_bitcast_fusion.2), channel_id=1, source_target_pairs={{0,48},{4,52},{8,56},{12,60},{16,0},{20,4},{24,8},{28,12},{32,16},... | collective-permute-start | bytes 1966088 | tf_op jit(solution)/shard_map/ppermute | solution.py:432
  15.0 0.5 collective-permute-start.3
  15.5 0.6 collective-permute-start.8
  16.1 2.4 %collective-permute-start.2 = (bf16[5,4,32,512]{3,2,1,0:T(8,128)(2,1)}, bf16[5,4,32,512]{3,2,1,0:T(8,128)(2,1)S(1)}, u32[]{:S(2)}, u32[]{:S(2)}) collective-permute-start(bf16[5,4,32,512]{3,2,1,0:T(8,128)(2,1)} %dynamic-slice_bitcast_fusion.5), channel_id=1, source_target_pairs={{0,8},{4,12},{8,0},{12,4},{16,24},{20,28},{24,16},{28,20},{32,40},... | collective-permute-start | bytes 1966088 | tf_op jit(solution)/shard_map/ppermute | solution.py:428
  18.6 1.0 collective-permute-start.7
  19.5 1.1 dynamic-slice_bitcast_fusion.1.own
  20.7 22.3 %collective-permute-done.9.r3 = bf16[5,4,32,512]{3,2,1,0:T(8,128)(2,1)S(1)} collective-permute-done((bf16[5,4,32,512]{3,2,1,0:T(8,128)(2,1)S(1)}, bf16[5,4,32,512]{3,2,1,0:T(8,128)(2,1)S(1)}, u32[]{:S(2)}, u32[]{:S(2)}) %collective-permute-start.9) | collective-permute-done | bytes 655392 | tf_op jit(solution)/shard_map/ppermute | solution.py:432
  43.0 1.5 collective-permute-start.1
  44.5 1.1 dynamic-slice_bitcast_fusion.own
  45.9 1.4 collective-permute-done.7.r1
  47.3 1.6 shard_map.51
  48.9 1.6 collective-permute-start.10
  50.6 3.4 %collective-permute-start.11 = (f32[5,32,512]{2,1,0:T(8,128)S(1)}, f32[5,32,512]{2,1,0:T(8,128)S(1)}, u32[]{:S(2)}, u32[]{:S(2)}) collective-permute-start(f32[5,32,512]{2,1,0:T(8,128)S(1)} %get-tuple-element.55), channel_id=1, source_target_pairs={{0,8},{4,12},{8,0},{12,4},{16,24},{20,28},{24,16},{28,20},{32,40},... | collective-permute-start | bytes 983048 | tf_op jit(solution)/shard_map/ppermute | solution.py:436
  54.0 0.2 collective-permute-start.12
  54.3 6.7 %collective-permute-done.1.r1 = bf16[5,4,32,512]{3,2,1,0:T(8,128)(2,1)} collective-permute-done((bf16[5,4,32,512]{3,2,1,0:T(8,128)(2,1)}, bf16[5,4,32,512]{3,2,1,0:T(8,128)(2,1)}, u32[]{:S(2)}, u32[]{:S(2)}) %collective-permute-start.1) | collective-permute-done | bytes 655392 | tf_op jit(solution)/shard_map/ppermute | solution.py:428
  60.9 1.4 shard_map.50
  62.5 5.1 %collective-permute-start.5 = (f32[5,32,512]{2,1,0:T(8,128)S(1)}, f32[5,32,512]{2,1,0:T(8,128)S(1)}, u32[]{:S(2)}, u32[]{:S(2)}) collective-permute-start(f32[5,32,512]{2,1,0:T(8,128)S(1)} %get-tuple-element.46), channel_id=1, source_target_pairs={{0,32},{4,36},{8,40},{12,44},{16,48},{20,52},{24,56},{28,60},{32,0... | collective-permute-start | bytes 983048 | tf_op jit(solution)/shard_map/ppermute | solution.py:435
  67.6 0.2 collective-permute-done.10.refs_5_
  67.8 3.7 %collective-permute-start.6 = (f32[5,32,512]{2,1,0:T(8,128)S(1)}, f32[5,32,512]{2,1,0:T(8,128)S(1)}, u32[]{:S(2)}, u32[]{:S(2)}) collective-permute-start(f32[5,32,512]{2,1,0:T(8,128)S(1)} %get-tuple-element.47), channel_id=1, source_target_pairs={{0,48},{4,52},{8,56},{12,60},{16,0},{20,4},{24,8},{28,12},{32,16},... | collective-permute-start | bytes 983048 | tf_op jit(solution)/shard_map/ppermute | solution.py:435
  71.5 0.6 fusion.4
  72.3 2.4 %collective-permute-done.4.refs_1_ = f32[5,32,512]{2,1,0:T(8,128)S(1)} collective-permute-done((f32[5,32,512]{2,1,0:T(8,128)S(1)}, f32[5,32,512]{2,1,0:T(8,128)S(1)}, u32[]{:S(2)}, u32[]{:S(2)}) %collective-permute-start.4) | collective-permute-done | bytes 327712 | tf_op jit(solution)/shard_map/ppermute | solution.py:435
  74.7 3.7 %collective-permute-done.5.refs_2_ = f32[5,32,512]{2,1,0:T(8,128)S(1)} collective-permute-done((f32[5,32,512]{2,1,0:T(8,128)S(1)}, f32[5,32,512]{2,1,0:T(8,128)S(1)}, u32[]{:S(2)}, u32[]{:S(2)}) %collective-permute-start.5) | collective-permute-done | bytes 327712 | tf_op jit(solution)/shard_map/ppermute | solution.py:435
  78.4 0.9 add_again.1
  79.3 4.0 %collective-permute-start.13 = (f32[2,5,16,512]{3,2,1,0:T(8,128)S(1)}, f32[2,5,16,512]{3,2,1,0:T(8,128)S(1)}, u32[]{:S(2)}, u32[]{:S(2)}) collective-permute-start(f32[2,5,16,512]{3,2,1,0:T(8,128)S(1)} %get-tuple-element.58), channel_id=1, source_target_pairs={{0,64},{4,68},{8,72},{12,76},{16,80},{20,84},{24,88},{28,92},{32,9... | collective-permute-start | bytes 983048 | tf_op jit(solution)/shard_map/ppermute | solution.py:440
  83.5 1.4 pad_add_fusion.1.occ
  84.8 4.0 %collective-permute-done.13.recv = f32[2,5,16,512]{3,2,1,0:T(8,128)S(1)} collective-permute-done((f32[2,5,16,512]{3,2,1,0:T(8,128)S(1)}, f32[2,5,16,512]{3,2,1,0:T(8,128)S(1)}, u32[]{:S(2)}, u32[]{:S(2)}) %collective-permute-start.13) | collective-permute-done | bytes 327712 | tf_op jit(solution)/shard_map/ppermute | solution.py:440
  88.8 2.4 %pack.1 = f32[32,136,128]{2,1,0:T(8,128)} custom-call(s32[2,32]{1,0:T(2,128)S(1)} %fusion.1.index_ref, f32[2,5,16,512]{3,2,1,0:T(8,128)S(1)} %get-tuple-element.57.keep, f32[2,5,16,512]{3,2,1,0:T(8,128)S(1)} %collective-permute-done.13.recv), custom_call_target="tpu_custom_call" | custom-call | flops 300000 | bytes 3000000 | tf_op jit(solution)/shard_map/pack/pallas_call | solution.py:145
  91.2 10.8 %all-to-all-start = ((f32[32,136,128]{2,1,0:T(8,128)}), f32[32,136,128]{2,1,0:T(8,128)S(1)}, u32[]{:S(2)}, u32[]{:S(2)}) async-start(f32[32,136,128]{2,1,0:T(8,128)} %pack.1), calls=%async_computation | async-start | bytes 4456448 | tf_op jit(solution)/shard_map/all_to_all | solution.py:441
  102.1 3.1 %slice.37 = f32[1,1,1,2,512,512]{5,4,3,2,1,0:T(8,128)} slice(f32[1,1,2,2,512,512]{5,4,3,2,1,0:T(8,128)} %old_ref.1), slice={[0:1], [0:1], [1:2], [0:2], [0:512], [0:512]} | slice | bytes 4194304 | tf_op jit(solution)/shard_map/slice | solution.py:418
  105.2 24.3 %all-to-all-done.own_g.g_ref = f32[32,136,128]{2,1,0:T(8,128)S(1)} async-done(((f32[32,136,128]{2,1,0:T(8,128)}), f32[32,136,128]{2,1,0:T(8,128)S(1)}, u32[]{:S(2)}, u32[]{:S(2)}) %all-to-all-start) | async-done | bytes 2228256 | tf_op jit(solution)/shard_map/all_to_all | solution.py:441
  129.7 1.2 collective-permute-start.16
  130.9 1.0 collective-permute-start.15
  131.9 0.9 collective-permute-done.16.s3
  132.8 1.7 collective-permute-done.15.s2
  134.5 2.2 copy-done
  136.7 20.6 %tasks.1 = (bf16[32,1,16,512]{3,2,1,0:T(8,128)(2,1)S(1)}, bf16[32,1,16,512]{3,2,1,0:T(8,128)(2,1)S(1)}) custom-call(s32[2]{0:T(128)S(1)} %pad_add_fusion.1.occ, f32[8,128]{1,0:T(8,128)S(1)} %slice_reduce_fusion.s0, f32[8,128]{1,0:T(8,128)S(1)} %collective-permute-done.14.s1, f32[8,128]{1,0:T(8,128)S(1)} %collective-permute-done.15.s2, ...), custom_call_target="tpu_custom_call" | custom-call | flops 16000000000 | bytes 3500000 | tf_op jit(solution)/shard_map/tasks/pallas_call | solution.py:273
  157.4 1.9 collective-permute-done.19
  159.4 23.3 %all_to_all.10.recv_ref = bf16[32,2,16,512]{3,2,1,0:T(8,128)(2,1)S(1)} all-to-all(bf16[32,2,16,512]{3,2,1,0:T(8,128)(2,1)S(1)} %pad_maximum_fusion), channel_id=1, replica_groups=mesh['dp'=32,'mp'=4] {'dp'}, dimensions={0} | all-to-all | bytes 2097152 | tf_op jit(solution)/shard_map/all_to_all | solution.py:448
  182.6 0.6 pick.1
  183.2 0.6 collective-permute-start.20
  183.8 6.3 %collective-permute-done.20 = bf16[10,16,512]{2,1,0:T(8,128)(2,1)S(1)} collective-permute-done((bf16[10,16,512]{2,1,0:T(8,128)(2,1)S(1)}, bf16[10,16,512]{2,1,0:T(8,128)(2,1)S(1)}, u32[]{:S(2)}, u32[]{:S(2)}) %collective-permute-start.20) | collective-permute-done | bytes 163872 | tf_op jit(solution)/shard_map/ppermute | solution.py:396
  190.1 1.3 collective-permute-start.23
  191.4 0.8 collective-permute-start.22
  192.2 0.2 collective-permute-start.21
  192.5 2.3 collective-permute-start.29
  194.8 1.3 collective-permute-start.28
  196.0 2.2 collective-permute-start.30
  198.3 1.7 collective-permute-done.21
  200.1 2.1 collective-permute-start.26
  202.2 0.9 collective-permute-done.30
  203.2 3.6 %collective-permute-start.33 = (bf16[4,2,5,16,512]{4,3,2,1,0:T(8,128)(2,1)S(1)}, bf16[4,2,5,16,512]{4,3,2,1,0:T(8,128)(2,1)S(1)}, u32[]{:S(2)}, u32[]{:S(2)}) collective-permute-start(bf16[4,2,5,16,512]{4,3,2,1,0:T(8,128)(2,1)S(1)} %pad_maximum_fusion.2.refs_5_), channel_id=1, source_target_pairs={{0,48},{4,52},{8,56},{12,60},{16,0},{20,4},{24,8},{28,12},{32,16},... | collective-permute-start | bytes 1966088 | tf_op jit(solution)/shard_map/ppermute | solution.py:390
  206.8 8.3 %collective-permute-done.26.refs_4_ = bf16[4,2,5,16,512]{4,3,2,1,0:T(8,128)(2,1)S(1)} collective-permute-done((bf16[4,2,5,16,512]{4,3,2,1,0:T(8,128)(2,1)S(1)}, bf16[4,2,5,16,512]{4,3,2,1,0:T(8,128)(2,1)S(1)}, u32[]{:S(2)}, u32[]{:S(2)}) %collective-permute-start.26) | collective-permute-done | bytes 655392 | tf_op jit(solution)/shard_map/ppermute | solution.py:390
  215.1 1.9 collective-permute-start.27
  217.1 0.2 collective-permute-start.25
  217.4 3.2 %collective-permute-start.34 = (bf16[2,2,5,16,512]{4,3,2,1,0:T(8,128)(2,1)S(1)}, bf16[2,2,5,16,512]{4,3,2,1,0:T(8,128)(2,1)S(1)}, u32[]{:S(2)}, u32[]{:S(2)}) collective-permute-start(bf16[2,2,5,16,512]{4,3,2,1,0:T(8,128)(2,1)S(1)} %slice.51), channel_id=1, source_target_pairs={{0,48},{4,52},{8,56},{12,60},{16,0},{20,4},{24,8},{28,12},{32,16},... | collective-permute-start | bytes 983048 | tf_op jit(solution)/shard_map/ppermute | solution.py:391
  220.6 4.8 %state.1 = f32[1,1,2,2,512,512]{5,4,3,2,1,0:T(8,128)} custom-call(s32[2]{0:T(128)S(1)} %fusion.3.occ, f32[8,128]{1,0:T(8,128)S(1)} %slice_reduce_fusion.s0, f32[8,128]{1,0:T(8,128)S(1)} %collective-permute-done.14.s1, f32[8,128]{1,0:T(8,128)S(1)} %collective-permute-done.15.s2, f32[8,128]{1,0:T(8,128)S(1)} %collective-permute-done.16.s3, ...), custom_call_target="tpu_custom_call" | custom-call | flops 3000000000 | bytes 10000000 | tf_op jit(solution)/shard_map/state/pallas_call | solution.py:318
  225.4 3.5 %collective-permute-done.32.refs_7_ = bf16[2,2,5,16,512]{4,3,2,1,0:T(8,128)(2,1)S(1)} collective-permute-done((bf16[2,2,5,16,512]{4,3,2,1,0:T(8,128)(2,1)S(1)}, bf16[2,2,5,16,512]{4,3,2,1,0:T(8,128)(2,1)S(1)}, u32[]{:S(2)}, u32[]{:S(2)}) %collective-permute-start.32) | collective-permute-done | bytes 327712 | tf_op jit(solution)/shard_map/ppermute | solution.py:391
  228.9 3.4 %place.1 = bf16[10,512,512]{2,1,0:T(8,128)(2,1)} custom-call(s32[3]{0:T(128)S(1)} %pad_add_fusion.place, bf16[4,2,5,16,512]{4,3,2,1,0:T(8,128)(2,1)S(1)} %pad_maximum_fusion.1.refs_0_, bf16[4,2,5,16,512]{4,3,2,1,0:T(8,128)(2,1)S(1)} %collective-permute-done.24.refs_1_, bf16[2,2,5,16,512]{4,3,2,1,0:T(8,128)(2,1)S(1)} %collective-permute-done.25.refs_2_, ...), custom_call_target="tpu_custom_call" | custom-call | tf_op jit(solution)/shard_map/place/pallas_call | solution.py:376
  (50 shorter events, 1.8 us)
Async XLA Ops:
  0.8 45.0 %copy-start.1 = (s32[1,10]{1,0:T(1,128)S(1)}, s32[1,10]{1,0:T(1,128)}, u32[]{:S(2)}) copy-start(s32[1,10]{1,0:T(1,128)} %param.5) | copy-start | bytes 124
  11.9 31.1 %collective-permute-start.9 = (bf16[5,4,32,512]{3,2,1,0:T(8,128)(2,1)S(1)}, bf16[5,4,32,512]{3,2,1,0:T(8,128)(2,1)S(1)}, u32[]{:S(2)}, u32[]{:S(2)}) collective-permute-start(bf16[5,4,32,512]{3,2,1,0:T(8,128)(2,1)S(1)} %dynamic-slice_bitcast_fusion.2), channel_id=1, source_target_pairs={{0,48},{4,52},{8,56},{12,60},{16,0},{20,4},{24,8},{28,12},{32,16},... | collective-permute-start | bytes 1966088 | tf_op jit(solution)/shard_map/ppermute | solution.py:432
  15.0 39.1 %collective-permute-start.3 = (bf16[5,4,32,512]{3,2,1,0:T(8,128)(2,1)}, bf16[5,4,32,512]{3,2,1,0:T(8,128)(2,1)S(1)}, u32[]{:S(2)}, u32[]{:S(2)}) collective-permute-start(bf16[5,4,32,512]{3,2,1,0:T(8,128)(2,1)} %dynamic-slice_bitcast_fusion.3), channel_id=1, source_target_pairs={{0,12},{4,0},{8,4},{12,8},{16,28},{20,16},{24,20},{28,24},{32,44},... | collective-permute-start | bytes 1966088 | tf_op jit(solution)/shard_map/ppermute | solution.py:428
  15.5 30.4 %collective-permute-start.8 = (bf16[5,4,32,512]{3,2,1,0:T(8,128)(2,1)}, bf16[5,4,32,512]{3,2,1,0:T(8,128)(2,1)}, u32[]{:S(2)}, u32[]{:S(2)}) collective-permute-start(bf16[5,4,32,512]{3,2,1,0:T(8,128)(2,1)} %dynamic-slice_bitcast_fusion.4), channel_id=1, source_target_pairs={{0,32},{4,36},{8,40},{12,44},{16,48},{20,52},{24,56},{28,60},{32,0... | collective-permute-start | bytes 1966088 | tf_op jit(solution)/shard_map/ppermute | solution.py:432
  16.1 38.1 %collective-permute-start.2 = (bf16[5,4,32,512]{3,2,1,0:T(8,128)(2,1)}, bf16[5,4,32,512]{3,2,1,0:T(8,128)(2,1)S(1)}, u32[]{:S(2)}, u32[]{:S(2)}) collective-permute-start(bf16[5,4,32,512]{3,2,1,0:T(8,128)(2,1)} %dynamic-slice_bitcast_fusion.5), channel_id=1, source_target_pairs={{0,8},{4,12},{8,0},{12,4},{16,24},{20,28},{24,16},{28,20},{32,40},... | collective-permute-start | bytes 1966088 | tf_op jit(solution)/shard_map/ppermute | solution.py:428
  18.6 28.7 %collective-permute-start.7 = (bf16[5,4,32,512]{3,2,1,0:T(8,128)(2,1)}, bf16[5,4,32,512]{3,2,1,0:T(8,128)(2,1)}, u32[]{:S(2)}, u32[]{:S(2)}) collective-permute-start(bf16[5,4,32,512]{3,2,1,0:T(8,128)(2,1)} %dynamic-slice_bitcast_fusion.6), channel_id=1, source_target_pairs={{0,16},{4,20},{8,24},{12,28},{16,32},{20,36},{24,40},{28,44},{32,4... | collective-permute-start | bytes 1966088 | tf_op jit(solution)/shard_map/ppermute | solution.py:432
  43.0 17.9 %collective-permute-start.1 = (bf16[5,4,32,512]{3,2,1,0:T(8,128)(2,1)}, bf16[5,4,32,512]{3,2,1,0:T(8,128)(2,1)}, u32[]{:S(2)}, u32[]{:S(2)}) collective-permute-start(bf16[5,4,32,512]{3,2,1,0:T(8,128)(2,1)} %dynamic-slice_bitcast_fusion.7), channel_id=1, source_target_pairs={{0,4},{4,8},{8,12},{12,0},{16,20},{20,24},{24,28},{28,16},{32,36},... | collective-permute-start | bytes 1966088 | tf_op jit(solution)/shard_map/ppermute | solution.py:428
  48.9 18.9 %collective-permute-start.10 = (f32[5,32,512]{2,1,0:T(8,128)S(1)}, f32[5,32,512]{2,1,0:T(8,128)S(1)}, u32[]{:S(2)}, u32[]{:S(2)}) collective-permute-start(f32[5,32,512]{2,1,0:T(8,128)S(1)} %get-tuple-element.54), channel_id=1, source_target_pairs={{0,4},{4,8},{8,12},{12,0},{16,20},{20,24},{24,28},{28,16},{32,36},... | collective-permute-start | bytes 983048 | tf_op jit(solution)/shard_map/ppermute | solution.py:436
  50.6 21.6 %collective-permute-start.11 = (f32[5,32,512]{2,1,0:T(8,128)S(1)}, f32[5,32,512]{2,1,0:T(8,128)S(1)}, u32[]{:S(2)}, u32[]{:S(2)}) collective-permute-start(f32[5,32,512]{2,1,0:T(8,128)S(1)} %get-tuple-element.55), channel_id=1, source_target_pairs={{0,8},{4,12},{8,0},{12,4},{16,24},{20,28},{24,16},{28,20},{32,40},... | collective-permute-start | bytes 983048 | tf_op jit(solution)/shard_map/ppermute | solution.py:436
  54.0 18.2 %collective-permute-start.12 = (f32[5,32,512]{2,1,0:T(8,128)S(1)}, f32[5,32,512]{2,1,0:T(8,128)S(1)}, u32[]{:S(2)}, u32[]{:S(2)}) collective-permute-start(f32[5,32,512]{2,1,0:T(8,128)S(1)} %get-tuple-element.56), channel_id=1, source_target_pairs={{0,12},{4,0},{8,4},{12,8},{16,28},{20,16},{24,20},{28,24},{32,44},... | collective-permute-start | bytes 983048 | tf_op jit(solution)/shard_map/ppermute | solution.py:436
  62.4 12.3 %collective-permute-start.4 = (f32[5,32,512]{2,1,0:T(8,128)S(1)}, f32[5,32,512]{2,1,0:T(8,128)S(1)}, u32[]{:S(2)}, u32[]{:S(2)}) collective-permute-start(f32[5,32,512]{2,1,0:T(8,128)S(1)} %get-tuple-element.45), channel_id=1, source_target_pairs={{0,16},{4,20},{8,24},{12,28},{16,32},{20,36},{24,40},{28,44},{32,4... | collective-permute-start | bytes 983048 | tf_op jit(solution)/shard_map/ppermute | solution.py:435
  62.5 15.9 %collective-permute-start.5 = (f32[5,32,512]{2,1,0:T(8,128)S(1)}, f32[5,32,512]{2,1,0:T(8,128)S(1)}, u32[]{:S(2)}, u32[]{:S(2)}) collective-permute-start(f32[5,32,512]{2,1,0:T(8,128)S(1)} %get-tuple-element.46), channel_id=1, source_target_pairs={{0,32},{4,36},{8,40},{12,44},{16,48},{20,52},{24,56},{28,60},{32,0... | collective-permute-start | bytes 983048 | tf_op jit(solution)/shard_map/ppermute | solution.py:435
  67.8 10.6 %collective-permute-start.6 = (f32[5,32,512]{2,1,0:T(8,128)S(1)}, f32[5,32,512]{2,1,0:T(8,128)S(1)}, u32[]{:S(2)}, u32[]{:S(2)}) collective-permute-start(f32[5,32,512]{2,1,0:T(8,128)S(1)} %get-tuple-element.47), channel_id=1, source_target_pairs={{0,48},{4,52},{8,56},{12,60},{16,0},{20,4},{24,8},{28,12},{32,16},... | collective-permute-start | bytes 983048 | tf_op jit(solution)/shard_map/ppermute | solution.py:435
  72.2 11.2 %collective-permute-start = (s32[1]{0:T(128)}, s32[1]{0:T(128)}, u32[]{:S(2)}, u32[]{:S(2)}) collective-permute-start(s32[1]{0:T(128)} %get-tuple-element.64), channel_id=1, source_target_pairs={{0,1},{1,0},{2,3},{3,2},{4,5},{5,4},{6,7},{7,6},{8,9},{9,8},{10,11... | collective-permute-start | bytes 20 | tf_op jit(solution)/shard_map/ppermute | solution.py:417
  79.3 9.6 %collective-permute-start.13 = (f32[2,5,16,512]{3,2,1,0:T(8,128)S(1)}, f32[2,5,16,512]{3,2,1,0:T(8,128)S(1)}, u32[]{:S(2)}, u32[]{:S(2)}) collective-permute-start(f32[2,5,16,512]{3,2,1,0:T(8,128)S(1)} %get-tuple-element.58), channel_id=1, source_target_pairs={{0,64},{4,68},{8,72},{12,76},{16,80},{20,84},{24,88},{28,92},{32,9... | collective-permute-start | bytes 983048 | tf_op jit(solution)/shard_map/ppermute | solution.py:440
  91.2 38.2 %all-to-all-start = ((f32[32,136,128]{2,1,0:T(8,128)}), f32[32,136,128]{2,1,0:T(8,128)S(1)}, u32[]{:S(2)}, u32[]{:S(2)}) async-start(f32[32,136,128]{2,1,0:T(8,128)} %pack.1), calls=%async_computation | async-start | bytes 4456448 | tf_op jit(solution)/shard_map/all_to_all | solution.py:441
  105.2 26.8 %collective-permute-start.18 = (f32[1,1,1,2,512,512]{5,4,3,2,1,0:T(8,128)}, f32[1,1,1,2,512,512]{5,4,3,2,1,0:T(8,128)}, u32[]{:S(2)}, u32[]{:S(2)}) collective-permute-start(f32[1,1,1,2,512,512]{5,4,3,2,1,0:T(8,128)} %slice.37), channel_id=1, source_target_pairs={{0,1},{1,0},{2,3},{3,2},{4,5},{5,4},{6,7},{7,6},{8,9},{9,8},{10,11... | collective-permute-start | bytes 6291464 | tf_op jit(solution)/shard_map/ppermute | solution.py:418
  129.6 4.9 %collective-permute-start.17 = (f32[32,64,128]{2,1,0:T(8,128)S(1)}, f32[32,64,128]{2,1,0:T(8,128)S(1)}, u32[]{:S(2)}, u32[]{:S(2)}) collective-permute-start(f32[32,64,128]{2,1,0:T(8,128)S(1)} %slice.45), channel_id=1, source_target_pairs={{0,1},{1,0},{2,3},{3,2},{4,5},{5,4},{6,7},{7,6},{8,9},{9,8},{10,11... | collective-permute-start | bytes 3145736 | tf_op jit(solution)/shard_map/ppermute | solution.py:442
  129.7 3.1 %collective-permute-start.16 = (f32[8,128]{1,0:T(8,128)S(1)}, f32[8,128]{1,0:T(8,128)S(1)}, u32[]{:S(2)}, u32[]{:S(2)}) collective-permute-start(f32[8,128]{1,0:T(8,128)S(1)} %slice_reduce_fusion.s0), channel_id=1, source_target_pairs={{0,3},{1,2},{2,1},{3,0},{4,7},{5,6},{6,5},{7,4},{8,11},{9,10},{10,... | collective-permute-start | bytes 12296 | tf_op jit(solution)/shard_map/ppermute | solution.py:444
  130.9 3.6 %collective-permute-start.15 = (f32[8,128]{1,0:T(8,128)S(1)}, f32[8,128]{1,0:T(8,128)S(1)}, u32[]{:S(2)}, u32[]{:S(2)}) collective-permute-start(f32[8,128]{1,0:T(8,128)S(1)} %slice_reduce_fusion.s0), channel_id=1, source_target_pairs={{0,2},{1,3},{2,0},{3,1},{4,6},{5,7},{6,4},{7,5},{8,10},{9,11},{10,... | collective-permute-start | bytes 12296 | tf_op jit(solution)/shard_map/ppermute | solution.py:444
  131.9 2.6 %collective-permute-start.14 = (f32[8,128]{1,0:T(8,128)S(1)}, f32[8,128]{1,0:T(8,128)S(1)}, u32[]{:S(2)}, u32[]{:S(2)}) collective-permute-start(f32[8,128]{1,0:T(8,128)S(1)} %slice_reduce_fusion.s0), channel_id=1, source_target_pairs={{0,1},{1,0},{2,3},{3,2},{4,5},{5,4},{6,7},{7,6},{8,9},{9,8},{10,11... | collective-permute-start | bytes 12296 | tf_op jit(solution)/shard_map/ppermute | solution.py:444
  134.5 2.2 copy-start
  157.3 2.0 collective-permute-start.19
  183.2 6.9 %collective-permute-start.20 = (bf16[10,16,512]{2,1,0:T(8,128)(2,1)S(1)}, bf16[10,16,512]{2,1,0:T(8,128)(2,1)S(1)}, u32[]{:S(2)}, u32[]{:S(2)}) collective-permute-start(bf16[10,16,512]{2,1,0:T(8,128)(2,1)S(1)} %pick.1), channel_id=1, source_target_pairs={{0,64},{4,68},{8,72},{12,76},{16,80},{20,84},{24,88},{28,92},{32,9... | collective-permute-start | bytes 491528 | tf_op jit(solution)/shard_map/ppermute | solution.py:396
  190.1 5.9 %collective-permute-start.23 = (bf16[2,5,16,512]{3,2,1,0:T(8,128)(2,1)S(1)}, bf16[2,5,16,512]{3,2,1,0:T(8,128)(2,1)S(1)}, u32[]{:S(2)}, u32[]{:S(2)}) collective-permute-start(bf16[2,5,16,512]{3,2,1,0:T(8,128)(2,1)S(1)} %get-tuple-element.63), channel_id=1, source_target_pairs={{0,48},{4,52},{8,56},{12,60},{16,0},{20,4},{24,8},{28,12},{32,16},... | collective-permute-start | bytes 491528 | tf_op jit(solution)/shard_map/ppermute | solution.py:396
  191.4 6.9 %collective-permute-start.22 = (bf16[2,5,16,512]{3,2,1,0:T(8,128)(2,1)S(1)}, bf16[2,5,16,512]{3,2,1,0:T(8,128)(2,1)S(1)}, u32[]{:S(2)}, u32[]{:S(2)}) collective-permute-start(bf16[2,5,16,512]{3,2,1,0:T(8,128)(2,1)S(1)} %get-tuple-element.63), channel_id=1, source_target_pairs={{0,32},{4,36},{8,40},{12,44},{16,48},{20,52},{24,56},{28,60},{32,0... | collective-permute-start | bytes 491528 | tf_op jit(solution)/shard_map/ppermute | solution.py:396
  192.2 7.7 %collective-permute-start.21 = (bf16[2,5,16,512]{3,2,1,0:T(8,128)(2,1)S(1)}, bf16[2,5,16,512]{3,2,1,0:T(8,128)(2,1)S(1)}, u32[]{:S(2)}, u32[]{:S(2)}) collective-permute-start(bf16[2,5,16,512]{3,2,1,0:T(8,128)(2,1)S(1)} %get-tuple-element.63), channel_id=1, source_target_pairs={{0,16},{4,20},{8,24},{12,28},{16,32},{20,36},{24,40},{28,44},{32,4... | collective-permute-start | bytes 491528 | tf_op jit(solution)/shard_map/ppermute | solution.py:396
  192.5 9.7 %collective-permute-start.29 = (bf16[2,5,16,512]{3,2,1,0:T(8,128)(2,1)S(1)}, bf16[2,5,16,512]{3,2,1,0:T(8,128)(2,1)S(1)}, u32[]{:S(2)}, u32[]{:S(2)}) collective-permute-start(bf16[2,5,16,512]{3,2,1,0:T(8,128)(2,1)S(1)} %get-tuple-element.62), channel_id=1, source_target_pairs={{0,8},{4,12},{8,0},{12,4},{16,24},{20,28},{24,16},{28,20},{32,40},... | collective-permute-start | bytes 491528 | tf_op jit(solution)/shard_map/ppermute | solution.py:396
  194.8 7.4 %collective-permute-start.28 = (bf16[2,5,16,512]{3,2,1,0:T(8,128)(2,1)S(1)}, bf16[2,5,16,512]{3,2,1,0:T(8,128)(2,1)S(1)}, u32[]{:S(2)}, u32[]{:S(2)}) collective-permute-start(bf16[2,5,16,512]{3,2,1,0:T(8,128)(2,1)S(1)} %get-tuple-element.62), channel_id=1, source_target_pairs={{0,4},{4,8},{8,12},{12,0},{16,20},{20,24},{24,28},{28,16},{32,36},... | collective-permute-start | bytes 491528 | tf_op jit(solution)/shard_map/ppermute | solution.py:396
  196.0 7.1 %collective-permute-start.30 = (bf16[2,5,16,512]{3,2,1,0:T(8,128)(2,1)S(1)}, bf16[2,5,16,512]{3,2,1,0:T(8,128)(2,1)S(1)}, u32[]{:S(2)}, u32[]{:S(2)}) collective-permute-start(bf16[2,5,16,512]{3,2,1,0:T(8,128)(2,1)S(1)} %get-tuple-element.62), channel_id=1, source_target_pairs={{0,12},{4,0},{8,4},{12,8},{16,28},{20,16},{24,20},{28,24},{32,44},... | collective-permute-start | bytes 491528 | tf_op jit(solution)/shard_map/ppermute | solution.py:396
  200.1 15.0 %collective-permute-start.26 = (bf16[4,2,5,16,512]{4,3,2,1,0:T(8,128)(2,1)S(1)}, bf16[4,2,5,16,512]{4,3,2,1,0:T(8,128)(2,1)S(1)}, u32[]{:S(2)}, u32[]{:S(2)}) collective-permute-start(bf16[4,2,5,16,512]{4,3,2,1,0:T(8,128)(2,1)S(1)} %pad_maximum_fusion.1.refs_0_), channel_id=1, source_target_pairs={{0,12},{4,0},{8,4},{12,8},{16,28},{20,16},{24,20},{28,24},{32,44},... | collective-permute-start | bytes 1966088 | tf_op jit(solution)/shard_map/ppermute | solution.py:390
  202.2 14.9 %collective-permute-start.24 = (bf16[4,2,5,16,512]{4,3,2,1,0:T(8,128)(2,1)S(1)}, bf16[4,2,5,16,512]{4,3,2,1,0:T(8,128)(2,1)S(1)}, u32[]{:S(2)}, u32[]{:S(2)}) collective-permute-start(bf16[4,2,5,16,512]{4,3,2,1,0:T(8,128)(2,1)S(1)} %pad_maximum_fusion.1.refs_0_), channel_id=1, source_target_pairs={{0,4},{4,8},{8,12},{12,0},{16,20},{20,24},{24,28},{28,16},{32,36},... | collective-permute-start | bytes 1966088 | tf_op jit(solution)/shard_map/ppermute | solution.py:389
  203.2 14.2 %collective-permute-start.33 = (bf16[4,2,5,16,512]{4,3,2,1,0:T(8,128)(2,1)S(1)}, bf16[4,2,5,16,512]{4,3,2,1,0:T(8,128)(2,1)S(1)}, u32[]{:S(2)}, u32[]{:S(2)}) collective-permute-start(bf16[4,2,5,16,512]{4,3,2,1,0:T(8,128)(2,1)S(1)} %pad_maximum_fusion.2.refs_5_), channel_id=1, source_target_pairs={{0,48},{4,52},{8,56},{12,60},{16,0},{20,4},{24,8},{28,12},{32,16},... | collective-permute-start | bytes 1966088 | tf_op jit(solution)/shard_map/ppermute | solution.py:390
  206.8 13.7 %collective-permute-start.31 = (bf16[4,2,5,16,512]{4,3,2,1,0:T(8,128)(2,1)S(1)}, bf16[4,2,5,16,512]{4,3,2,1,0:T(8,128)(2,1)S(1)}, u32[]{:S(2)}, u32[]{:S(2)}) collective-permute-start(bf16[4,2,5,16,512]{4,3,2,1,0:T(8,128)(2,1)S(1)} %pad_maximum_fusion.2.refs_5_), channel_id=1, source_target_pairs={{0,16},{4,20},{8,24},{12,28},{16,32},{20,36},{24,40},{28,44},{32,4... | collective-permute-start | bytes 1966088 | tf_op jit(solution)/shard_map/ppermute | solution.py:389
  215.1 10.3 %collective-permute-start.27 = (bf16[2,2,5,16,512]{4,3,2,1,0:T(8,128)(2,1)S(1)}, bf16[2,2,5,16,512]{4,3,2,1,0:T(8,128)(2,1)S(1)}, u32[]{:S(2)}, u32[]{:S(2)}) collective-permute-start(bf16[2,2,5,16,512]{4,3,2,1,0:T(8,128)(2,1)S(1)} %slice.49), channel_id=1, source_target_pairs={{0,12},{4,0},{8,4},{12,8},{16,28},{20,16},{24,20},{28,24},{32,44},... | collective-permute-start | bytes 983048 | tf_op jit(solution)/shard_map/ppermute | solution.py:391
  217.1 8.3 %collective-permute-start.25 = (bf16[2,2,5,16,512]{4,3,2,1,0:T(8,128)(2,1)S(1)}, bf16[2,2,5,16,512]{4,3,2,1,0:T(8,128)(2,1)S(1)}, u32[]{:S(2)}, u32[]{:S(2)}) collective-permute-start(bf16[2,2,5,16,512]{4,3,2,1,0:T(8,128)(2,1)S(1)} %slice.48), channel_id=1, source_target_pairs={{0,4},{4,8},{8,12},{12,0},{16,20},{20,24},{24,28},{28,16},{32,36},... | collective-permute-start | bytes 983048 | tf_op jit(solution)/shard_map/ppermute | solution.py:391
  217.4 8.0 %collective-permute-start.34 = (bf16[2,2,5,16,512]{4,3,2,1,0:T(8,128)(2,1)S(1)}, bf16[2,2,5,16,512]{4,3,2,1,0:T(8,128)(2,1)S(1)}, u32[]{:S(2)}, u32[]{:S(2)}) collective-permute-start(bf16[2,2,5,16,512]{4,3,2,1,0:T(8,128)(2,1)S(1)} %slice.51), channel_id=1, source_target_pairs={{0,48},{4,52},{8,56},{12,60},{16,0},{20,4},{24,8},{28,12},{32,16},... | collective-permute-start | bytes 983048 | tf_op jit(solution)/shard_map/ppermute | solution.py:391
  220.5 8.4 %collective-permute-start.32 = (bf16[2,2,5,16,512]{4,3,2,1,0:T(8,128)(2,1)S(1)}, bf16[2,2,5,16,512]{4,3,2,1,0:T(8,128)(2,1)S(1)}, u32[]{:S(2)}, u32[]{:S(2)}) collective-permute-start(bf16[2,2,5,16,512]{4,3,2,1,0:T(8,128)(2,1)S(1)} %slice.50), channel_id=1, source_target_pairs={{0,16},{4,20},{8,24},{12,28},{16,32},{20,36},{24,40},{28,44},{32,4... | collective-permute-start | bytes 983048 | tf_op jit(solution)/shard_map/ppermute | solution.py:391

commit v2 on v1

--- a/solution.py
+++ b/solution.py
@@ -49,16 +49,27 @@
     return jnp.dot(a, b, preferred_element_type=F32)
 
 
-def on_diagonal(r):
-    i = lax.broadcasted_iota(jnp.int32, (TR, N), 0) + r * TR
-    j = lax.broadcasted_iota(jnp.int32, (TR, N), 1)
-    return i == j
+def scaled_eye(value):
+    i = lax.broadcasted_iota(jnp.int32, (TR, TR), 0)
+    j = lax.broadcasted_iota(jnp.int32, (TR, TR), 1)
+    return jnp.where(i == j, value, 0.0)
 
 
 def store(ref, rows, v):
     hi, lo = split(v)
     ref[0, rows, :] = hi
     ref[1, rows, :] = lo
+
+
+def area(i, j):
+    return pl.ds(i * TR, TR), pl.ds(j * TR, TR)
+
+
+def store_block(ref, i, j, v):
+    rows, columns = area(i, j)
+    hi, lo = split(v)
+    ref[0, rows, columns] = hi
+    ref[1, rows, columns] = lo
 
 
 def product(a, b, finish):
@@ -69,9 +80,50 @@
         finish(r, rows, dot(ah, b[0]) + (dot(ah, b[1]) + dot(al, b[0])))
 
 
+def symmetric(a, b, finish):
+    top = pl.ds(0, TR)
+    low = pl.ds(TR, TR)
+    ah = a[0, top, :]
+    al = a[1, top, :]
+    acc = dot(ah, b[0]) + (dot(ah, b[1]) + dot(al, b[0]))
+    finish(0, 0, acc[:, :TR])
+    side = acc[:, TR:]
+    finish(0, 1, side)
+    finish(1, 0, side.T)
+    ah = a[0, low, :]
+    al = a[1, low, :]
+    finish(1, 1, dot(ah, b[0, :, low]) + (dot(ah, b[1, :, low]) + dot(al, b[0, :, low])))
+
+
 def power_eighth(total):
     wide = jnp.full((8, 128), total, F32)
     return (1.0 / jnp.sqrt(jnp.sqrt(jnp.sqrt(wide))))[0:1, 0:1]
+
+
+def cut_kernel(place, grads, *refs):
+    outs, sems = refs[:6], refs[6]
+    copies = []
+    for k in range(1, 4):
+        x = lax.rem(place[0] + k, 4)
+        y = lax.rem(place[1] + k, 4)
+        copies.append(pltpu.make_async_copy(grads.at[pl.ds(0, HALF), x], outs[k - 1], sems.at[k - 1]))
+        copies.append(pltpu.make_async_copy(grads.at[pl.ds(HALF, HALF), :, y], outs[k + 2], sems.at[k + 2]))
+    for copy in copies:
+        copy.start()
+    for copy in copies:
+        copy.wait()
+
+
+def cut(place, grads):
+    return pl.pallas_call(
+        cut_kernel,
+        in_specs=[pl.BlockSpec(memory_space=pltpu.SMEM), pl.BlockSpec(memory_space=pltpu.HBM)],
+        out_specs=[pl.BlockSpec(memory_space=pltpu.VMEM)] * 6,
+        out_shape=[jax.ShapeDtypeStruct((HALF, 4, ROWS, N), BF)] * 6,
+        scratch_shapes=[pltpu.SemaphoreType.DMA((6,))],
+        compiler_params=pltpu.CompilerParams(vmem_limit_bytes=SMALL),
+        name="cut",
+    )(place, pltpu.with_memory_space_constraint(grads, pltpu.HBM))
 
 
 def add_kernel(across, place, own, r1, r2, r3, *outs):
@@ -170,14 +222,15 @@
     return (device % 4) * 128 + (device // 4 % 4) * ROWS + (device // 16) * PIECE
 
 
-def task_kernel(occ, s0, s1, s2, s3, own_g, own_old, other_g, other_old, own_dir, other_dir, g2, gt2, full, m, f, p, q, m1, f1, x, u, old, norms, sem):
+def task_kernel(occ, s0, s1, s2, s3, own_g, own_old, other_g, other_old, own_dir, other_dir, g2, gt2, full, whole, old, norms, sem, *pairs):
+    m, f, p, q, m1, f1, x = (pairs[2 * k : 2 * k + 2] for k in range(7))
     task = pl.program_id(0)
 
     def halves_to(ref):
-        return lambda r, rows, acc: store(ref, rows, acc)
-
-    def factor(r, moving):
-        return jnp.where(on_diagonal(r), 1.25, 0.0) - 0.25 * moving
+        return lambda i, j, acc: store_block(ref, i, j, acc)
+
+    def factor(i, j, moving):
+        return scaled_eye(1.25) - 0.25 * moving if i == j else -0.25 * moving
 
     @pl.when(occ[task] > 0)
     def _():
@@ -198,54 +251,58 @@
         store(g2, pl.ds(0, N), g)
         store(gt2, pl.ds(0, N), g.T)
 
-        def root(side, carry):
-            def gram(a, b):
-                def finish(r, rows, acc):
-                    full[rows, :] = (1.0 - decay_rate) * acc + jnp.where(on_diagonal(r), ridge_term, 0.0)
-
-                product(a, b, finish)
-
-            @pl.when(side == 0)
-            def _():
-                gram(g2, gt2)
-                pltpu.make_async_copy(own_old.at[0, 0, 0], old, sem).wait()
-
-            @pl.when(side == 1)
-            def _():
-                gram(gt2, g2)
-
-            full[...] += decay_rate * old[side]
-            whole = full[...]
-            norm2 = jnp.sum(whole * whole)
+        def gram(side, a, b):
+            def finish(i, j, acc):
+                whole[side, *area(i, j)] = (1.0 - decay_rate) * acc + (scaled_eye(ridge_term) if i == j else 0.0)
+
+            symmetric(a, b, finish)
+
+        gram(0, g2, gt2)
+        gram(1, gt2, g2)
+        pltpu.make_async_copy(own_old.at[0, 0, 0], old, sem).wait()
+        sides = (0, 1)
+        for side in sides:
+            mixed = whole[side] + decay_rate * old[side]
+            whole[side] = mixed
+            norm2 = jnp.sum(mixed * mixed)
             norms[side] = norm2
             inverse = (1.0 / jnp.sqrt(jnp.full((8, 128), norm2, F32)))[0:1, 0:1]
-            for r in range(N // TR):
-                rows = pl.ds(r * TR, TR)
-                moving = full[rows, :] * inverse
-                store(m, rows, moving)
-                store(f, rows, factor(r, moving))
-
-            def first(r, rows, acc):
-                store(m1, rows, acc)
-                store(f1, rows, factor(r, acc))
-
-            product(f, f, halves_to(p))
-            product(p, p, halves_to(q))
-            product(q, m, first)
-            product(f, f1, halves_to(x))
-            product(f1, f1, halves_to(p))
-            product(p, p, halves_to(q))
-            product(q, m1, lambda r, rows, acc: store(m, rows, factor(r, acc)))
-            product(x, m, halves_to(u.at[side]))
-            return carry
-
-        lax.fori_loop(0, 2, root, 0)
+            for i in range(2):
+                for j in range(2):
+                    moving = whole[side, *area(i, j)] * inverse
+                    store_block(m[side], i, j, moving)
+                    store_block(f[side], i, j, factor(i, j, moving))
+
+        def moved(to, factor_to):
+            def finish(i, j, acc):
+                if to is not None:
+                    store_block(to, i, j, acc)
+                store_block(factor_to, i, j, factor(i, j, acc))
+
+            return finish
+
+        for side in sides:
+            symmetric(f[side], f[side], halves_to(p[side]))
+        for side in sides:
+            symmetric(p[side], p[side], halves_to(q[side]))
+        for side in sides:
+            symmetric(q[side], m[side], moved(m1[side], f1[side]))
+        for side in sides:
+            symmetric(f1[side], f1[side], halves_to(p[side]))
+        for side in sides:
+            symmetric(f[side], f1[side], halves_to(x[side]))
+        for side in sides:
+            symmetric(p[side], p[side], halves_to(q[side]))
+        for side in sides:
+            symmetric(q[side], m1[side], moved(None, m[side]))
+        for side in sides:
+            symmetric(x[side], m[side], halves_to(f[side]))
 
         def last(r, rows, acc):
             full[rows, :] = acc
 
-        product(u.at[0], g2, halves_to(p))
-        product(p, u.at[1], last)
+        product(f[0], g2, lambda r, rows, acc: store(p[0], rows, acc))
+        product(p[0], f[1], last)
         precond = full[...] * (power_eighth(norms[0]) * power_eighth(norms[1]))
         entries = N * N
         actual = jnp.full((8, 128), jnp.sum(precond * precond) / entries + tiny_offset, F32)
@@ -279,12 +336,12 @@
         out_specs=[pl.BlockSpec(memory_space=pltpu.VMEM)] * 2,
         out_shape=[result, result],
         scratch_shapes=[pair(), pair(), pltpu.VMEM((N, N), F32)]
-        + [pair() for _ in range(7)]
-        + [pltpu.VMEM((2, 2, N, N), BF), pltpu.VMEM((2, N, N), F32), pltpu.SMEM((2,), F32), pltpu.SemaphoreType.DMA],
+        + [pltpu.VMEM((2, N, N), F32), pltpu.VMEM((2, N, N), F32), pltpu.SMEM((2,), F32), pltpu.SemaphoreType.DMA]
+        + [pair() for _ in range(14)],
         compiler_params=pltpu.CompilerParams(dimension_semantics=("arbitrary",), vmem_limit_bytes=36 << 20),
         cost_estimate=pl.CostEstimate(flops=16_000_000_000, bytes_accessed=3_500_000, transcendentals=0),
         name="tasks",
-    )(occupied, *sums, own_g, own_pairs, other_g, other_pair)
+    )(occupied, *sums, own_g, pltpu.with_memory_space_constraint(own_pairs, pltpu.HBM), other_g, other_pair)
 
 
 def state_kernel(occ, s0, s1, s2, s3, g_ref, old_ref, new_ref, full, g2, gt2):
@@ -348,20 +405,20 @@
     )(owner, slot, recv)
 
 
-def place_kernel(place, *refs):
-    groups, out, sems = (refs[:5], refs[5:10]), refs[10], refs[11]
+def place_kernel(steps, place, *refs):
+    count = 2 * len(steps)
+    groups, out, sems = (refs[: len(steps)], refs[len(steps) : count]), refs[-2], refs[-1]
     x, y, z = place[0], place[1], place[2]
     copies = []
-    for far in range(4):
-        for near in range(4):
+    for number, (far, low) in enumerate(steps):
+        for near in range(2) if far == 2 else range(4):
             for dz in range(2):
-                for group, dx, dy in ((0, far, near), (1, near, far)):
-                    here, back, low, high, front = groups[group]
-                    source = (here, back, low if near < 2 else high, front)[far]
+                for group in range(2):
+                    dx, dy = (far, near + low) if group == 0 else (near + low, far)
                     row = lax.rem(z + dz, 2) * PIECE + lax.rem(y + 4 - dy, 4) * ROWS + lax.rem(x + 4 - dx, 4) * 128
                     copies.append(
                         pltpu.make_async_copy(
-                            source.at[near % 2 if far == 2 else near, dz],
+                            groups[group][number].at[near, dz],
                             out.at[pl.ds(group * HALF, HALF), pl.ds(pl.multiple_of(row, PIECE), PIECE), :],
                             sems.at[len(copies)],
                         )
@@ -372,23 +429,38 @@
         copy.wait()
 
 
-def place_all(place, first, second):
-    return pl.pallas_call(
-        place_kernel,
-        in_specs=[pl.BlockSpec(memory_space=pltpu.SMEM)] + [pl.BlockSpec(memory_space=pltpu.VMEM)] * 10,
+def place_some(place, first, second, steps, placed):
+    refs = [*first, *second] + ([] if placed is None else [placed])
+    return pl.pallas_call(
+        functools.partial(place_kernel, steps),
+        in_specs=[pl.BlockSpec(memory_space=pltpu.SMEM)]
+        + [pl.BlockSpec(memory_space=pltpu.VMEM)] * (2 * len(steps))
+        + ([] if placed is None else [pl.BlockSpec(memory_space=pl.ANY)]),
         out_specs=pl.BlockSpec(memory_space=pl.ANY),
         out_shape=jax.ShapeDtypeStruct((BLK, N, N), BF),
-        scratch_shapes=[pltpu.SemaphoreType.DMA((64,))],
+        scratch_shapes=[pltpu.SemaphoreType.DMA((48 if placed is None else 16,))],
+        input_output_aliases={} if placed is None else {len(refs): 0},
         compiler_params=pltpu.CompilerParams(vmem_limit_bytes=SMALL),
-        name="place",
-    )(place, *first, *second)
+        cost_estimate=pl.CostEstimate(flops=0, bytes_accessed=8_000_000, transcendentals=0),
+        name="place" if placed is None else "place_last",
+    )(place, *refs)
+
+
+def place_all(place, first, second):
+    near = place_some(place, first[:3], second[:3], ((0, 0), (1, 0), (3, 0)), None)
+    return place_some(place, first[3:], second[3:], ((2, 0), (2, 2)), near)
+
+
+def spread(v, dx, dy, dz):
+    steps = 2 if dz else 4
+    return [v] + [lax.ppermute(v, "dp", dp_pairs(dx * k, dy * k, dz * k)) for k in range(1, steps)]
 
 
 def around(v, dx, dy):
     ahead, behind = dp_pairs(dx, dy, 0), dp_pairs(3 * dx, 3 * dy, 0)
     back = lax.ppermute(v, "dp", ahead)
     front = lax.ppermute(v, "dp", behind)
-    return [v, back, lax.ppermute(back[:2], "dp", ahead), lax.ppermute(front[2:], "dp", behind), front]
+    return [v, back, front, lax.ppermute(back[:2], "dp", ahead), lax.ppermute(front[2:], "dp", behind)]
 
 
 def spread(v, dx, dy, dz):
@@ -419,21 +491,22 @@
 
     place = jnp.stack([myself % 4, (myself // 4) % 4, myself // 16]).astype(jnp.int32)
     grads = gradients[0].reshape(BLK, 4, 4, ROWS, N)
+    pieces = cut(place, grads)
+    grads, pieces = lax.optimization_barrier((grads, pieces))
     first, second = [None] * 4, [None] * 4
+    for k in (1, 3, 2):
+        first[k] = lax.ppermute(pieces[k - 1], "dp", dp_pairs(k, 0, 0))
+        second[k] = lax.ppermute(pieces[k + 2], "dp", dp_pairs(0, k, 0))
     zero = jnp.int32(0)
-    for k in (1, 2, 3, 0):
-        start = (zero, (place[0] + k) % 4, zero, zero, zero)
-        piece = lax.dynamic_slice(grads, start, (HALF, 1, 4, ROWS, N)).reshape(HALF, 4, ROWS, N)
-        grads, piece = lax.optimization_barrier((grads, piece))
-        first[k] = lax.ppermute(piece, "dp", dp_pairs(k, 0, 0)) if k else piece
-        start = (jnp.int32(HALF), zero, (place[1] + k) % 4, zero, zero)
-        piece = lax.dynamic_slice(grads, start, (HALF, 4, 1, ROWS, N)).reshape(HALF, 4, ROWS, N)
-        grads, piece = lax.optimization_barrier((grads, piece))
-        second[k] = lax.ppermute(piece, "dp", dp_pairs(0, k, 0)) if k else piece
-    first = add_pieces(place, first, 1)
-    second = add_pieces(place, second, 0)
-    first = [first[0]] + [lax.ppermute(first[k], "dp", dp_pairs(0, k, 0)) for k in range(1, 4)]
-    second = [second[0]] + [lax.ppermute(second[k], "dp", dp_pairs(k, 0, 0)) for k in range(1, 4)]
+    start = (zero, place[0], zero, zero, zero)
+    first[0] = lax.dynamic_slice(grads, start, (HALF, 1, 4, ROWS, N)).reshape(HALF, 4, ROWS, N)
+    start = (jnp.int32(HALF), zero, place[1], zero, zero)
+    second[0] = lax.dynamic_slice(grads, start, (HALF, 4, 1, ROWS, N)).reshape(HALF, 4, ROWS, N)
+    first = list(add_pieces(place, first, 1))
+    second = list(add_pieces(place, second, 0))
+    for k in (1, 3, 2):
+        first[k] = lax.ppermute(first[k], "dp", dp_pairs(0, k, 0))
+        second[k] = lax.ppermute(second[k], "dp", dp_pairs(k, 0, 0))
     keep, send = add_again(place, first, second)
     tasks = jnp.concatenate([other_occupied, occupied[0:1]])
     index, tasks, occupied = lax.optimization_barrier((index, tasks, occupied))

time: 235 us -> 214 us (0.911)
  local copies, waits for them, and re-layouts: 19.6 us -> 7.13 us
  waiting for transfers between devices: 90.4 us -> 85.3 us
  starting transfers between devices: 60.2 us -> 57.5 us
    ppermute x12, waiting for transfers between devices: 36.7 us -> 30.2 us  [the longest x3 19.1 us: shards(): first[k] = lax.ppermute(pieces[k - 1], 'dp', dp_pairs(k, 0, 0))]
    reshape x4 -> x1, local copies, waits for them, and re-layouts: 7.09 us -> 1.14 us  [shards(): lax.dynamic_slice(grads, start, (HALF, 1, 4, ROWS, N))]
    pallas_call x1 -> x3, Pallas kernels: 3.42 us -> 8.98 us  [the longest x2 4.61 us: place_some(): pl.pallas_call(functools.partial(place_kernel, steps), in_specs=[pl.Block...]
    pallas_call x1, Pallas kernels: 20.6 us -> 15.1 us  [run_tasks(): pl.pallas_call(task_kernel, grid=(2,), in_specs=[pl.BlockSpec(memory_spac...]
    reshape x4 -> x1, local copies, waits for them, and re-layouts: 6.29 us -> 1.15 us  [shards(): lax.dynamic_slice(grads, start, (HALF, 4, 1, ROWS, N))]
    all_to_all x1, starting transfers between devices: 10.8 us -> 7.51 us  [shards(): lax.all_to_all(packed, 'dp', split_axis=0, concat_axis=0, tiled=True)]
    ppermute x2, waiting for transfers between devices: 3.51 us -> 0.56 us  [around(): lax.ppermute(back[:2], 'dp', ahead)]
  transfers between devices with their start and end apart: 36 -> 36, of which waited for: 17 -> 17; matrix products, arithmetic and copies ran while one was open for 4% -> 4% of each run, Pallas kernels for 4% -> 5%
where the time goes in v2:
time: 214 us; the launch traced here: 211 us
  waiting for transfers between devices  85.3 us (40%)
  starting transfers between devices  57.5 us (27%)
  Pallas kernels  34.5 us (16%)
  blocking collectives  23.8 us (11%)
  local copies, waits for them, and re-layouts  7.13 us (3%)
  other arithmetic  2.16 us (1%)
    all_to_all x1, waiting for transfers between devices, shards(): lax.all_to_all(packed, 'dp', split_axis=0, concat_axis=0, tiled=True)  26.4 us
    all_to_all x1, blocking collectives, shards(): lax.all_to_all(outgoing, 'dp', split_axis=0, concat_axis=0, tiled=True)  23.8 us
    ppermute x3, waiting for transfers between devices, shards(): first[k] = lax.ppermute(pieces[k - 1], 'dp', dp_pairs(k, 0, 0))  19.1 us
    pallas_call x1, Pallas kernels, run_tasks(): pl.pallas_call(task_kernel, grid=(2,), in_specs=[pl.BlockSpec(memory_spac...  15.1 us
    ppermute x7, waiting for transfers between devices, spread(): lax.ppermute(v, 'dp', dp_pairs(dx * k, dy * k, dz * k))  9.01 us
    ppermute x7, starting transfers between devices, spread(): lax.ppermute(v, 'dp', dp_pairs(dx * k, dy * k, dz * k))  8.66 us
    ppermute x2, waiting for transfers between devices, around(): front = lax.ppermute(v, 'dp', behind)  8.31 us
    all_to_all x1, starting transfers between devices, shards(): lax.all_to_all(packed, 'dp', split_axis=0, concat_axis=0, tiled=True)  7.51 us
  transfers between devices with their start and end apart: 36, of which 17 were waited for; matrix products, arithmetic and copies ran while one was open for 4% of the time, Pallas kernels for 5%

profile of v2, /device:TPU:2, one launch (start us, length us, event | category | flops | bytes accessed | tf_op | source)
XLA Modules:
  0.0 211.5 jit_solution(15813401930019713222)
XLA Ops:
  0.8 4.4 %cut.1 = (bf16[5,4,32,512]{3,2,1,0:T(8,128)(2,1)}, bf16[5,4,32,512]{3,2,1,0:T(8,128)(2,1)}, bf16[5,4,32,512]{3,2,1,0:T(8,128)(2,1)}, bf16[5,4,32,512]{3,2,1,0:T(...) custom-call(s32[3]{0:T(128)S(1)} %pad_add_fusion.place, ...), custom_call_target="tpu_custom_call" | custom-call | tf_op jit(solution)/shard_map/cut/pallas_call | solution.py:118
  5.1 0.8 copy-done.2
  6.0 1.5 collective-permute-start.1
  7.5 1.0 collective-permute-start.2
  8.5 2.3 %collective-permute-start.3 = (bf16[5,4,32,512]{3,2,1,0:T(8,128)(2,1)}, bf16[5,4,32,512]{3,2,1,0:T(8,128)(2,1)S(1)}, u32[]{:S(2)}, u32[]{:S(2)}) collective-permute-start(bf16[5,4,32,512]{3,2,1,0:T(8,128)(2,1)} %get-tuple-element.41), channel_id=1, source_target_pairs={{0,12},{4,0},{8,4},{12,8},{16,28},{20,16},{24,20},{28,24},{32,44},... | collective-permute-start | bytes 1966088 | tf_op jit(solution)/shard_map/ppermute | solution.py:498
  10.7 1.6 collective-permute-start.7
  12.3 2.9 %collective-permute-start.8 = (bf16[5,4,32,512]{3,2,1,0:T(8,128)(2,1)}, bf16[5,4,32,512]{3,2,1,0:T(8,128)(2,1)S(1)}, u32[]{:S(2)}, u32[]{:S(2)}) collective-permute-start(bf16[5,4,32,512]{3,2,1,0:T(8,128)(2,1)} %get-tuple-element.47), channel_id=1, source_target_pairs={{0,32},{4,36},{8,40},{12,44},{16,48},{20,52},{24,56},{28,60},{32,0... | collective-permute-start | bytes 1966088 | tf_op jit(solution)/shard_map/ppermute | solution.py:499
  15.2 8.6 %collective-permute-done.1.r1 = bf16[5,4,32,512]{3,2,1,0:T(8,128)(2,1)S(1)} collective-permute-done((bf16[5,4,32,512]{3,2,1,0:T(8,128)(2,1)}, bf16[5,4,32,512]{3,2,1,0:T(8,128)(2,1)S(1)}, u32[]{:S(2)}, u32[]{:S(2)}) %collective-permute-start.1) | collective-permute-done | bytes 655392 | tf_op jit(solution)/shard_map/ppermute | solution.py:498
  23.8 3.0 %collective-permute-start.9 = (bf16[5,4,32,512]{3,2,1,0:T(8,128)(2,1)}, bf16[5,4,32,512]{3,2,1,0:T(8,128)(2,1)S(1)}, u32[]{:S(2)}, u32[]{:S(2)}) collective-permute-start(bf16[5,4,32,512]{3,2,1,0:T(8,128)(2,1)} %copy-done.2), channel_id=1, source_target_pairs={{0,48},{4,52},{8,56},{12,60},{16,0},{20,4},{24,8},{28,12},{32,16},... | collective-permute-start | bytes 1966088 | tf_op jit(solution)/shard_map/ppermute | solution.py:499
  26.8 1.1 dynamic-slice_bitcast_fusion.1.own
  28.0 10.6 %collective-permute-done.3.r3 = bf16[5,4,32,512]{3,2,1,0:T(8,128)(2,1)S(1)} collective-permute-done((bf16[5,4,32,512]{3,2,1,0:T(8,128)(2,1)}, bf16[5,4,32,512]{3,2,1,0:T(8,128)(2,1)S(1)}, u32[]{:S(2)}, u32[]{:S(2)}) %collective-permute-start.3) | collective-permute-done | bytes 655392 | tf_op jit(solution)/shard_map/ppermute | solution.py:498
  38.6 0.9 shard_map.50
  39.5 1.8 collective-permute-start.4
  41.3 0.2 convert_reduce_fusion.slot
  41.5 0.1 fusion.3.occ
  41.6 1.1 dynamic-slice_bitcast_fusion.own
  42.8 3.0 %collective-permute-start.5 = (f32[5,32,512]{2,1,0:T(8,128)S(1)}, f32[5,32,512]{2,1,0:T(8,128)S(1)}, u32[]{:S(2)}, u32[]{:S(2)}) collective-permute-start(f32[5,32,512]{2,1,0:T(8,128)S(1)} %get-tuple-element.44), channel_id=1, source_target_pairs={{0,32},{4,36},{8,40},{12,44},{16,48},{20,52},{24,56},{28,60},{32,0... | collective-permute-start | bytes 983048 | tf_op jit(solution)/shard_map/ppermute | solution.py:508
  45.7 1.3 collective-permute-start.6
  47.1 0.9 shard_map.51
  48.0 1.4 collective-permute-start.10
  49.3 1.5 collective-permute-start.11
  50.8 2.6 %collective-permute-start.12 = (f32[5,32,512]{2,1,0:T(8,128)S(1)}, f32[5,32,512]{2,1,0:T(8,128)S(1)}, u32[]{:S(2)}, u32[]{:S(2)}) collective-permute-start(f32[5,32,512]{2,1,0:T(8,128)S(1)} %get-tuple-element.52), channel_id=1, source_target_pairs={{0,12},{4,0},{8,4},{12,8},{16,28},{20,16},{24,20},{28,24},{32,44},... | collective-permute-start | bytes 983048 | tf_op jit(solution)/shard_map/ppermute | solution.py:509
  53.4 0.6 fusion.4
  54.1 4.1 %collective-permute-done.5.refs_2_ = f32[5,32,512]{2,1,0:T(8,128)S(1)} collective-permute-done((f32[5,32,512]{2,1,0:T(8,128)S(1)}, f32[5,32,512]{2,1,0:T(8,128)S(1)}, u32[]{:S(2)}, u32[]{:S(2)}) %collective-permute-start.5) | collective-permute-done | bytes 327712 | tf_op jit(solution)/shard_map/ppermute | solution.py:508
  58.2 1.0 collective-permute-done.6.refs_3_
  59.1 2.3 %collective-permute-done.11.refs_6_ = f32[5,32,512]{2,1,0:T(8,128)S(1)} collective-permute-done((f32[5,32,512]{2,1,0:T(8,128)S(1)}, f32[5,32,512]{2,1,0:T(8,128)S(1)}, u32[]{:S(2)}, u32[]{:S(2)}) %collective-permute-start.11) | collective-permute-done | bytes 327712 | tf_op jit(solution)/shard_map/ppermute | solution.py:509
  61.4 3.7 %collective-permute-done.12.refs_7_ = f32[5,32,512]{2,1,0:T(8,128)S(1)} collective-permute-done((f32[5,32,512]{2,1,0:T(8,128)S(1)}, f32[5,32,512]{2,1,0:T(8,128)S(1)}, u32[]{:S(2)}, u32[]{:S(2)}) %collective-permute-start.12) | collective-permute-done | bytes 327712 | tf_op jit(solution)/shard_map/ppermute | solution.py:509
  65.1 0.9 add_again.1
  66.0 4.0 %collective-permute-start.13 = (f32[2,5,16,512]{3,2,1,0:T(8,128)S(1)}, f32[2,5,16,512]{3,2,1,0:T(8,128)S(1)}, u32[]{:S(2)}, u32[]{:S(2)}) collective-permute-start(f32[2,5,16,512]{3,2,1,0:T(8,128)S(1)} %get-tuple-element.54), channel_id=1, source_target_pairs={{0,64},{4,68},{8,72},{12,76},{16,80},{20,84},{24,88},{28,92},{32,9... | collective-permute-start | bytes 983048 | tf_op jit(solution)/shard_map/ppermute | solution.py:513
  70.2 1.3 pad_add_fusion.1.occ
  71.4 6.4 %collective-permute-done.13.recv = f32[2,5,16,512]{3,2,1,0:T(8,128)S(1)} collective-permute-done((f32[2,5,16,512]{3,2,1,0:T(8,128)S(1)}, f32[2,5,16,512]{3,2,1,0:T(8,128)S(1)}, u32[]{:S(2)}, u32[]{:S(2)}) %collective-permute-start.13) | collective-permute-done | bytes 327712 | tf_op jit(solution)/shard_map/ppermute | solution.py:513
  77.8 2.4 %pack.1 = f32[32,136,128]{2,1,0:T(8,128)} custom-call(s32[2,32]{1,0:T(2,128)S(1)} %fusion.1.index_ref, f32[2,5,16,512]{3,2,1,0:T(8,128)S(1)} %get-tuple-element.53.keep, f32[2,5,16,512]{3,2,1,0:T(8,128)S(1)} %collective-permute-done.13.recv), custom_call_target="tpu_custom_call" | custom-call | flops 300000 | bytes 3000000 | tf_op jit(solution)/shard_map/pack/pallas_call | solution.py:197
  80.2 7.5 %all-to-all-start = ((f32[32,136,128]{2,1,0:T(8,128)}), f32[32,136,128]{2,1,0:T(8,128)S(1)}, u32[]{:S(2)}, u32[]{:S(2)}) async-start(f32[32,136,128]{2,1,0:T(8,128)} %pack.1), calls=%async_computation | async-start | bytes 4456448 | tf_op jit(solution)/shard_map/all_to_all | solution.py:514
  87.7 3.1 %slice.37 = f32[1,1,1,2,512,512]{5,4,3,2,1,0:T(8,128)} slice(f32[1,1,2,2,512,512]{5,4,3,2,1,0:T(8,128)} %old_ref.1), slice={[0:1], [0:1], [1:2], [0:2], [0:512], [0:512]} | slice | bytes 4194304 | tf_op jit(solution)/shard_map/slice | solution.py:490
  90.8 26.4 %all-to-all-done.own_g.g_ref = f32[32,136,128]{2,1,0:T(8,128)S(1)} async-done(((f32[32,136,128]{2,1,0:T(8,128)}), f32[32,136,128]{2,1,0:T(8,128)S(1)}, u32[]{:S(2)}, u32[]{:S(2)}) %all-to-all-start) | async-done | bytes 2228256 | tf_op jit(solution)/shard_map/all_to_all | solution.py:514
  117.2 0.1 slice.45
  117.5 1.2 collective-permute-start.16
  118.6 1.0 collective-permute-start.15
  119.7 0.9 collective-permute-done.16.s3
  120.6 1.7 collective-permute-done.15.s2
  122.3 15.1 %tasks.1 = (bf16[32,1,16,512]{3,2,1,0:T(8,128)(2,1)S(1)}, bf16[32,1,16,512]{3,2,1,0:T(8,128)(2,1)S(1)}) custom-call(s32[2]{0:T(128)S(1)} %pad_add_fusion.1.occ, f32[8,128]{1,0:T(8,128)S(1)} %slice_reduce_fusion.s0, f32[8,128]{1,0:T(8,128)S(1)} %collective-permute-done.14.s1, f32[8,128]{1,0:T(8,128)S(1)} %collective-permute-done.15.s2, ...), custom_call_target="tpu_custom_call" | custom-call | flops 16000000000 | bytes 3500000 | tf_op jit(solution)/shard_map/tasks/pallas_call | solution.py:330
  137.5 1.9 collective-permute-done.19
  139.5 23.8 %all_to_all.10.recv_ref = bf16[32,2,16,512]{3,2,1,0:T(8,128)(2,1)S(1)} all-to-all(bf16[32,2,16,512]{3,2,1,0:T(8,128)(2,1)S(1)} %pad_maximum_fusion), channel_id=1, replica_groups=mesh['dp'=32,'mp'=4] {'dp'}, dimensions={0} | all-to-all | bytes 2097152 | tf_op jit(solution)/shard_map/all_to_all | solution.py:521
  163.3 0.6 pick.1
  163.8 0.6 collective-permute-start.20
  164.4 6.3 %collective-permute-done.20 = bf16[10,16,512]{2,1,0:T(8,128)(2,1)S(1)} collective-permute-done((bf16[10,16,512]{2,1,0:T(8,128)(2,1)S(1)}, bf16[10,16,512]{2,1,0:T(8,128)(2,1)S(1)}, u32[]{:S(2)}, u32[]{:S(2)}) %collective-permute-start.20) | collective-permute-done | bytes 163872 | tf_op jit(solution)/shard_map/ppermute | solution.py:468
  170.8 1.3 collective-permute-start.23
  172.1 0.8 collective-permute-start.22
  172.9 0.2 collective-permute-start.21
  173.1 2.3 %collective-permute-start.29 = (bf16[2,5,16,512]{3,2,1,0:T(8,128)(2,1)S(1)}, bf16[2,5,16,512]{3,2,1,0:T(8,128)(2,1)S(1)}, u32[]{:S(2)}, u32[]{:S(2)}) collective-permute-start(bf16[2,5,16,512]{3,2,1,0:T(8,128)(2,1)S(1)} %get-tuple-element.58), channel_id=1, source_target_pairs={{0,8},{4,12},{8,0},{12,4},{16,24},{20,28},{24,16},{28,20},{32,40},... | collective-permute-start | bytes 491528 | tf_op jit(solution)/shard_map/ppermute | solution.py:468
  175.4 1.3 collective-permute-start.28
  176.7 2.2 %collective-permute-start.30 = (bf16[2,5,16,512]{3,2,1,0:T(8,128)(2,1)S(1)}, bf16[2,5,16,512]{3,2,1,0:T(8,128)(2,1)S(1)}, u32[]{:S(2)}, u32[]{:S(2)}) collective-permute-start(bf16[2,5,16,512]{3,2,1,0:T(8,128)(2,1)S(1)} %get-tuple-element.58), channel_id=1, source_target_pairs={{0,12},{4,0},{8,4},{12,8},{16,28},{20,16},{24,20},{28,24},{32,44},... | collective-permute-start | bytes 491528 | tf_op jit(solution)/shard_map/ppermute | solution.py:468
  179.0 1.7 collective-permute-done.21
  180.7 2.1 collective-permute-start.26
  182.8 0.9 collective-permute-done.30
  183.8 3.6 %collective-permute-start.33 = (bf16[4,2,5,16,512]{4,3,2,1,0:T(8,128)(2,1)S(1)}, bf16[4,2,5,16,512]{4,3,2,1,0:T(8,128)(2,1)S(1)}, u32[]{:S(2)}, u32[]{:S(2)}) collective-permute-start(bf16[4,2,5,16,512]{4,3,2,1,0:T(8,128)(2,1)S(1)} %pad_maximum_fusion.2.refs_3_), channel_id=1, source_target_pairs={{0,48},{4,52},{8,56},{12,60},{16,0},{20,4},{24,8},{28,12},{32,16},... | collective-permute-start | bytes 1966088 | tf_op jit(solution)/shard_map/ppermute | solution.py:462
  187.4 8.3 %collective-permute-done.26.refs_2_ = bf16[4,2,5,16,512]{4,3,2,1,0:T(8,128)(2,1)S(1)} collective-permute-done((bf16[4,2,5,16,512]{4,3,2,1,0:T(8,128)(2,1)S(1)}, bf16[4,2,5,16,512]{4,3,2,1,0:T(8,128)(2,1)S(1)}, u32[]{:S(2)}, u32[]{:S(2)}) %collective-permute-start.26) | collective-permute-done | bytes 655392 | tf_op jit(solution)/shard_map/ppermute | solution.py:462
  195.8 1.9 collective-permute-start.27
  197.7 0.2 collective-permute-start.25
  198.0 3.2 %collective-permute-start.34 = (bf16[2,2,5,16,512]{4,3,2,1,0:T(8,128)(2,1)S(1)}, bf16[2,2,5,16,512]{4,3,2,1,0:T(8,128)(2,1)S(1)}, u32[]{:S(2)}, u32[]{:S(2)}) collective-permute-start(bf16[2,2,5,16,512]{4,3,2,1,0:T(8,128)(2,1)S(1)} %slice.51), channel_id=1, source_target_pairs={{0,48},{4,52},{8,56},{12,60},{16,0},{20,4},{24,8},{28,12},{32,16},... | collective-permute-start | bytes 983048 | tf_op jit(solution)/shard_map/ppermute | solution.py:463
  201.3 4.8 %state.1 = f32[1,1,2,2,512,512]{5,4,3,2,1,0:T(8,128)} custom-call(s32[2]{0:T(128)S(1)} %fusion.3.occ, f32[8,128]{1,0:T(8,128)S(1)} %slice_reduce_fusion.s0, f32[8,128]{1,0:T(8,128)S(1)} %collective-permute-done.14.s1, f32[8,128]{1,0:T(8,128)S(1)} %collective-permute-done.15.s2, f32[8,128]{1,0:T(8,128)S(1)} %collective-permute-done.16.s3, ...), custom_call_target="tpu_custom_call" | custom-call | flops 3000000000 | bytes 10000000 | tf_op jit(solution)/shard_map/state/pallas_call | solution.py:375
  206.1 2.9 %place.1.refs_4_ = bf16[10,512,512]{2,1,0:T(8,128)(2,1)} custom-call(s32[3]{0:T(128)S(1)} %pad_add_fusion.place, bf16[4,2,5,16,512]{4,3,2,1,0:T(8,128)(2,1)S(1)} %pad_maximum_fusion.1.refs_0_, bf16[4,2,5,16,512]{4,3,2,1,0:T(8,128)(2,1)S(1)} %collective-permute-done.24.refs_1_, bf16[4,2,5,16,512]{4,3,2,1,0:T(8,128)(2,1)S(1)} %collective-permute-done.26.refs_2_, ...), custom_call_target="tpu_custom_call" | custom-call | bytes 8000000 | tf_op jit(solution)/shard_map/place/pallas_call | solution.py:434
  209.0 0.6 collective-permute-done.32.refs_2_
  209.6 1.7 place_last.1
  (48 shorter events, 1.2 us)
Async XLA Ops:
  0.6 27.3 %copy-start.1 = (s32[1,10]{1,0:T(1,128)S(1)}, s32[1,10]{1,0:T(1,128)}, u32[]{:S(2)}) copy-start(s32[1,10]{1,0:T(1,128)} %param.5) | copy-start | bytes 124
  5.1 0.9 copy-start.2
  6.0 17.8 %collective-permute-start.1 = (bf16[5,4,32,512]{3,2,1,0:T(8,128)(2,1)}, bf16[5,4,32,512]{3,2,1,0:T(8,128)(2,1)S(1)}, u32[]{:S(2)}, u32[]{:S(2)}) collective-permute-start(bf16[5,4,32,512]{3,2,1,0:T(8,128)(2,1)} %get-tuple-element.39), channel_id=1, source_target_pairs={{0,4},{4,8},{8,12},{12,0},{16,20},{20,24},{24,28},{28,16},{32,36},... | collective-permute-start | bytes 1966088 | tf_op jit(solution)/shard_map/ppermute | solution.py:498
  7.5 20.5 %collective-permute-start.2 = (bf16[5,4,32,512]{3,2,1,0:T(8,128)(2,1)}, bf16[5,4,32,512]{3,2,1,0:T(8,128)(2,1)S(1)}, u32[]{:S(2)}, u32[]{:S(2)}) collective-permute-start(bf16[5,4,32,512]{3,2,1,0:T(8,128)(2,1)} %get-tuple-element.40), channel_id=1, source_target_pairs={{0,8},{4,12},{8,0},{12,4},{16,24},{20,28},{24,16},{28,20},{32,40},... | collective-permute-start | bytes 1966088 | tf_op jit(solution)/shard_map/ppermute | solution.py:498
  8.5 30.1 %collective-permute-start.3 = (bf16[5,4,32,512]{3,2,1,0:T(8,128)(2,1)}, bf16[5,4,32,512]{3,2,1,0:T(8,128)(2,1)S(1)}, u32[]{:S(2)}, u32[]{:S(2)}) collective-permute-start(bf16[5,4,32,512]{3,2,1,0:T(8,128)(2,1)} %get-tuple-element.41), channel_id=1, source_target_pairs={{0,12},{4,0},{8,4},{12,8},{16,28},{20,16},{24,20},{28,24},{32,44},... | collective-permute-start | bytes 1966088 | tf_op jit(solution)/shard_map/ppermute | solution.py:498
  10.7 35.0 %collective-permute-start.7 = (bf16[5,4,32,512]{3,2,1,0:T(8,128)(2,1)}, bf16[5,4,32,512]{3,2,1,0:T(8,128)(2,1)S(1)}, u32[]{:S(2)}, u32[]{:S(2)}) collective-permute-start(bf16[5,4,32,512]{3,2,1,0:T(8,128)(2,1)} %get-tuple-element.46), channel_id=1, source_target_pairs={{0,16},{4,20},{8,24},{12,28},{16,32},{20,36},{24,40},{28,44},{32,4... | collective-permute-start | bytes 1966088 | tf_op jit(solution)/shard_map/ppermute | solution.py:499
  12.3 34.8 %collective-permute-start.8 = (bf16[5,4,32,512]{3,2,1,0:T(8,128)(2,1)}, bf16[5,4,32,512]{3,2,1,0:T(8,128)(2,1)S(1)}, u32[]{:S(2)}, u32[]{:S(2)}) collective-permute-start(bf16[5,4,32,512]{3,2,1,0:T(8,128)(2,1)} %get-tuple-element.47), channel_id=1, source_target_pairs={{0,32},{4,36},{8,40},{12,44},{16,48},{20,52},{24,56},{28,60},{32,0... | collective-permute-start | bytes 1966088 | tf_op jit(solution)/shard_map/ppermute | solution.py:499
  23.8 23.3 %collective-permute-start.9 = (bf16[5,4,32,512]{3,2,1,0:T(8,128)(2,1)}, bf16[5,4,32,512]{3,2,1,0:T(8,128)(2,1)S(1)}, u32[]{:S(2)}, u32[]{:S(2)}) collective-permute-start(bf16[5,4,32,512]{3,2,1,0:T(8,128)(2,1)} %copy-done.2), channel_id=1, source_target_pairs={{0,48},{4,52},{8,56},{12,60},{16,0},{20,4},{24,8},{28,12},{32,16},... | collective-permute-start | bytes 1966088 | tf_op jit(solution)/shard_map/ppermute | solution.py:499
  39.5 11.4 %collective-permute-start.4 = (f32[5,32,512]{2,1,0:T(8,128)S(1)}, f32[5,32,512]{2,1,0:T(8,128)S(1)}, u32[]{:S(2)}, u32[]{:S(2)}) collective-permute-start(f32[5,32,512]{2,1,0:T(8,128)S(1)} %get-tuple-element.43), channel_id=1, source_target_pairs={{0,16},{4,20},{8,24},{12,28},{16,32},{20,36},{24,40},{28,44},{32,4... | collective-permute-start | bytes 983048 | tf_op jit(solution)/shard_map/ppermute | solution.py:508
  42.8 15.4 %collective-permute-start.5 = (f32[5,32,512]{2,1,0:T(8,128)S(1)}, f32[5,32,512]{2,1,0:T(8,128)S(1)}, u32[]{:S(2)}, u32[]{:S(2)}) collective-permute-start(f32[5,32,512]{2,1,0:T(8,128)S(1)} %get-tuple-element.44), channel_id=1, source_target_pairs={{0,32},{4,36},{8,40},{12,44},{16,48},{20,52},{24,56},{28,60},{32,0... | collective-permute-start | bytes 983048 | tf_op jit(solution)/shard_map/ppermute | solution.py:508
  45.7 13.4 %collective-permute-start.6 = (f32[5,32,512]{2,1,0:T(8,128)S(1)}, f32[5,32,512]{2,1,0:T(8,128)S(1)}, u32[]{:S(2)}, u32[]{:S(2)}) collective-permute-start(f32[5,32,512]{2,1,0:T(8,128)S(1)} %get-tuple-element.45), channel_id=1, source_target_pairs={{0,48},{4,52},{8,56},{12,60},{16,0},{20,4},{24,8},{28,12},{32,16},... | collective-permute-start | bytes 983048 | tf_op jit(solution)/shard_map/ppermute | solution.py:508
  48.0 11.2 %collective-permute-start.10 = (f32[5,32,512]{2,1,0:T(8,128)S(1)}, f32[5,32,512]{2,1,0:T(8,128)S(1)}, u32[]{:S(2)}, u32[]{:S(2)}) collective-permute-start(f32[5,32,512]{2,1,0:T(8,128)S(1)} %get-tuple-element.50), channel_id=1, source_target_pairs={{0,4},{4,8},{8,12},{12,0},{16,20},{20,24},{24,28},{28,16},{32,36},... | collective-permute-start | bytes 983048 | tf_op jit(solution)/shard_map/ppermute | solution.py:509
  49.3 12.1 %collective-permute-start.11 = (f32[5,32,512]{2,1,0:T(8,128)S(1)}, f32[5,32,512]{2,1,0:T(8,128)S(1)}, u32[]{:S(2)}, u32[]{:S(2)}) collective-permute-start(f32[5,32,512]{2,1,0:T(8,128)S(1)} %get-tuple-element.51), channel_id=1, source_target_pairs={{0,8},{4,12},{8,0},{12,4},{16,24},{20,28},{24,16},{28,20},{32,40},... | collective-permute-start | bytes 983048 | tf_op jit(solution)/shard_map/ppermute | solution.py:509
  50.8 14.3 %collective-permute-start.12 = (f32[5,32,512]{2,1,0:T(8,128)S(1)}, f32[5,32,512]{2,1,0:T(8,128)S(1)}, u32[]{:S(2)}, u32[]{:S(2)}) collective-permute-start(f32[5,32,512]{2,1,0:T(8,128)S(1)} %get-tuple-element.52), channel_id=1, source_target_pairs={{0,12},{4,0},{8,4},{12,8},{16,28},{20,16},{24,20},{28,24},{32,44},... | collective-permute-start | bytes 983048 | tf_op jit(solution)/shard_map/ppermute | solution.py:509
  58.1 12.0 %collective-permute-start = (s32[1]{0:T(128)}, s32[1]{0:T(128)}, u32[]{:S(2)}, u32[]{:S(2)}) collective-permute-start(s32[1]{0:T(128)} %get-tuple-element.60), channel_id=1, source_target_pairs={{0,1},{1,0},{2,3},{3,2},{4,5},{5,4},{6,7},{7,6},{8,9},{9,8},{10,11... | collective-permute-start | bytes 20 | tf_op jit(solution)/shard_map/ppermute | solution.py:489
  66.0 11.8 %collective-permute-start.13 = (f32[2,5,16,512]{3,2,1,0:T(8,128)S(1)}, f32[2,5,16,512]{3,2,1,0:T(8,128)S(1)}, u32[]{:S(2)}, u32[]{:S(2)}) collective-permute-start(f32[2,5,16,512]{3,2,1,0:T(8,128)S(1)} %get-tuple-element.54), channel_id=1, source_target_pairs={{0,64},{4,68},{8,72},{12,76},{16,80},{20,84},{24,88},{28,92},{32,9... | collective-permute-start | bytes 983048 | tf_op jit(solution)/shard_map/ppermute | solution.py:513
  80.2 37.0 %all-to-all-start = ((f32[32,136,128]{2,1,0:T(8,128)}), f32[32,136,128]{2,1,0:T(8,128)S(1)}, u32[]{:S(2)}, u32[]{:S(2)}) async-start(f32[32,136,128]{2,1,0:T(8,128)} %pack.1), calls=%async_computation | async-start | bytes 4456448 | tf_op jit(solution)/shard_map/all_to_all | solution.py:514
  90.8 28.8 %collective-permute-start.18 = (f32[1,1,1,2,512,512]{5,4,3,2,1,0:T(8,128)}, f32[1,1,1,2,512,512]{5,4,3,2,1,0:T(8,128)}, u32[]{:S(2)}, u32[]{:S(2)}) collective-permute-start(f32[1,1,1,2,512,512]{5,4,3,2,1,0:T(8,128)} %slice.37), channel_id=1, source_target_pairs={{0,1},{1,0},{2,3},{3,2},{4,5},{5,4},{6,7},{7,6},{8,9},{9,8},{10,11... | collective-permute-start | bytes 6291464 | tf_op jit(solution)/shard_map/ppermute | solution.py:490
  117.3 4.9 %collective-permute-start.17 = (f32[32,64,128]{2,1,0:T(8,128)S(1)}, f32[32,64,128]{2,1,0:T(8,128)S(1)}, u32[]{:S(2)}, u32[]{:S(2)}) collective-permute-start(f32[32,64,128]{2,1,0:T(8,128)S(1)} %slice.45), channel_id=1, source_target_pairs={{0,1},{1,0},{2,3},{3,2},{4,5},{5,4},{6,7},{7,6},{8,9},{9,8},{10,11... | collective-permute-start | bytes 3145736 | tf_op jit(solution)/shard_map/ppermute | solution.py:515
  117.5 3.1 %collective-permute-start.16 = (f32[8,128]{1,0:T(8,128)S(1)}, f32[8,128]{1,0:T(8,128)S(1)}, u32[]{:S(2)}, u32[]{:S(2)}) collective-permute-start(f32[8,128]{1,0:T(8,128)S(1)} %slice_reduce_fusion.s0), channel_id=1, source_target_pairs={{0,3},{1,2},{2,1},{3,0},{4,7},{5,6},{6,5},{7,4},{8,11},{9,10},{10,... | collective-permute-start | bytes 12296 | tf_op jit(solution)/shard_map/ppermute | solution.py:517
  118.6 3.6 %collective-permute-start.15 = (f32[8,128]{1,0:T(8,128)S(1)}, f32[8,128]{1,0:T(8,128)S(1)}, u32[]{:S(2)}, u32[]{:S(2)}) collective-permute-start(f32[8,128]{1,0:T(8,128)S(1)} %slice_reduce_fusion.s0), channel_id=1, source_target_pairs={{0,2},{1,3},{2,0},{3,1},{4,6},{5,7},{6,4},{7,5},{8,10},{9,11},{10,... | collective-permute-start | bytes 12296 | tf_op jit(solution)/shard_map/ppermute | solution.py:517
  119.7 2.6 %collective-permute-start.14 = (f32[8,128]{1,0:T(8,128)S(1)}, f32[8,128]{1,0:T(8,128)S(1)}, u32[]{:S(2)}, u32[]{:S(2)}) collective-permute-start(f32[8,128]{1,0:T(8,128)S(1)} %slice_reduce_fusion.s0), channel_id=1, source_target_pairs={{0,1},{1,0},{2,3},{3,2},{4,5},{5,4},{6,7},{7,6},{8,9},{9,8},{10,11... | collective-permute-start | bytes 12296 | tf_op jit(solution)/shard_map/ppermute | solution.py:517
  137.4 2.0 collective-permute-start.19
  139.5 61.8 %copy-start = (f32[1,1,2,2,512,512]{5,4,3,2,1,0:T(8,128)S(1)}, f32[1,1,2,2,512,512]{5,4,3,2,1,0:T(8,128)}, u32[]{:S(2)}) copy-start(f32[1,1,2,2,512,512]{5,4,3,2,1,0:T(8,128)} %old_ref.1) | copy-start | bytes 12582916
  163.8 6.9 %collective-permute-start.20 = (bf16[10,16,512]{2,1,0:T(8,128)(2,1)S(1)}, bf16[10,16,512]{2,1,0:T(8,128)(2,1)S(1)}, u32[]{:S(2)}, u32[]{:S(2)}) collective-permute-start(bf16[10,16,512]{2,1,0:T(8,128)(2,1)S(1)} %pick.1), channel_id=1, source_target_pairs={{0,64},{4,68},{8,72},{12,76},{16,80},{20,84},{24,88},{28,92},{32,9... | collective-permute-start | bytes 491528 | tf_op jit(solution)/shard_map/ppermute | solution.py:468
  170.8 5.9 %collective-permute-start.23 = (bf16[2,5,16,512]{3,2,1,0:T(8,128)(2,1)S(1)}, bf16[2,5,16,512]{3,2,1,0:T(8,128)(2,1)S(1)}, u32[]{:S(2)}, u32[]{:S(2)}) collective-permute-start(bf16[2,5,16,512]{3,2,1,0:T(8,128)(2,1)S(1)} %get-tuple-element.59), channel_id=1, source_target_pairs={{0,48},{4,52},{8,56},{12,60},{16,0},{20,4},{24,8},{28,12},{32,16},... | collective-permute-start | bytes 491528 | tf_op jit(solution)/shard_map/ppermute | solution.py:468
  172.1 6.9 %collective-permute-start.22 = (bf16[2,5,16,512]{3,2,1,0:T(8,128)(2,1)S(1)}, bf16[2,5,16,512]{3,2,1,0:T(8,128)(2,1)S(1)}, u32[]{:S(2)}, u32[]{:S(2)}) collective-permute-start(bf16[2,5,16,512]{3,2,1,0:T(8,128)(2,1)S(1)} %get-tuple-element.59), channel_id=1, source_target_pairs={{0,32},{4,36},{8,40},{12,44},{16,48},{20,52},{24,56},{28,60},{32,0... | collective-permute-start | bytes 491528 | tf_op jit(solution)/shard_map/ppermute | solution.py:468
  172.9 7.7 %collective-permute-start.21 = (bf16[2,5,16,512]{3,2,1,0:T(8,128)(2,1)S(1)}, bf16[2,5,16,512]{3,2,1,0:T(8,128)(2,1)S(1)}, u32[]{:S(2)}, u32[]{:S(2)}) collective-permute-start(bf16[2,5,16,512]{3,2,1,0:T(8,128)(2,1)S(1)} %get-tuple-element.59), channel_id=1, source_target_pairs={{0,16},{4,20},{8,24},{12,28},{16,32},{20,36},{24,40},{28,44},{32,4... | collective-permute-start | bytes 491528 | tf_op jit(solution)/shard_map/ppermute | solution.py:468
  173.1 9.7 %collective-permute-start.29 = (bf16[2,5,16,512]{3,2,1,0:T(8,128)(2,1)S(1)}, bf16[2,5,16,512]{3,2,1,0:T(8,128)(2,1)S(1)}, u32[]{:S(2)}, u32[]{:S(2)}) collective-permute-start(bf16[2,5,16,512]{3,2,1,0:T(8,128)(2,1)S(1)} %get-tuple-element.58), channel_id=1, source_target_pairs={{0,8},{4,12},{8,0},{12,4},{16,24},{20,28},{24,16},{28,20},{32,40},... | collective-permute-start | bytes 491528 | tf_op jit(solution)/shard_map/ppermute | solution.py:468
  175.4 7.4 %collective-permute-start.28 = (bf16[2,5,16,512]{3,2,1,0:T(8,128)(2,1)S(1)}, bf16[2,5,16,512]{3,2,1,0:T(8,128)(2,1)S(1)}, u32[]{:S(2)}, u32[]{:S(2)}) collective-permute-start(bf16[2,5,16,512]{3,2,1,0:T(8,128)(2,1)S(1)} %get-tuple-element.58), channel_id=1, source_target_pairs={{0,4},{4,8},{8,12},{12,0},{16,20},{20,24},{24,28},{28,16},{32,36},... | collective-permute-start | bytes 491528 | tf_op jit(solution)/shard_map/ppermute | solution.py:468
  176.7 7.1 %collective-permute-start.30 = (bf16[2,5,16,512]{3,2,1,0:T(8,128)(2,1)S(1)}, bf16[2,5,16,512]{3,2,1,0:T(8,128)(2,1)S(1)}, u32[]{:S(2)}, u32[]{:S(2)}) collective-permute-start(bf16[2,5,16,512]{3,2,1,0:T(8,128)(2,1)S(1)} %get-tuple-element.58), channel_id=1, source_target_pairs={{0,12},{4,0},{8,4},{12,8},{16,28},{20,16},{24,20},{28,24},{32,44},... | collective-permute-start | bytes 491528 | tf_op jit(solution)/shard_map/ppermute | solution.py:468
  180.7 15.0 %collective-permute-start.26 = (bf16[4,2,5,16,512]{4,3,2,1,0:T(8,128)(2,1)S(1)}, bf16[4,2,5,16,512]{4,3,2,1,0:T(8,128)(2,1)S(1)}, u32[]{:S(2)}, u32[]{:S(2)}) collective-permute-start(bf16[4,2,5,16,512]{4,3,2,1,0:T(8,128)(2,1)S(1)} %pad_maximum_fusion.1.refs_0_), channel_id=1, source_target_pairs={{0,12},{4,0},{8,4},{12,8},{16,28},{20,16},{24,20},{28,24},{32,44},... | collective-permute-start | bytes 1966088 | tf_op jit(solution)/shard_map/ppermute | solution.py:462
  182.8 14.9 %collective-permute-start.24 = (bf16[4,2,5,16,512]{4,3,2,1,0:T(8,128)(2,1)S(1)}, bf16[4,2,5,16,512]{4,3,2,1,0:T(8,128)(2,1)S(1)}, u32[]{:S(2)}, u32[]{:S(2)}) collective-permute-start(bf16[4,2,5,16,512]{4,3,2,1,0:T(8,128)(2,1)S(1)} %pad_maximum_fusion.1.refs_0_), channel_id=1, source_target_pairs={{0,4},{4,8},{8,12},{12,0},{16,20},{20,24},{24,28},{28,16},{32,36},... | collective-permute-start | bytes 1966088 | tf_op jit(solution)/shard_map/ppermute | solution.py:461
  183.8 14.2 %collective-permute-start.33 = (bf16[4,2,5,16,512]{4,3,2,1,0:T(8,128)(2,1)S(1)}, bf16[4,2,5,16,512]{4,3,2,1,0:T(8,128)(2,1)S(1)}, u32[]{:S(2)}, u32[]{:S(2)}) collective-permute-start(bf16[4,2,5,16,512]{4,3,2,1,0:T(8,128)(2,1)S(1)} %pad_maximum_fusion.2.refs_3_), channel_id=1, source_target_pairs={{0,48},{4,52},{8,56},{12,60},{16,0},{20,4},{24,8},{28,12},{32,16},... | collective-permute-start | bytes 1966088 | tf_op jit(solution)/shard_map/ppermute | solution.py:462
  187.4 13.7 %collective-permute-start.31 = (bf16[4,2,5,16,512]{4,3,2,1,0:T(8,128)(2,1)S(1)}, bf16[4,2,5,16,512]{4,3,2,1,0:T(8,128)(2,1)S(1)}, u32[]{:S(2)}, u32[]{:S(2)}) collective-permute-start(bf16[4,2,5,16,512]{4,3,2,1,0:T(8,128)(2,1)S(1)} %pad_maximum_fusion.2.refs_3_), channel_id=1, source_target_pairs={{0,16},{4,20},{8,24},{12,28},{16,32},{20,36},{24,40},{28,44},{32,4... | collective-permute-start | bytes 1966088 | tf_op jit(solution)/shard_map/ppermute | solution.py:461
  195.8 13.2 %collective-permute-start.27 = (bf16[2,2,5,16,512]{4,3,2,1,0:T(8,128)(2,1)S(1)}, bf16[2,2,5,16,512]{4,3,2,1,0:T(8,128)(2,1)S(1)}, u32[]{:S(2)}, u32[]{:S(2)}) collective-permute-start(bf16[2,2,5,16,512]{4,3,2,1,0:T(8,128)(2,1)S(1)} %slice.49), channel_id=1, source_target_pairs={{0,12},{4,0},{8,4},{12,8},{16,28},{20,16},{24,20},{28,24},{32,44},... | collective-permute-start | bytes 983048 | tf_op jit(solution)/shard_map/ppermute | solution.py:463
  197.7 11.2 %collective-permute-start.25 = (bf16[2,2,5,16,512]{4,3,2,1,0:T(8,128)(2,1)S(1)}, bf16[2,2,5,16,512]{4,3,2,1,0:T(8,128)(2,1)S(1)}, u32[]{:S(2)}, u32[]{:S(2)}) collective-permute-start(bf16[2,2,5,16,512]{4,3,2,1,0:T(8,128)(2,1)S(1)} %slice.48), channel_id=1, source_target_pairs={{0,4},{4,8},{8,12},{12,0},{16,20},{20,24},{24,28},{28,16},{32,36},... | collective-permute-start | bytes 983048 | tf_op jit(solution)/shard_map/ppermute | solution.py:463
  198.0 11.0 %collective-permute-start.34 = (bf16[2,2,5,16,512]{4,3,2,1,0:T(8,128)(2,1)S(1)}, bf16[2,2,5,16,512]{4,3,2,1,0:T(8,128)(2,1)S(1)}, u32[]{:S(2)}, u32[]{:S(2)}) collective-permute-start(bf16[2,2,5,16,512]{4,3,2,1,0:T(8,128)(2,1)S(1)} %slice.51), channel_id=1, source_target_pairs={{0,48},{4,52},{8,56},{12,60},{16,0},{20,4},{24,8},{28,12},{32,16},... | collective-permute-start | bytes 983048 | tf_op jit(solution)/shard_map/ppermute | solution.py:463
  201.2 8.4 %collective-permute-start.32 = (bf16[2,2,5,16,512]{4,3,2,1,0:T(8,128)(2,1)S(1)}, bf16[2,2,5,16,512]{4,3,2,1,0:T(8,128)(2,1)S(1)}, u32[]{:S(2)}, u32[]{:S(2)}) collective-permute-start(bf16[2,2,5,16,512]{4,3,2,1,0:T(8,128)(2,1)S(1)} %slice.50), channel_id=1, source_target_pairs={{0,16},{4,20},{8,24},{12,28},{16,32},{20,36},{24,40},{28,44},{32,4... | collective-permute-start | bytes 983048 | tf_op jit(solution)/shard_map/ppermute | solution.py:463

commit v3 on v2

--- a/solution.py
+++ b/solution.py
@@ -101,16 +101,22 @@
 
 
 def cut_kernel(place, grads, *refs):
-    outs, sems = refs[:6], refs[6]
-    copies = []
-    for k in range(1, 4):
+    outs, held, ins, puts = refs[:6], refs[6], refs[7], refs[8]
+    gets = []
+    for k in (1, 3, 2):
         x = lax.rem(place[0] + k, 4)
         y = lax.rem(place[1] + k, 4)
-        copies.append(pltpu.make_async_copy(grads.at[pl.ds(0, HALF), x], outs[k - 1], sems.at[k - 1]))
-        copies.append(pltpu.make_async_copy(grads.at[pl.ds(HALF, HALF), :, y], outs[k + 2], sems.at[k + 2]))
-    for copy in copies:
+        gets.append((k - 1, grads.at[pl.ds(0, HALF), x]))
+        gets.append((k + 2, grads.at[pl.ds(HALF, HALF), :, y]))
+    copies = [(n, pltpu.make_async_copy(source, held.at[n], ins.at[n])) for n, source in gets]
+    for _, copy in copies:
         copy.start()
-    for copy in copies:
+    stores = []
+    for n, copy in copies:
+        copy.wait()
+        stores.append(pltpu.make_async_copy(held.at[n], outs[n], puts.at[n]))
+        stores[-1].start()
+    for copy in stores:
         copy.wait()
 
 
@@ -118,9 +124,13 @@
     return pl.pallas_call(
         cut_kernel,
         in_specs=[pl.BlockSpec(memory_space=pltpu.SMEM), pl.BlockSpec(memory_space=pltpu.HBM)],
-        out_specs=[pl.BlockSpec(memory_space=pltpu.VMEM)] * 6,
+        out_specs=[pl.BlockSpec(memory_space=pl.ANY)] * 6,
         out_shape=[jax.ShapeDtypeStruct((HALF, 4, ROWS, N), BF)] * 6,
-        scratch_shapes=[pltpu.SemaphoreType.DMA((6,))],
+        scratch_shapes=[
+            pltpu.VMEM((6, HALF, 4, ROWS, N), BF),
+            pltpu.SemaphoreType.DMA((6,)),
+            pltpu.SemaphoreType.DMA((6,)),
+        ],
         compiler_params=pltpu.CompilerParams(vmem_limit_bytes=SMALL),
         name="cut",
     )(place, pltpu.with_memory_space_constraint(grads, pltpu.HBM))

time: 214 us -> 213 us (level)
  no operation moved by 1% of the time
where the time goes in v3:
time: 213 us; the launch traced here: 211 us
  waiting for transfers between devices  85.3 us (40%)
  starting transfers between devices  57.5 us (27%)
  Pallas kernels  33.9 us (16%)
  blocking collectives  23.8 us (11%)
  local copies, waits for them, and re-layouts  7.13 us (3%)
  other arithmetic  2.16 us (1%)
    all_to_all x1, waiting for transfers between devices, shards(): lax.all_to_all(packed, 'dp', split_axis=0, concat_axis=0, tiled=True)  26.4 us
    all_to_all x1, blocking collectives, shards(): lax.all_to_all(outgoing, 'dp', split_axis=0, concat_axis=0, tiled=True)  23.8 us
    ppermute x3, waiting for transfers between devices, shards(): first[k] = lax.ppermute(pieces[k - 1], 'dp', dp_pairs(k, 0, 0))  19.1 us
    pallas_call x1, Pallas kernels, run_tasks(): pl.pallas_call(task_kernel, grid=(2,), in_specs=[pl.BlockSpec(memory_spac...  15.1 us
    ppermute x7, waiting for transfers between devices, spread(): lax.ppermute(v, 'dp', dp_pairs(dx * k, dy * k, dz * k))  9.01 us
    ppermute x7, starting transfers between devices, spread(): lax.ppermute(v, 'dp', dp_pairs(dx * k, dy * k, dz * k))  8.66 us
    ppermute x2, waiting for transfers between devices, around(): front = lax.ppermute(v, 'dp', behind)  8.31 us
    all_to_all x1, starting transfers between devices, shards(): lax.all_to_all(packed, 'dp', split_axis=0, concat_axis=0, tiled=True)  7.51 us
  transfers between devices with their start and end apart: 36, of which 17 were waited for; matrix products, arithmetic and copies ran while one was open for 4% of the time, Pallas kernels for 5%

profile of v3, /device:TPU:2, one launch (start us, length us, event | category | flops | bytes accessed | tf_op | source)
XLA Modules:
  0.0 210.9 jit_solution(83438520035629734)
XLA Ops:
  0.8 3.8 %cut.1 = (bf16[5,4,32,512]{3,2,1,0:T(8,128)(2,1)}, bf16[5,4,32,512]{3,2,1,0:T(8,128)(2,1)}, bf16[5,4,32,512]{3,2,1,0:T(8,128)(2,1)}, bf16[5,4,32,512]{3,2,1,0:T(...) custom-call(s32[3]{0:T(128)S(1)} %pad_add_fusion.place, ...), custom_call_target="tpu_custom_call" | custom-call | tf_op jit(solution)/shard_map/cut/pallas_call | solution.py:124
  4.5 0.8 copy-done.2
  5.4 1.5 collective-permute-start.1
  6.9 1.0 collective-permute-start.2
  7.9 2.3 %collective-permute-start.3 = (bf16[5,4,32,512]{3,2,1,0:T(8,128)(2,1)}, bf16[5,4,32,512]{3,2,1,0:T(8,128)(2,1)S(1)}, u32[]{:S(2)}, u32[]{:S(2)}) collective-permute-start(bf16[5,4,32,512]{3,2,1,0:T(8,128)(2,1)} %get-tuple-element.41), channel_id=1, source_target_pairs={{0,12},{4,0},{8,4},{12,8},{16,28},{20,16},{24,20},{28,24},{32,44},... | collective-permute-start | bytes 1966088 | tf_op jit(solution)/shard_map/ppermute | solution.py:508
  10.1 1.6 collective-permute-start.7
  11.7 2.9 %collective-permute-start.8 = (bf16[5,4,32,512]{3,2,1,0:T(8,128)(2,1)}, bf16[5,4,32,512]{3,2,1,0:T(8,128)(2,1)S(1)}, u32[]{:S(2)}, u32[]{:S(2)}) collective-permute-start(bf16[5,4,32,512]{3,2,1,0:T(8,128)(2,1)} %get-tuple-element.47), channel_id=1, source_target_pairs={{0,32},{4,36},{8,40},{12,44},{16,48},{20,52},{24,56},{28,60},{32,0... | collective-permute-start | bytes 1966088 | tf_op jit(solution)/shard_map/ppermute | solution.py:509
  14.6 8.6 %collective-permute-done.1.r1 = bf16[5,4,32,512]{3,2,1,0:T(8,128)(2,1)S(1)} collective-permute-done((bf16[5,4,32,512]{3,2,1,0:T(8,128)(2,1)}, bf16[5,4,32,512]{3,2,1,0:T(8,128)(2,1)S(1)}, u32[]{:S(2)}, u32[]{:S(2)}) %collective-permute-start.1) | collective-permute-done | bytes 655392 | tf_op jit(solution)/shard_map/ppermute | solution.py:508
  23.2 3.0 %collective-permute-start.9 = (bf16[5,4,32,512]{3,2,1,0:T(8,128)(2,1)}, bf16[5,4,32,512]{3,2,1,0:T(8,128)(2,1)S(1)}, u32[]{:S(2)}, u32[]{:S(2)}) collective-permute-start(bf16[5,4,32,512]{3,2,1,0:T(8,128)(2,1)} %copy-done.2), channel_id=1, source_target_pairs={{0,48},{4,52},{8,56},{12,60},{16,0},{20,4},{24,8},{28,12},{32,16},... | collective-permute-start | bytes 1966088 | tf_op jit(solution)/shard_map/ppermute | solution.py:509
  26.2 1.1 dynamic-slice_bitcast_fusion.1.own
  27.4 10.6 %collective-permute-done.3.r3 = bf16[5,4,32,512]{3,2,1,0:T(8,128)(2,1)S(1)} collective-permute-done((bf16[5,4,32,512]{3,2,1,0:T(8,128)(2,1)}, bf16[5,4,32,512]{3,2,1,0:T(8,128)(2,1)S(1)}, u32[]{:S(2)}, u32[]{:S(2)}) %collective-permute-start.3) | collective-permute-done | bytes 655392 | tf_op jit(solution)/shard_map/ppermute | solution.py:508
  38.0 0.9 shard_map.50
  38.9 1.8 collective-permute-start.4
  40.7 0.2 convert_reduce_fusion.slot
  40.9 0.1 fusion.3.occ
  41.0 1.1 dynamic-slice_bitcast_fusion.own
  42.2 3.0 %collective-permute-start.5 = (f32[5,32,512]{2,1,0:T(8,128)S(1)}, f32[5,32,512]{2,1,0:T(8,128)S(1)}, u32[]{:S(2)}, u32[]{:S(2)}) collective-permute-start(f32[5,32,512]{2,1,0:T(8,128)S(1)} %get-tuple-element.44), channel_id=1, source_target_pairs={{0,32},{4,36},{8,40},{12,44},{16,48},{20,52},{24,56},{28,60},{32,0... | collective-permute-start | bytes 983048 | tf_op jit(solution)/shard_map/ppermute | solution.py:518
  45.1 1.3 collective-permute-start.6
  46.5 0.9 shard_map.51
  47.4 1.4 collective-permute-start.10
  48.7 1.5 collective-permute-start.11
  50.2 2.6 %collective-permute-start.12 = (f32[5,32,512]{2,1,0:T(8,128)S(1)}, f32[5,32,512]{2,1,0:T(8,128)S(1)}, u32[]{:S(2)}, u32[]{:S(2)}) collective-permute-start(f32[5,32,512]{2,1,0:T(8,128)S(1)} %get-tuple-element.52), channel_id=1, source_target_pairs={{0,12},{4,0},{8,4},{12,8},{16,28},{20,16},{24,20},{28,24},{32,44},... | collective-permute-start | bytes 983048 | tf_op jit(solution)/shard_map/ppermute | solution.py:519
  52.8 0.6 fusion.4
  53.5 4.1 %collective-permute-done.5.refs_2_ = f32[5,32,512]{2,1,0:T(8,128)S(1)} collective-permute-done((f32[5,32,512]{2,1,0:T(8,128)S(1)}, f32[5,32,512]{2,1,0:T(8,128)S(1)}, u32[]{:S(2)}, u32[]{:S(2)}) %collective-permute-start.5) | collective-permute-done | bytes 327712 | tf_op jit(solution)/shard_map/ppermute | solution.py:518
  57.6 1.0 collective-permute-done.6.refs_3_
  58.5 2.3 %collective-permute-done.11.refs_6_ = f32[5,32,512]{2,1,0:T(8,128)S(1)} collective-permute-done((f32[5,32,512]{2,1,0:T(8,128)S(1)}, f32[5,32,512]{2,1,0:T(8,128)S(1)}, u32[]{:S(2)}, u32[]{:S(2)}) %collective-permute-start.11) | collective-permute-done | bytes 327712 | tf_op jit(solution)/shard_map/ppermute | solution.py:519
  60.8 3.7 %collective-permute-done.12.refs_7_ = f32[5,32,512]{2,1,0:T(8,128)S(1)} collective-permute-done((f32[5,32,512]{2,1,0:T(8,128)S(1)}, f32[5,32,512]{2,1,0:T(8,128)S(1)}, u32[]{:S(2)}, u32[]{:S(2)}) %collective-permute-start.12) | collective-permute-done | bytes 327712 | tf_op jit(solution)/shard_map/ppermute | solution.py:519
  64.5 0.9 add_again.1
  65.4 4.0 %collective-permute-start.13 = (f32[2,5,16,512]{3,2,1,0:T(8,128)S(1)}, f32[2,5,16,512]{3,2,1,0:T(8,128)S(1)}, u32[]{:S(2)}, u32[]{:S(2)}) collective-permute-start(f32[2,5,16,512]{3,2,1,0:T(8,128)S(1)} %get-tuple-element.54), channel_id=1, source_target_pairs={{0,64},{4,68},{8,72},{12,76},{16,80},{20,84},{24,88},{28,92},{32,9... | collective-permute-start | bytes 983048 | tf_op jit(solution)/shard_map/ppermute | solution.py:523
  69.6 1.3 pad_add_fusion.1.occ
  70.8 6.4 %collective-permute-done.13.recv = f32[2,5,16,512]{3,2,1,0:T(8,128)S(1)} collective-permute-done((f32[2,5,16,512]{3,2,1,0:T(8,128)S(1)}, f32[2,5,16,512]{3,2,1,0:T(8,128)S(1)}, u32[]{:S(2)}, u32[]{:S(2)}) %collective-permute-start.13) | collective-permute-done | bytes 327712 | tf_op jit(solution)/shard_map/ppermute | solution.py:523
  77.2 2.4 %pack.1 = f32[32,136,128]{2,1,0:T(8,128)} custom-call(s32[2,32]{1,0:T(2,128)S(1)} %fusion.1.index_ref, f32[2,5,16,512]{3,2,1,0:T(8,128)S(1)} %get-tuple-element.53.keep, f32[2,5,16,512]{3,2,1,0:T(8,128)S(1)} %collective-permute-done.13.recv), custom_call_target="tpu_custom_call" | custom-call | flops 300000 | bytes 3000000 | tf_op jit(solution)/shard_map/pack/pallas_call | solution.py:207
  79.6 7.5 %all-to-all-start = ((f32[32,136,128]{2,1,0:T(8,128)}), f32[32,136,128]{2,1,0:T(8,128)S(1)}, u32[]{:S(2)}, u32[]{:S(2)}) async-start(f32[32,136,128]{2,1,0:T(8,128)} %pack.1), calls=%async_computation | async-start | bytes 4456448 | tf_op jit(solution)/shard_map/all_to_all | solution.py:524
  87.1 3.1 %slice.37 = f32[1,1,1,2,512,512]{5,4,3,2,1,0:T(8,128)} slice(f32[1,1,2,2,512,512]{5,4,3,2,1,0:T(8,128)} %old_ref.1), slice={[0:1], [0:1], [1:2], [0:2], [0:512], [0:512]} | slice | bytes 4194304 | tf_op jit(solution)/shard_map/slice | solution.py:500
  90.2 26.4 %all-to-all-done.own_g.g_ref = f32[32,136,128]{2,1,0:T(8,128)S(1)} async-done(((f32[32,136,128]{2,1,0:T(8,128)}), f32[32,136,128]{2,1,0:T(8,128)S(1)}, u32[]{:S(2)}, u32[]{:S(2)}) %all-to-all-start) | async-done | bytes 2228256 | tf_op jit(solution)/shard_map/all_to_all | solution.py:524
  116.6 0.1 slice.45
  116.9 1.2 collective-permute-start.16
  118.0 1.0 collective-permute-start.15
  119.1 0.9 collective-permute-done.16.s3
  120.0 1.7 collective-permute-done.15.s2
  121.7 15.1 %tasks.1 = (bf16[32,1,16,512]{3,2,1,0:T(8,128)(2,1)S(1)}, bf16[32,1,16,512]{3,2,1,0:T(8,128)(2,1)S(1)}) custom-call(s32[2]{0:T(128)S(1)} %pad_add_fusion.1.occ, f32[8,128]{1,0:T(8,128)S(1)} %slice_reduce_fusion.s0, f32[8,128]{1,0:T(8,128)S(1)} %collective-permute-done.14.s1, f32[8,128]{1,0:T(8,128)S(1)} %collective-permute-done.15.s2, ...), custom_call_target="tpu_custom_call" | custom-call | flops 16000000000 | bytes 3500000 | tf_op jit(solution)/shard_map/tasks/pallas_call | solution.py:340
  136.9 1.9 collective-permute-done.19
  138.9 23.8 %all_to_all.10.recv_ref = bf16[32,2,16,512]{3,2,1,0:T(8,128)(2,1)S(1)} all-to-all(bf16[32,2,16,512]{3,2,1,0:T(8,128)(2,1)S(1)} %pad_maximum_fusion), channel_id=1, replica_groups=mesh['dp'=32,'mp'=4] {'dp'}, dimensions={0} | all-to-all | bytes 2097152 | tf_op jit(solution)/shard_map/all_to_all | solution.py:531
  162.7 0.6 pick.1
  163.2 0.6 collective-permute-start.20
  163.8 6.3 %collective-permute-done.20 = bf16[10,16,512]{2,1,0:T(8,128)(2,1)S(1)} collective-permute-done((bf16[10,16,512]{2,1,0:T(8,128)(2,1)S(1)}, bf16[10,16,512]{2,1,0:T(8,128)(2,1)S(1)}, u32[]{:S(2)}, u32[]{:S(2)}) %collective-permute-start.20) | collective-permute-done | bytes 163872 | tf_op jit(solution)/shard_map/ppermute | solution.py:478
  170.2 1.3 collective-permute-start.23
  171.5 0.8 collective-permute-start.22
  172.3 0.2 collective-permute-start.21
  172.5 2.3 %collective-permute-start.29 = (bf16[2,5,16,512]{3,2,1,0:T(8,128)(2,1)S(1)}, bf16[2,5,16,512]{3,2,1,0:T(8,128)(2,1)S(1)}, u32[]{:S(2)}, u32[]{:S(2)}) collective-permute-start(bf16[2,5,16,512]{3,2,1,0:T(8,128)(2,1)S(1)} %get-tuple-element.58), channel_id=1, source_target_pairs={{0,8},{4,12},{8,0},{12,4},{16,24},{20,28},{24,16},{28,20},{32,40},... | collective-permute-start | bytes 491528 | tf_op jit(solution)/shard_map/ppermute | solution.py:478
  174.8 1.3 collective-permute-start.28
  176.1 2.2 %collective-permute-start.30 = (bf16[2,5,16,512]{3,2,1,0:T(8,128)(2,1)S(1)}, bf16[2,5,16,512]{3,2,1,0:T(8,128)(2,1)S(1)}, u32[]{:S(2)}, u32[]{:S(2)}) collective-permute-start(bf16[2,5,16,512]{3,2,1,0:T(8,128)(2,1)S(1)} %get-tuple-element.58), channel_id=1, source_target_pairs={{0,12},{4,0},{8,4},{12,8},{16,28},{20,16},{24,20},{28,24},{32,44},... | collective-permute-start | bytes 491528 | tf_op jit(solution)/shard_map/ppermute | solution.py:478
  178.4 1.7 collective-permute-done.21
  180.1 2.1 collective-permute-start.26
  182.2 0.9 collective-permute-done.30
  183.2 3.6 %collective-permute-start.33 = (bf16[4,2,5,16,512]{4,3,2,1,0:T(8,128)(2,1)S(1)}, bf16[4,2,5,16,512]{4,3,2,1,0:T(8,128)(2,1)S(1)}, u32[]{:S(2)}, u32[]{:S(2)}) collective-permute-start(bf16[4,2,5,16,512]{4,3,2,1,0:T(8,128)(2,1)S(1)} %pad_maximum_fusion.2.refs_3_), channel_id=1, source_target_pairs={{0,48},{4,52},{8,56},{12,60},{16,0},{20,4},{24,8},{28,12},{32,16},... | collective-permute-start | bytes 1966088 | tf_op jit(solution)/shard_map/ppermute | solution.py:472
  186.9 8.3 %collective-permute-done.26.refs_2_ = bf16[4,2,5,16,512]{4,3,2,1,0:T(8,128)(2,1)S(1)} collective-permute-done((bf16[4,2,5,16,512]{4,3,2,1,0:T(8,128)(2,1)S(1)}, bf16[4,2,5,16,512]{4,3,2,1,0:T(8,128)(2,1)S(1)}, u32[]{:S(2)}, u32[]{:S(2)}) %collective-permute-start.26) | collective-permute-done | bytes 655392 | tf_op jit(solution)/shard_map/ppermute | solution.py:472
  195.2 1.9 collective-permute-start.27
  197.1 0.2 collective-permute-start.25
  197.4 3.2 %collective-permute-start.34 = (bf16[2,2,5,16,512]{4,3,2,1,0:T(8,128)(2,1)S(1)}, bf16[2,2,5,16,512]{4,3,2,1,0:T(8,128)(2,1)S(1)}, u32[]{:S(2)}, u32[]{:S(2)}) collective-permute-start(bf16[2,2,5,16,512]{4,3,2,1,0:T(8,128)(2,1)S(1)} %slice.51), channel_id=1, source_target_pairs={{0,48},{4,52},{8,56},{12,60},{16,0},{20,4},{24,8},{28,12},{32,16},... | collective-permute-start | bytes 983048 | tf_op jit(solution)/shard_map/ppermute | solution.py:473
  200.7 4.8 %state.1 = f32[1,1,2,2,512,512]{5,4,3,2,1,0:T(8,128)} custom-call(s32[2]{0:T(128)S(1)} %fusion.3.occ, f32[8,128]{1,0:T(8,128)S(1)} %slice_reduce_fusion.s0, f32[8,128]{1,0:T(8,128)S(1)} %collective-permute-done.14.s1, f32[8,128]{1,0:T(8,128)S(1)} %collective-permute-done.15.s2, f32[8,128]{1,0:T(8,128)S(1)} %collective-permute-done.16.s3, ...), custom_call_target="tpu_custom_call" | custom-call | flops 3000000000 | bytes 10000000 | tf_op jit(solution)/shard_map/state/pallas_call | solution.py:385
  205.5 2.9 %place.1.refs_4_ = bf16[10,512,512]{2,1,0:T(8,128)(2,1)} custom-call(s32[3]{0:T(128)S(1)} %pad_add_fusion.place, bf16[4,2,5,16,512]{4,3,2,1,0:T(8,128)(2,1)S(1)} %pad_maximum_fusion.1.refs_0_, bf16[4,2,5,16,512]{4,3,2,1,0:T(8,128)(2,1)S(1)} %collective-permute-done.24.refs_1_, bf16[4,2,5,16,512]{4,3,2,1,0:T(8,128)(2,1)S(1)} %collective-permute-done.26.refs_2_, ...), custom_call_target="tpu_custom_call" | custom-call | bytes 8000000 | tf_op jit(solution)/shard_map/place/pallas_call | solution.py:444
  208.4 0.6 collective-permute-done.32.refs_2_
  209.0 1.7 place_last.1
  (48 shorter events, 1.2 us)
Async XLA Ops:
  0.6 26.7 %copy-start.1 = (s32[1,10]{1,0:T(1,128)S(1)}, s32[1,10]{1,0:T(1,128)}, u32[]{:S(2)}) copy-start(s32[1,10]{1,0:T(1,128)} %param.5) | copy-start | bytes 124
  4.5 0.9 copy-start.2
  5.4 17.8 %collective-permute-start.1 = (bf16[5,4,32,512]{3,2,1,0:T(8,128)(2,1)}, bf16[5,4,32,512]{3,2,1,0:T(8,128)(2,1)S(1)}, u32[]{:S(2)}, u32[]{:S(2)}) collective-permute-start(bf16[5,4,32,512]{3,2,1,0:T(8,128)(2,1)} %get-tuple-element.39), channel_id=1, source_target_pairs={{0,4},{4,8},{8,12},{12,0},{16,20},{20,24},{24,28},{28,16},{32,36},... | collective-permute-start | bytes 1966088 | tf_op jit(solution)/shard_map/ppermute | solution.py:508
  6.9 20.5 %collective-permute-start.2 = (bf16[5,4,32,512]{3,2,1,0:T(8,128)(2,1)}, bf16[5,4,32,512]{3,2,1,0:T(8,128)(2,1)S(1)}, u32[]{:S(2)}, u32[]{:S(2)}) collective-permute-start(bf16[5,4,32,512]{3,2,1,0:T(8,128)(2,1)} %get-tuple-element.40), channel_id=1, source_target_pairs={{0,8},{4,12},{8,0},{12,4},{16,24},{20,28},{24,16},{28,20},{32,40},... | collective-permute-start | bytes 1966088 | tf_op jit(solution)/shard_map/ppermute | solution.py:508
  7.9 30.1 %collective-permute-start.3 = (bf16[5,4,32,512]{3,2,1,0:T(8,128)(2,1)}, bf16[5,4,32,512]{3,2,1,0:T(8,128)(2,1)S(1)}, u32[]{:S(2)}, u32[]{:S(2)}) collective-permute-start(bf16[5,4,32,512]{3,2,1,0:T(8,128)(2,1)} %get-tuple-element.41), channel_id=1, source_target_pairs={{0,12},{4,0},{8,4},{12,8},{16,28},{20,16},{24,20},{28,24},{32,44},... | collective-permute-start | bytes 1966088 | tf_op jit(solution)/shard_map/ppermute | solution.py:508
  10.1 35.0 %collective-permute-start.7 = (bf16[5,4,32,512]{3,2,1,0:T(8,128)(2,1)}, bf16[5,4,32,512]{3,2,1,0:T(8,128)(2,1)S(1)}, u32[]{:S(2)}, u32[]{:S(2)}) collective-permute-start(bf16[5,4,32,512]{3,2,1,0:T(8,128)(2,1)} %get-tuple-element.46), channel_id=1, source_target_pairs={{0,16},{4,20},{8,24},{12,28},{16,32},{20,36},{24,40},{28,44},{32,4... | collective-permute-start | bytes 1966088 | tf_op jit(solution)/shard_map/ppermute | solution.py:509
  11.7 34.8 %collective-permute-start.8 = (bf16[5,4,32,512]{3,2,1,0:T(8,128)(2,1)}, bf16[5,4,32,512]{3,2,1,0:T(8,128)(2,1)S(1)}, u32[]{:S(2)}, u32[]{:S(2)}) collective-permute-start(bf16[5,4,32,512]{3,2,1,0:T(8,128)(2,1)} %get-tuple-element.47), channel_id=1, source_target_pairs={{0,32},{4,36},{8,40},{12,44},{16,48},{20,52},{24,56},{28,60},{32,0... | collective-permute-start | bytes 1966088 | tf_op jit(solution)/shard_map/ppermute | solution.py:509
  23.2 23.3 %collective-permute-start.9 = (bf16[5,4,32,512]{3,2,1,0:T(8,128)(2,1)}, bf16[5,4,32,512]{3,2,1,0:T(8,128)(2,1)S(1)}, u32[]{:S(2)}, u32[]{:S(2)}) collective-permute-start(bf16[5,4,32,512]{3,2,1,0:T(8,128)(2,1)} %copy-done.2), channel_id=1, source_target_pairs={{0,48},{4,52},{8,56},{12,60},{16,0},{20,4},{24,8},{28,12},{32,16},... | collective-permute-start | bytes 1966088 | tf_op jit(solution)/shard_map/ppermute | solution.py:509
  38.9 11.4 %collective-permute-start.4 = (f32[5,32,512]{2,1,0:T(8,128)S(1)}, f32[5,32,512]{2,1,0:T(8,128)S(1)}, u32[]{:S(2)}, u32[]{:S(2)}) collective-permute-start(f32[5,32,512]{2,1,0:T(8,128)S(1)} %get-tuple-element.43), channel_id=1, source_target_pairs={{0,16},{4,20},{8,24},{12,28},{16,32},{20,36},{24,40},{28,44},{32,4... | collective-permute-start | bytes 983048 | tf_op jit(solution)/shard_map/ppermute | solution.py:518
  42.2 15.4 %collective-permute-start.5 = (f32[5,32,512]{2,1,0:T(8,128)S(1)}, f32[5,32,512]{2,1,0:T(8,128)S(1)}, u32[]{:S(2)}, u32[]{:S(2)}) collective-permute-start(f32[5,32,512]{2,1,0:T(8,128)S(1)} %get-tuple-element.44), channel_id=1, source_target_pairs={{0,32},{4,36},{8,40},{12,44},{16,48},{20,52},{24,56},{28,60},{32,0... | collective-permute-start | bytes 983048 | tf_op jit(solution)/shard_map/ppermute | solution.py:518
  45.1 13.4 %collective-permute-start.6 = (f32[5,32,512]{2,1,0:T(8,128)S(1)}, f32[5,32,512]{2,1,0:T(8,128)S(1)}, u32[]{:S(2)}, u32[]{:S(2)}) collective-permute-start(f32[5,32,512]{2,1,0:T(8,128)S(1)} %get-tuple-element.45), channel_id=1, source_target_pairs={{0,48},{4,52},{8,56},{12,60},{16,0},{20,4},{24,8},{28,12},{32,16},... | collective-permute-start | bytes 983048 | tf_op jit(solution)/shard_map/ppermute | solution.py:518
  47.4 11.2 %collective-permute-start.10 = (f32[5,32,512]{2,1,0:T(8,128)S(1)}, f32[5,32,512]{2,1,0:T(8,128)S(1)}, u32[]{:S(2)}, u32[]{:S(2)}) collective-permute-start(f32[5,32,512]{2,1,0:T(8,128)S(1)} %get-tuple-element.50), channel_id=1, source_target_pairs={{0,4},{4,8},{8,12},{12,0},{16,20},{20,24},{24,28},{28,16},{32,36},... | collective-permute-start | bytes 983048 | tf_op jit(solution)/shard_map/ppermute | solution.py:519
  48.7 12.1 %collective-permute-start.11 = (f32[5,32,512]{2,1,0:T(8,128)S(1)}, f32[5,32,512]{2,1,0:T(8,128)S(1)}, u32[]{:S(2)}, u32[]{:S(2)}) collective-permute-start(f32[5,32,512]{2,1,0:T(8,128)S(1)} %get-tuple-element.51), channel_id=1, source_target_pairs={{0,8},{4,12},{8,0},{12,4},{16,24},{20,28},{24,16},{28,20},{32,40},... | collective-permute-start | bytes 983048 | tf_op jit(solution)/shard_map/ppermute | solution.py:519
  50.2 14.3 %collective-permute-start.12 = (f32[5,32,512]{2,1,0:T(8,128)S(1)}, f32[5,32,512]{2,1,0:T(8,128)S(1)}, u32[]{:S(2)}, u32[]{:S(2)}) collective-permute-start(f32[5,32,512]{2,1,0:T(8,128)S(1)} %get-tuple-element.52), channel_id=1, source_target_pairs={{0,12},{4,0},{8,4},{12,8},{16,28},{20,16},{24,20},{28,24},{32,44},... | collective-permute-start | bytes 983048 | tf_op jit(solution)/shard_map/ppermute | solution.py:519
  57.6 12.0 %collective-permute-start = (s32[1]{0:T(128)}, s32[1]{0:T(128)}, u32[]{:S(2)}, u32[]{:S(2)}) collective-permute-start(s32[1]{0:T(128)} %get-tuple-element.60), channel_id=1, source_target_pairs={{0,1},{1,0},{2,3},{3,2},{4,5},{5,4},{6,7},{7,6},{8,9},{9,8},{10,11... | collective-permute-start | bytes 20 | tf_op jit(solution)/shard_map/ppermute | solution.py:499
  65.4 11.8 %collective-permute-start.13 = (f32[2,5,16,512]{3,2,1,0:T(8,128)S(1)}, f32[2,5,16,512]{3,2,1,0:T(8,128)S(1)}, u32[]{:S(2)}, u32[]{:S(2)}) collective-permute-start(f32[2,5,16,512]{3,2,1,0:T(8,128)S(1)} %get-tuple-element.54), channel_id=1, source_target_pairs={{0,64},{4,68},{8,72},{12,76},{16,80},{20,84},{24,88},{28,92},{32,9... | collective-permute-start | bytes 983048 | tf_op jit(solution)/shard_map/ppermute | solution.py:523
  79.6 37.0 %all-to-all-start = ((f32[32,136,128]{2,1,0:T(8,128)}), f32[32,136,128]{2,1,0:T(8,128)S(1)}, u32[]{:S(2)}, u32[]{:S(2)}) async-start(f32[32,136,128]{2,1,0:T(8,128)} %pack.1), calls=%async_computation | async-start | bytes 4456448 | tf_op jit(solution)/shard_map/all_to_all | solution.py:524
  90.2 28.8 %collective-permute-start.18 = (f32[1,1,1,2,512,512]{5,4,3,2,1,0:T(8,128)}, f32[1,1,1,2,512,512]{5,4,3,2,1,0:T(8,128)}, u32[]{:S(2)}, u32[]{:S(2)}) collective-permute-start(f32[1,1,1,2,512,512]{5,4,3,2,1,0:T(8,128)} %slice.37), channel_id=1, source_target_pairs={{0,1},{1,0},{2,3},{3,2},{4,5},{5,4},{6,7},{7,6},{8,9},{9,8},{10,11... | collective-permute-start | bytes 6291464 | tf_op jit(solution)/shard_map/ppermute | solution.py:500
  116.7 4.9 %collective-permute-start.17 = (f32[32,64,128]{2,1,0:T(8,128)S(1)}, f32[32,64,128]{2,1,0:T(8,128)S(1)}, u32[]{:S(2)}, u32[]{:S(2)}) collective-permute-start(f32[32,64,128]{2,1,0:T(8,128)S(1)} %slice.45), channel_id=1, source_target_pairs={{0,1},{1,0},{2,3},{3,2},{4,5},{5,4},{6,7},{7,6},{8,9},{9,8},{10,11... | collective-permute-start | bytes 3145736 | tf_op jit(solution)/shard_map/ppermute | solution.py:525
  116.9 3.1 %collective-permute-start.16 = (f32[8,128]{1,0:T(8,128)S(1)}, f32[8,128]{1,0:T(8,128)S(1)}, u32[]{:S(2)}, u32[]{:S(2)}) collective-permute-start(f32[8,128]{1,0:T(8,128)S(1)} %slice_reduce_fusion.s0), channel_id=1, source_target_pairs={{0,3},{1,2},{2,1},{3,0},{4,7},{5,6},{6,5},{7,4},{8,11},{9,10},{10,... | collective-permute-start | bytes 12296 | tf_op jit(solution)/shard_map/ppermute | solution.py:527
  118.0 3.6 %collective-permute-start.15 = (f32[8,128]{1,0:T(8,128)S(1)}, f32[8,128]{1,0:T(8,128)S(1)}, u32[]{:S(2)}, u32[]{:S(2)}) collective-permute-start(f32[8,128]{1,0:T(8,128)S(1)} %slice_reduce_fusion.s0), channel_id=1, source_target_pairs={{0,2},{1,3},{2,0},{3,1},{4,6},{5,7},{6,4},{7,5},{8,10},{9,11},{10,... | collective-permute-start | bytes 12296 | tf_op jit(solution)/shard_map/ppermute | solution.py:527
  119.1 2.6 %collective-permute-start.14 = (f32[8,128]{1,0:T(8,128)S(1)}, f32[8,128]{1,0:T(8,128)S(1)}, u32[]{:S(2)}, u32[]{:S(2)}) collective-permute-start(f32[8,128]{1,0:T(8,128)S(1)} %slice_reduce_fusion.s0), channel_id=1, source_target_pairs={{0,1},{1,0},{2,3},{3,2},{4,5},{5,4},{6,7},{7,6},{8,9},{9,8},{10,11... | collective-permute-start | bytes 12296 | tf_op jit(solution)/shard_map/ppermute | solution.py:527
  136.8 2.0 collective-permute-start.19
  138.9 61.8 %copy-start = (f32[1,1,2,2,512,512]{5,4,3,2,1,0:T(8,128)S(1)}, f32[1,1,2,2,512,512]{5,4,3,2,1,0:T(8,128)}, u32[]{:S(2)}) copy-start(f32[1,1,2,2,512,512]{5,4,3,2,1,0:T(8,128)} %old_ref.1) | copy-start | bytes 12582916
  163.2 6.9 %collective-permute-start.20 = (bf16[10,16,512]{2,1,0:T(8,128)(2,1)S(1)}, bf16[10,16,512]{2,1,0:T(8,128)(2,1)S(1)}, u32[]{:S(2)}, u32[]{:S(2)}) collective-permute-start(bf16[10,16,512]{2,1,0:T(8,128)(2,1)S(1)} %pick.1), channel_id=1, source_target_pairs={{0,64},{4,68},{8,72},{12,76},{16,80},{20,84},{24,88},{28,92},{32,9... | collective-permute-start | bytes 491528 | tf_op jit(solution)/shard_map/ppermute | solution.py:478
  170.2 5.9 %collective-permute-start.23 = (bf16[2,5,16,512]{3,2,1,0:T(8,128)(2,1)S(1)}, bf16[2,5,16,512]{3,2,1,0:T(8,128)(2,1)S(1)}, u32[]{:S(2)}, u32[]{:S(2)}) collective-permute-start(bf16[2,5,16,512]{3,2,1,0:T(8,128)(2,1)S(1)} %get-tuple-element.59), channel_id=1, source_target_pairs={{0,48},{4,52},{8,56},{12,60},{16,0},{20,4},{24,8},{28,12},{32,16},... | collective-permute-start | bytes 491528 | tf_op jit(solution)/shard_map/ppermute | solution.py:478
  171.5 6.9 %collective-permute-start.22 = (bf16[2,5,16,512]{3,2,1,0:T(8,128)(2,1)S(1)}, bf16[2,5,16,512]{3,2,1,0:T(8,128)(2,1)S(1)}, u32[]{:S(2)}, u32[]{:S(2)}) collective-permute-start(bf16[2,5,16,512]{3,2,1,0:T(8,128)(2,1)S(1)} %get-tuple-element.59), channel_id=1, source_target_pairs={{0,32},{4,36},{8,40},{12,44},{16,48},{20,52},{24,56},{28,60},{32,0... | collective-permute-start | bytes 491528 | tf_op jit(solution)/shard_map/ppermute | solution.py:478
  172.3 7.7 %collective-permute-start.21 = (bf16[2,5,16,512]{3,2,1,0:T(8,128)(2,1)S(1)}, bf16[2,5,16,512]{3,2,1,0:T(8,128)(2,1)S(1)}, u32[]{:S(2)}, u32[]{:S(2)}) collective-permute-start(bf16[2,5,16,512]{3,2,1,0:T(8,128)(2,1)S(1)} %get-tuple-element.59), channel_id=1, source_target_pairs={{0,16},{4,20},{8,24},{12,28},{16,32},{20,36},{24,40},{28,44},{32,4... | collective-permute-start | bytes 491528 | tf_op jit(solution)/shard_map/ppermute | solution.py:478
  172.5 9.7 %collective-permute-start.29 = (bf16[2,5,16,512]{3,2,1,0:T(8,128)(2,1)S(1)}, bf16[2,5,16,512]{3,2,1,0:T(8,128)(2,1)S(1)}, u32[]{:S(2)}, u32[]{:S(2)}) collective-permute-start(bf16[2,5,16,512]{3,2,1,0:T(8,128)(2,1)S(1)} %get-tuple-element.58), channel_id=1, source_target_pairs={{0,8},{4,12},{8,0},{12,4},{16,24},{20,28},{24,16},{28,20},{32,40},... | collective-permute-start | bytes 491528 | tf_op jit(solution)/shard_map/ppermute | solution.py:478
  174.8 7.4 %collective-permute-start.28 = (bf16[2,5,16,512]{3,2,1,0:T(8,128)(2,1)S(1)}, bf16[2,5,16,512]{3,2,1,0:T(8,128)(2,1)S(1)}, u32[]{:S(2)}, u32[]{:S(2)}) collective-permute-start(bf16[2,5,16,512]{3,2,1,0:T(8,128)(2,1)S(1)} %get-tuple-element.58), channel_id=1, source_target_pairs={{0,4},{4,8},{8,12},{12,0},{16,20},{20,24},{24,28},{28,16},{32,36},... | collective-permute-start | bytes 491528 | tf_op jit(solution)/shard_map/ppermute | solution.py:478
  176.1 7.1 %collective-permute-start.30 = (bf16[2,5,16,512]{3,2,1,0:T(8,128)(2,1)S(1)}, bf16[2,5,16,512]{3,2,1,0:T(8,128)(2,1)S(1)}, u32[]{:S(2)}, u32[]{:S(2)}) collective-permute-start(bf16[2,5,16,512]{3,2,1,0:T(8,128)(2,1)S(1)} %get-tuple-element.58), channel_id=1, source_target_pairs={{0,12},{4,0},{8,4},{12,8},{16,28},{20,16},{24,20},{28,24},{32,44},... | collective-permute-start | bytes 491528 | tf_op jit(solution)/shard_map/ppermute | solution.py:478
  180.1 15.0 %collective-permute-start.26 = (bf16[4,2,5,16,512]{4,3,2,1,0:T(8,128)(2,1)S(1)}, bf16[4,2,5,16,512]{4,3,2,1,0:T(8,128)(2,1)S(1)}, u32[]{:S(2)}, u32[]{:S(2)}) collective-permute-start(bf16[4,2,5,16,512]{4,3,2,1,0:T(8,128)(2,1)S(1)} %pad_maximum_fusion.1.refs_0_), channel_id=1, source_target_pairs={{0,12},{4,0},{8,4},{12,8},{16,28},{20,16},{24,20},{28,24},{32,44},... | collective-permute-start | bytes 1966088 | tf_op jit(solution)/shard_map/ppermute | solution.py:472
  182.2 14.9 %collective-permute-start.24 = (bf16[4,2,5,16,512]{4,3,2,1,0:T(8,128)(2,1)S(1)}, bf16[4,2,5,16,512]{4,3,2,1,0:T(8,128)(2,1)S(1)}, u32[]{:S(2)}, u32[]{:S(2)}) collective-permute-start(bf16[4,2,5,16,512]{4,3,2,1,0:T(8,128)(2,1)S(1)} %pad_maximum_fusion.1.refs_0_), channel_id=1, source_target_pairs={{0,4},{4,8},{8,12},{12,0},{16,20},{20,24},{24,28},{28,16},{32,36},... | collective-permute-start | bytes 1966088 | tf_op jit(solution)/shard_map/ppermute | solution.py:471
  183.2 14.2 %collective-permute-start.33 = (bf16[4,2,5,16,512]{4,3,2,1,0:T(8,128)(2,1)S(1)}, bf16[4,2,5,16,512]{4,3,2,1,0:T(8,128)(2,1)S(1)}, u32[]{:S(2)}, u32[]{:S(2)}) collective-permute-start(bf16[4,2,5,16,512]{4,3,2,1,0:T(8,128)(2,1)S(1)} %pad_maximum_fusion.2.refs_3_), channel_id=1, source_target_pairs={{0,48},{4,52},{8,56},{12,60},{16,0},{20,4},{24,8},{28,12},{32,16},... | collective-permute-start | bytes 1966088 | tf_op jit(solution)/shard_map/ppermute | solution.py:472
  186.8 13.7 %collective-permute-start.31 = (bf16[4,2,5,16,512]{4,3,2,1,0:T(8,128)(2,1)S(1)}, bf16[4,2,5,16,512]{4,3,2,1,0:T(8,128)(2,1)S(1)}, u32[]{:S(2)}, u32[]{:S(2)}) collective-permute-start(bf16[4,2,5,16,512]{4,3,2,1,0:T(8,128)(2,1)S(1)} %pad_maximum_fusion.2.refs_3_), channel_id=1, source_target_pairs={{0,16},{4,20},{8,24},{12,28},{16,32},{20,36},{24,40},{28,44},{32,4... | collective-permute-start | bytes 1966088 | tf_op jit(solution)/shard_map/ppermute | solution.py:471
  195.2 13.2 %collective-permute-start.27 = (bf16[2,2,5,16,512]{4,3,2,1,0:T(8,128)(2,1)S(1)}, bf16[2,2,5,16,512]{4,3,2,1,0:T(8,128)(2,1)S(1)}, u32[]{:S(2)}, u32[]{:S(2)}) collective-permute-start(bf16[2,2,5,16,512]{4,3,2,1,0:T(8,128)(2,1)S(1)} %slice.49), channel_id=1, source_target_pairs={{0,12},{4,0},{8,4},{12,8},{16,28},{20,16},{24,20},{28,24},{32,44},... | collective-permute-start | bytes 983048 | tf_op jit(solution)/shard_map/ppermute | solution.py:473
  197.1 11.2 %collective-permute-start.25 = (bf16[2,2,5,16,512]{4,3,2,1,0:T(8,128)(2,1)S(1)}, bf16[2,2,5,16,512]{4,3,2,1,0:T(8,128)(2,1)S(1)}, u32[]{:S(2)}, u32[]{:S(2)}) collective-permute-start(bf16[2,2,5,16,512]{4,3,2,1,0:T(8,128)(2,1)S(1)} %slice.48), channel_id=1, source_target_pairs={{0,4},{4,8},{8,12},{12,0},{16,20},{20,24},{24,28},{28,16},{32,36},... | collective-permute-start | bytes 983048 | tf_op jit(solution)/shard_map/ppermute | solution.py:473
  197.4 11.0 %collective-permute-start.34 = (bf16[2,2,5,16,512]{4,3,2,1,0:T(8,128)(2,1)S(1)}, bf16[2,2,5,16,512]{4,3,2,1,0:T(8,128)(2,1)S(1)}, u32[]{:S(2)}, u32[]{:S(2)}) collective-permute-start(bf16[2,2,5,16,512]{4,3,2,1,0:T(8,128)(2,1)S(1)} %slice.51), channel_id=1, source_target_pairs={{0,48},{4,52},{8,56},{12,60},{16,0},{20,4},{24,8},{28,12},{32,16},... | collective-permute-start | bytes 983048 | tf_op jit(solution)/shard_map/ppermute | solution.py:473
  200.6 8.4 %collective-permute-start.32 = (bf16[2,2,5,16,512]{4,3,2,1,0:T(8,128)(2,1)S(1)}, bf16[2,2,5,16,512]{4,3,2,1,0:T(8,128)(2,1)S(1)}, u32[]{:S(2)}, u32[]{:S(2)}) collective-permute-start(bf16[2,2,5,16,512]{4,3,2,1,0:T(8,128)(2,1)S(1)} %slice.50), channel_id=1, source_target_pairs={{0,16},{4,20},{8,24},{12,28},{16,32},{20,36},{24,40},{28,44},{32,4... | collective-permute-start | bytes 983048 | tf_op jit(solution)/shard_map/ppermute | solution.py:473
